TPU v7x, 512 devices: a whole 4x8x8 slice. The times are simulated.
512 devices in a mesh: seq: 128 (over z, y, core), tp: 4 (over x).
Axes of the slice: x: 4, y: 8, z: 8, core: 2. Of those that a mesh axis runs over, the one named last changes fastest.
Arguments:
- tokens: bfloat16 [32768, 1536], P('seq', 'tp'), may hold values from -6 to 6
- norm_gain: float32 [1536], replicated, may hold values from 0.1 to 1.9
- query_weight: bfloat16 [1536, 1536], P(None, 'tp'), may hold values from -0.15625 to 0.15625
- query_bias: float32 [1536], P('tp'), may hold values from -10 to 10
- kv_weight: bfloat16 [1536, 512], P(None, 'tp'), may hold values from -0.15625 to 0.15625
- kv_bias: float32 [512], P('tp'), may hold values from -3 to 3
- out_weight: bfloat16 [1536, 1536], P('tp'), may hold values from -0.625 to 0.625
- shared_slot: bfloat16 [32768, 512], P('seq'), may hold values from -6 to 6
- shared_len: int32 [5], replicated, may hold values from 1 to 256, as said below
- shared_owner: int32 [5], replicated, may hold values from 0 to 127, as said below
- hist_pool: bfloat16 [2048, 64, 512], P('seq'), may hold values from -6 to 6
- hist_pages: int32 [128, 16], P('seq'), may hold values from 0 to 15, each once within a row
- hist_len: int32 [128, 4], P('seq'), may hold values from 1 to 256, as said below
- req_len: int32 [128, 4], P('seq'), may hold values from 1 to 128, 256 in all within a row
- req_offset: int32 [128, 4], P('seq'), may hold values from 0 to 3, each once within a row
- req_parent: int32 [128, 4], P('seq'), may hold values from 0 to 3
Outputs:
- hidden: bfloat16 [32768, 1536], P('seq', 'tp')
- new_cache: bfloat16 [32768, 512], P('seq', 'tp')
Inputs may be any that keep to these rules, and one draw needn't show every extreme that they name: `shared_owner`: all different; entry 0 is the root's. `shared_len`: some entry equals 256. `hist_len`: some request's history has exactly 256 rows.
All inputs are finite; a program needn't handle non-finite values.
Results may differ from a plain program's by a relative error of at most 0.017.
Values may be sent and summed in bfloat16 or wider, within the bound.
No kernel may reach another device: no remote copies, remote signals or barrier semaphores. Data moves between devices by JAX's collectives and lax.ppermute only.
A program may use at most 64 MiB of HBM per device.

v0:
```python
import jax
import jax.numpy as jnp
from jax import lax
from jax.sharding import PartitionSpec as P

norm_eps = 1e-06
rope_base = 1000000.0
neighbour_steps = (-2, -1, 1, 2)
masked_score = -1e30


def from_partner(shard, axis, apart):
    return lax.ppermute(shard, axis, [(i, i ^ 1 << apart) for i in range(lax.axis_size(axis))])


def spread(shard, axis, root):
    mine = lax.axis_index(axis) == root
    return lax.psum(jnp.where(mine, shard, jnp.zeros_like(shard)), axis)


def passed_along(block, axis, distance):
    devices = range(lax.axis_size(axis))
    route = [((i - distance) % len(devices), i) for i in devices]
    return lax.ppermute(block, axis, route)


def request_layout(req_len, req_parent, hist_len, shared_len, row_count):
    request_end = jnp.cumsum(req_len, axis=1)
    request_start = request_end - req_len
    row_index = jnp.arange(row_count, dtype=jnp.int32)
    row_request = jnp.sum(
        (row_index[None, :, None] >= request_end[:, None, :]).astype(jnp.int32), axis=2
    )
    slot_numbers = jnp.arange(req_len.shape[1], dtype=jnp.int32)
    chosen = row_request[:, :, None] == slot_numbers[None, None, :]

    def lookup(table):
        return jnp.sum(jnp.where(chosen, table[:, None, :], 0), axis=2)

    row_offset = row_index[None, :] - lookup(request_start)
    row_parent = lookup(req_parent)
    node_numbers = jnp.arange(shared_len.shape[0] - 1, dtype=jnp.int32)
    parent_length = jnp.sum(
        jnp.where(row_parent[:, :, None] == node_numbers, shared_len[1:], 0), axis=2
    )
    position = shared_len[0] + parent_length + lookup(hist_len) + row_offset
    return (row_request, row_parent, position)


def rotate(values, position):
    half_dim = values.shape[-1] // 2
    frequency = rope_base ** (-2.0 * jnp.arange(half_dim, dtype=jnp.float32) / values.shape[-1])
    angle = position.astype(jnp.float32)[:, None, None] * frequency
    cosine = jnp.cos(angle)
    sine = jnp.sin(angle)
    first_half = values[..., :half_dim]
    second_half = values[..., half_dim:]
    return jnp.concatenate(
        [first_half * cosine - second_half * sine, second_half * cosine + first_half * sine],
        axis=-1,
    )


def partial_attention(queries, key_vectors, value_vectors, key_mask):
    score_scale = queries.shape[-1] ** (-0.5)
    scores = (
        jnp.einsum("rhd,kd->rhk", queries, key_vectors, preferred_element_type=jnp.float32)
        * score_scale
    )
    scores = jnp.where(key_mask[:, None, :], scores, masked_score)
    top_score = jnp.max(scores, axis=2)
    weights = jnp.where(key_mask[:, None, :], jnp.exp(scores - top_score[:, :, None]), 0.0)
    weight_sum = jnp.sum(weights, axis=2)
    mixed = jnp.einsum(
        "rhk,kd->rhd",
        weights.astype(jnp.bfloat16),
        value_vectors,
        preferred_element_type=jnp.float32,
    )
    return (top_score, weight_sum, mixed)


def combine(first_part, second_part):
    top_score = jnp.maximum(first_part[0], second_part[0])
    first_scale = jnp.exp(first_part[0] - top_score)
    second_scale = jnp.exp(second_part[0] - top_score)
    weight_sum = first_part[1] * first_scale + second_part[1] * second_scale
    mixed = first_part[2] * first_scale[:, :, None] + second_part[2] * second_scale[:, :, None]
    return (top_score, weight_sum, mixed)


def on_device(
    tokens,
    norm_gain,
    query_weight,
    query_bias,
    kv_weight,
    kv_bias,
    out_weight,
    shared_slot,
    shared_len,
    shared_owner,
    hist_pool,
    hist_pages,
    hist_len,
    req_len,
    req_offset,
    req_parent,
):
    features = lax.all_gather(tokens, "tp", axis=1, tiled=True)
    widened = features.astype(jnp.float32)
    mean_square = jnp.mean(widened * widened, axis=1, keepdims=True)
    normed = (widened * lax.rsqrt(mean_square + norm_eps) * norm_gain).astype(jnp.bfloat16)
    head_dim = kv_bias.shape[0]
    head_count = query_weight.shape[1] // head_dim
    row_count = features.shape[0]
    tp_index = lax.axis_index("tp")
    kv_group = tp_index // 2
    holds_key = tp_index % 2 == 0
    row_request, row_parent, position = request_layout(
        req_len, req_parent, hist_len, shared_len, row_count
    )
    row_request = row_request[0]
    row_parent = row_parent[0]
    position = position[0]
    queries = jnp.dot(normed, query_weight, preferred_element_type=jnp.float32) + query_bias
    queries = rotate(queries.reshape(row_count, head_count, head_dim), position).astype(
        jnp.bfloat16
    )
    own_block = jnp.dot(normed, kv_weight, preferred_element_type=jnp.float32) + kv_bias
    own_block = jnp.where(
        holds_key, rotate(own_block[:, None, :], position)[:, 0, :], own_block
    ).astype(jnp.bfloat16)
    partner = from_partner(own_block, "tp", 0)
    fresh_keys = jnp.where(holds_key, own_block, partner)
    fresh_values = jnp.where(holds_key, partner, own_block)
    head_columns = lax.dynamic_slice_in_dim(shared_slot, kv_group * 2 * head_dim, 2 * head_dim, 1)
    node_total = shared_owner.shape[0]
    hot_list = [
        spread(head_columns, "seq", shared_owner[level_node]) for level_node in range(node_total)
    ]
    hot_rows = jnp.concatenate(hot_list, axis=0)
    slot_length = head_columns.shape[0]
    hot_node = jnp.repeat(jnp.arange(node_total, dtype=jnp.int32), slot_length)
    hot_place = jnp.tile(jnp.arange(slot_length, dtype=jnp.int32), node_total)
    hot_valid = hot_place < jnp.repeat(shared_len, slot_length)
    every_key = jnp.concatenate([hot_rows[:, :head_dim], fresh_keys], axis=0)
    every_value = jnp.concatenate([hot_rows[:, head_dim:], fresh_values], axis=0)
    block_rows = min(512, row_count)
    row_index = jnp.arange(row_count, dtype=jnp.int32)

    def local_block(block_number):
        row_start = block_number * block_rows
        block_places = row_start + jnp.arange(block_rows, dtype=jnp.int32)
        hot_mask = (
            (hot_node[None, :] == 0) | (hot_node[None, :] == row_parent[:, None] + 1)
        ) & hot_valid[None, :]
        own_mask = (row_request[None, :] == row_request[:, None]) & (
            row_index[None, :] <= block_places[:, None]
        )
        return partial_attention(
            queries, every_key, every_value, jnp.concatenate([hot_mask, own_mask], axis=1)
        )

    local_parts = lax.map(local_block, jnp.arange(row_count // block_rows, dtype=jnp.int32))
    local_parts = tuple((piece.reshape((row_count,) + piece.shape[2:]) for piece in local_parts))
    capacity = row_count // 2
    request_count = req_len.shape[1]
    page_count = hist_pages.shape[1] // request_count
    request_end = jnp.cumsum(req_len[0])
    request_start = request_end - req_len[0]
    padded_queries = jnp.concatenate(
        [queries, jnp.zeros((capacity, head_count, head_dim), jnp.bfloat16)], axis=0
    )
    history_top = jnp.full((row_count + capacity, head_count), masked_score, jnp.float32)
    history_sum = jnp.zeros((row_count + capacity, head_count), jnp.float32)
    history_mix = jnp.zeros((row_count + capacity, head_count, head_dim), jnp.float32)
    capacity_rows = jnp.arange(capacity, dtype=jnp.int32)
    for slot_number in range(request_count):
        offset_step = neighbour_steps[slot_number]
        chosen = req_offset[0] == slot_number
        row_start = jnp.sum(jnp.where(chosen, request_start, 0))
        row_total = jnp.sum(jnp.where(chosen, req_len[0], 0))
        node_depth = jnp.sum(jnp.where(chosen, hist_len[0], 0)).reshape(1)
        window = lax.dynamic_slice_in_dim(padded_queries, row_start, capacity, 0)
        page_rows = hist_pool[
            hist_pages[0, slot_number * page_count : (slot_number + 1) * page_count]
        ]
        flat_pages = page_rows.reshape(-1, page_rows.shape[-1])
        node_places = jnp.arange(flat_pages.shape[0], dtype=jnp.int32)
        node_rows = lax.dynamic_slice_in_dim(flat_pages, kv_group * 2 * head_dim, 2 * head_dim, 1)
        arrived_node = passed_along(node_rows, "seq", -offset_step)
        depth_mask = jnp.broadcast_to(
            (node_places < node_depth[0])[None, :], (capacity, flat_pages.shape[0])
        )
        answer = partial_attention(
            window, arrived_node[:, :head_dim], arrived_node[:, head_dim:], depth_mask
        )
        row_valid = capacity_rows < row_total

        def put_rows(whole_rows, fresh_part):
            region = lax.dynamic_slice_in_dim(whole_rows, row_start, capacity, 0)
            keep_rows = row_valid.reshape((capacity,) + (1,) * (fresh_part.ndim - 1))
            return lax.dynamic_update_slice_in_dim(
                whole_rows, jnp.where(keep_rows, fresh_part, region), row_start, 0
            )

        history_top = put_rows(history_top, answer[0])
        history_sum = put_rows(history_sum, answer[1])
        history_mix = put_rows(history_mix, answer[2])
    history_part = (history_top[:row_count], history_sum[:row_count], history_mix[:row_count])
    merged = combine(local_parts, history_part)
    attention = (
        (merged[2] / merged[1][:, :, None])
        .astype(jnp.bfloat16)
        .reshape(row_count, head_count * head_dim)
    )
    terms = jnp.dot(attention, out_weight, preferred_element_type=jnp.float32)
    summed = lax.psum_scatter(
        terms.astype(jnp.bfloat16), "tp", scatter_dimension=1, tiled=True
    ).astype(jnp.float32)
    hidden = (summed + tokens.astype(jnp.float32)).astype(jnp.bfloat16)
    return (hidden, own_block)


def solution(mesh):
    return jax.shard_map(
        on_device,
        mesh=mesh,
        in_specs=(
            P("seq", "tp"),
            P(),
            P(None, "tp"),
            P("tp"),
            P(None, "tp"),
            P("tp"),
            P("tp", None),
            P("seq", None),
            P(),
            P(),
            P("seq", None, None),
            P("seq", None),
            P("seq", None),
            P("seq", None),
            P("seq", None),
            P("seq", None),
        ),
        out_specs=(P("seq", "tp"), P("seq", "tp")),
        check_vma=False,
    )
```

profile of v0, /device:TPU:1, one launch (start us, length us, event | category | flops | bytes accessed | tf_op | source)
XLA Modules:
  0.0 298.2 jit_solution(13311774897615875516)
XLA Ops:
  7.3 0.9 fusion.93
  8.2 1.8 gather_fusion.1
  10.0 0.7 constant_dynamic-slice_fusion.8
  10.7 4.6 %collective-permute-start.2 = (bf16[256,256]{1,0:T(8,128)(2,1)}, bf16[256,256]{1,0:T(8,128)(2,1)}, u32[]{:S(2)}, u32[]{:S(2)}) collective-permute-start(bf16[256,256]{1,0:T(8,128)(2,1)} %constant_dynamic-slice_fusion.8), channel_id=1, source_target_pairs={{508,0},{0,4},{4,8},{8,12},{12,16},{16,20},{20,24},{24,28},{28,32}... | collective-permute-start | bytes 393224 | tf_op jit(solution)/shard_map/ppermute | solution.py:24
  15.3 1.8 gather_fusion.3
  17.1 0.7 constant_dynamic-slice_fusion.4
  17.8 11.7 %collective-permute-start.4 = (bf16[256,256]{1,0:T(8,128)(2,1)}, bf16[256,256]{1,0:T(8,128)(2,1)}, u32[]{:S(2)}, u32[]{:S(2)}) collective-permute-start(bf16[256,256]{1,0:T(8,128)(2,1)} %constant_dynamic-slice_fusion.4), channel_id=1, source_target_pairs={{8,0},{12,4},{16,8},{20,12},{24,16},{28,20},{32,24},{36,28},{40,32... | collective-permute-start | bytes 393224 | tf_op jit(solution)/shard_map/ppermute | solution.py:24
  29.5 1.8 gather_fusion
  31.3 0.7 constant_dynamic-slice_fusion.9
  32.0 1.9 collective-permute-start.1
  33.9 1.8 gather_fusion.2
  35.8 0.7 constant_dynamic-slice_fusion.6
  36.4 2.9 collective-permute-start.3
  39.7 12.1 %all_gather.3 = bf16[256,1536]{1,0:T(8,128)(2,1)S(1)} all-gather(bf16[256,384]{1,0:T(8,128)(2,1)S(1)} %copy-done.1), channel_id=1, replica_groups=mesh['seq'=128,'tp'=4] {'tp'}, dimensions={1}, use_global_device_ids=true | all-gather | bytes 983040 | tf_op jit(solution)/shard_map/all_gather | solution.py:110
  52.3 0.5 convolution_add_fusion.1
  52.8 0.3 fusion.63
  53.1 3.1 %collective-permute-start = (bf16[256,128]{0,1:T(8,128)(2,1)S(1)}, bf16[256,128]{0,1:T(8,128)(2,1)}, u32[]{:S(2)}, u32[]{:S(2)}) collective-permute-start(bf16[256,128]{0,1:T(8,128)(2,1)S(1)} %fusion.58), channel_id=1, source_target_pairs={{0,1},{1,0},{2,3},{3,2},{4,5},{5,4},{6,7},{7,6},{8,9},{9,8},{10,11... | collective-permute-start | bytes 196616 | tf_op jit(solution)/shard_map/ppermute | solution.py:13
  56.3 0.7 fusion.111
  60.1 0.8 broadcast_select_fusion
  61.3 0.9 fusion.87
  67.4 0.5 multiply_cosine_fusion
  67.9 1.2 iota_compare_fusion.9
  69.1 0.7 iota_compare_fusion.8
  69.8 1.3 iota_compare_fusion.7
  71.0 1.2 iota_compare_fusion.6
  72.3 0.6 iota_compare_fusion.5
  72.9 1.1 iota_compare_fusion.11
  74.0 1.1 iota_compare_fusion.10
  75.1 1.9 convolution_add_fusion
  80.1 0.3 or_and_fusion
  80.7 0.6 iota_compare_fusion.12
  81.4 0.9 broadcast_select_fusion.5
  82.3 0.7 copy.54
  83.0 0.7 copy.53
  83.7 1.2 fusion.112
  84.9 1.1 convolution_select_fusion.3
  86.1 1.5 dynamic_update_slice.48
  87.6 1.2 fusion.113
  88.8 1.2 convolution_select_fusion.2
  89.9 0.7 dynamic_update_slice.49
  90.7 0.9 fusion.32
  91.6 1.2 fusion.114
  92.8 0.9 fusion.34
  93.7 1.2 convolution_select_fusion.1
  94.9 0.7 dynamic_update_slice.50
  95.9 1.2 fusion.115
  97.1 1.2 convolution_select_fusion
  98.3 1.3 dynamic_update_slice.51
  99.6 0.3 dynamic_update_slice.44
  101.7 153.0 %all-reduce.4.cloned.1.call-done = (bf16[256,256]{1,0:T(8,128)(2,1)}, bf16[256,256]{1,0:T(8,128)(2,1)}, bf16[256,256]{1,0:T(8,128)(2,1)}, bf16[256,256]{1,0:T(8,128)(2,1)}, bf16[256,256]{1,0:T(8,128)(2,1)}) async-done(((bf16[256,256]{1,0:T(8,128)(2,1)}, bf16[256,256]{1,0:T(8,128)(2,1)}, bf16[256,256]{1,0:T(8,128)(2,1)}, bf16[256,256]{1,0:T(8,128)(2,1)}, bf16[256,256]{1,0:T(8,128)(2,1)}), ...) | async-done | bytes 655376 | tf_op jit(solution)/shard_map/psum | solution.py:18
  254.7 0.9 constant_dynamic-update-slice_fusion.4
  255.6 0.9 constant_dynamic-update-slice_fusion.3
  256.5 0.9 constant_dynamic-update-slice_fusion.2
  257.4 0.9 constant_dynamic-update-slice_fusion.1
  258.4 0.9 constant_dynamic-update-slice_fusion
  259.3 1.1 fusion
  260.5 1.6 fusion.1
  262.1 1.5 fusion.22
  263.6 0.6 convolution_convert_fusion
  264.2 1.2 copy.71
  265.3 0.7 copy.60
  266.1 23.5 %reduce-scatter.4.cloned.1.call-done = bf16[384,256]{1,0:T(8,128)(2,1)} async-done(((bf16[1536,256]{1,0:T(8,128)(2,1)}), bf16[384,256]{1,0:T(8,128)(2,1)}) %reduce-scatter.4.cloned.1.call-update) | async-done | bytes 196624
  289.6 1.1 copy.72
  290.7 0.7 add_convert_fusion
  (99 shorter events, 4.3 us)
Async XLA Ops:
  7.2 256.4 %copy-start = (bf16[384,1536]{1,0:T(8,128)(2,1)S(1)}, bf16[384,1536]{1,0:T(8,128)(2,1)}, u32[]{:S(2)}) copy-start(bf16[384,1536]{1,0:T(8,128)(2,1)} %param.22) | copy-start | bytes 3538948
  7.2 32.1 %copy-start.15 = (s32[1,4]{1,0:T(1,128)S(1)}, s32[1,4]{1,0:T(1,128)}, u32[]{:S(2)}) copy-start(s32[1,4]{1,0:T(1,128)} %param.29) | copy-start | bytes 52
  7.2 32.3 %copy-start.13 = (s32[5]{0:T(128)S(1)}, s32[5]{0:T(128)}, u32[]{:S(2)}) copy-start(s32[5]{0:T(128)} %param.24) | copy-start | bytes 64
  7.2 32.5 %copy-start.1 = (bf16[256,384]{1,0:T(8,128)(2,1)S(1)}, bf16[256,384]{1,0:T(8,128)(2,1)}, u32[]{:S(2)}) copy-start(bf16[256,384]{1,0:T(8,128)(2,1)} %param.16) | copy-start | bytes 589828
  7.2 247.5 %all-reduce.4.cloned.1.call-start = ((), (), s32[]{:S(2)}) async-start(), calls=%async_computation.2 | async-start | bytes 1310720 | tf_op jit(solution)/shard_map/psum | solution.py:18
  8.2 43.8 %copy-start.14 = (s32[1,4]{1,0:T(1,128)S(1)}, s32[1,4]{1,0:T(1,128)}, u32[]{:S(2)}) copy-start(s32[1,4]{1,0:T(1,128)} %param.28) | copy-start | bytes 52
  8.2 43.8 %copy-start.17 = (s32[1,4]{1,0:T(1,128)S(1)}, s32[1,4]{1,0:T(1,128)}, u32[]{:S(2)}) copy-start(s32[1,4]{1,0:T(1,128)} %param.31) | copy-start | bytes 52
  10.0 42.3 %copy-start.18 = (bf16[1536,128]{1,0:T(8,128)(2,1)S(1)}, bf16[1536,128]{1,0:T(8,128)(2,1)}, u32[]{:S(2)}) copy-start(bf16[1536,128]{1,0:T(8,128)(2,1)} %param.20) | copy-start | bytes 1179652
  10.0 42.3 %copy-start.19 = (f32[1536]{0:T(1024)S(1)}, f32[1536]{0:T(1024)}, u32[]{:S(2)}) copy-start(f32[1536]{0:T(1024)} %param.17) | copy-start | bytes 18436
  10.0 42.3 %copy-start.21 = (f32[128]{0:T(128)S(1)}, f32[128]{0:T(128)}, u32[]{:S(2)}) copy-start(f32[128]{0:T(128)} %param.21) | copy-start | bytes 1540
  10.7 76.9 %collective-permute-start.2 = (bf16[256,256]{1,0:T(8,128)(2,1)}, bf16[256,256]{1,0:T(8,128)(2,1)}, u32[]{:S(2)}, u32[]{:S(2)}) collective-permute-start(bf16[256,256]{1,0:T(8,128)(2,1)} %constant_dynamic-slice_fusion.8), channel_id=1, source_target_pairs={{508,0},{0,4},{4,8},{8,12},{12,16},{16,20},{20,24},{24,28},{28,32}... | collective-permute-start | bytes 393224 | tf_op jit(solution)/shard_map/ppermute | solution.py:24
  17.8 78.1 %collective-permute-start.4 = (bf16[256,256]{1,0:T(8,128)(2,1)}, bf16[256,256]{1,0:T(8,128)(2,1)}, u32[]{:S(2)}, u32[]{:S(2)}) collective-permute-start(bf16[256,256]{1,0:T(8,128)(2,1)} %constant_dynamic-slice_fusion.4), channel_id=1, source_target_pairs={{8,0},{12,4},{16,8},{20,12},{24,16},{28,20},{32,24},{36,28},{40,32... | collective-permute-start | bytes 393224 | tf_op jit(solution)/shard_map/ppermute | solution.py:24
  32.0 51.7 %collective-permute-start.1 = (bf16[256,256]{1,0:T(8,128)(2,1)}, bf16[256,256]{1,0:T(8,128)(2,1)}, u32[]{:S(2)}, u32[]{:S(2)}) collective-permute-start(bf16[256,256]{1,0:T(8,128)(2,1)} %constant_dynamic-slice_fusion.9), channel_id=1, source_target_pairs={{504,0},{508,4},{0,8},{4,12},{8,16},{12,20},{16,24},{20,28},{24,32... | collective-permute-start | bytes 393224 | tf_op jit(solution)/shard_map/ppermute | solution.py:24
  33.9 22.4 %copy-start.7 = (s32[5]{0:T(128)S(1)}, s32[5]{0:T(128)}, u32[]{:S(2)}) copy-start(s32[5]{0:T(128)} %param.25) | copy-start | bytes 64
  33.9 26.2 %copy-start.6 = (bf16[256,512]{1,0:T(8,128)(2,1)S(1)}, bf16[256,512]{1,0:T(8,128)(2,1)}, u32[]{:S(2)}) copy-start(bf16[256,512]{1,0:T(8,128)(2,1)} %param.23) | copy-start | bytes 786436
  36.4 55.2 %collective-permute-start.3 = (bf16[256,256]{1,0:T(8,128)(2,1)}, bf16[256,256]{1,0:T(8,128)(2,1)}, u32[]{:S(2)}, u32[]{:S(2)}) collective-permute-start(bf16[256,256]{1,0:T(8,128)(2,1)} %constant_dynamic-slice_fusion.6), channel_id=1, source_target_pairs={{4,0},{8,4},{12,8},{16,12},{20,16},{24,20},{28,24},{32,28},{36,32}... | collective-permute-start | bytes 393224 | tf_op jit(solution)/shard_map/ppermute | solution.py:24
  51.8 9.5 %copy-start.16 = (s32[1,4]{1,0:T(1,128)S(1)}, s32[1,4]{1,0:T(1,128)}, u32[]{:S(2)}) copy-start(s32[1,4]{1,0:T(1,128)} %param.30) | copy-start | bytes 52
  51.8 23.3 %copy-start.20 = (f32[384]{0:T(512)S(1)}, f32[384]{0:T(512)}, u32[]{:S(2)}) copy-start(f32[384]{0:T(512)} %param.19) | copy-start | bytes 4612
  53.1 28.3 %copy-start.2 = (bf16[256,128]{0,1:T(8,128)(2,1)}, bf16[256,128]{0,1:T(8,128)(2,1)S(1)}, u32[]{:S(2)}) copy-start(bf16[256,128]{0,1:T(8,128)(2,1)S(1)} %fusion.58) | copy-start | bytes 196612
  53.1 28.2 %collective-permute-start = (bf16[256,128]{0,1:T(8,128)(2,1)S(1)}, bf16[256,128]{0,1:T(8,128)(2,1)}, u32[]{:S(2)}, u32[]{:S(2)}) collective-permute-start(bf16[256,128]{0,1:T(8,128)(2,1)S(1)} %fusion.58), channel_id=1, source_target_pairs={{0,1},{1,0},{2,3},{3,2},{4,5},{5,4},{6,7},{7,6},{8,9},{9,8},{10,11... | collective-permute-start | bytes 196616 | tf_op jit(solution)/shard_map/ppermute | solution.py:13
  61.0 228.6 %reduce-scatter.4.cloned.1.call-start = ((), (), s32[]{:S(2)}) async-start(), calls=%async_computation.1 | async-start | bytes 983040
  81.4 6.2 %copy-start.8 = (pred[128]{0:T(512)(128)(4,1)}, pred[128]{0:T(512)(128)(4,1)S(1)}, u32[]{:S(2)}) copy-start(pred[128]{0:T(512)(128)(4,1)S(1)} %iota_compare_fusion.12) | copy-start | bytes 388
  91.6 8.0 %copy-start.9 = (pred[128]{0:T(512)(128)(4,1)S(1)}, pred[128]{0:T(512)(128)(4,1)}, u32[]{:S(2)}) copy-start(pred[128]{0:T(512)(128)(4,1)} %copy-done.8) | copy-start | bytes 388
  91.6 8.5 %copy-start.12 = (pred[128]{0:T(512)(128)(4,1)S(1)}, pred[128]{0:T(512)(128)(4,1)}, u32[]{:S(2)}) copy-start(pred[128]{0:T(512)(128)(4,1)} %iota_compare_fusion.11) | copy-start | bytes 388
  91.6 8.9 %copy-start.11 = (pred[128]{0:T(512)(128)(4,1)S(1)}, pred[128]{0:T(512)(128)(4,1)}, u32[]{:S(2)}) copy-start(pred[128]{0:T(512)(128)(4,1)} %iota_compare_fusion.10) | copy-start | bytes 388
  92.8 8.3 %copy-start.10 = (pred[128]{0:T(512)(128)(4,1)S(1)}, pred[128]{0:T(512)(128)(4,1)}, u32[]{:S(2)}) copy-start(pred[128]{0:T(512)(128)(4,1)} %iota_compare_fusion.9) | copy-start | bytes 388
  97.0 162.3 %copy-start.5 = (bf16[256,128]{1,0:T(8,128)(2,1)S(1)}, bf16[256,128]{1,0:T(8,128)(2,1)}, u32[]{:S(2)}) copy-start(bf16[256,128]{1,0:T(8,128)(2,1)} %copy.53) | copy-start | bytes 196612
  260.5 1.6 copy-start.4
  263.5 1.8 copy-start.3
Sparse Core Ops, SparseCore 0:
  61.1 193.5 all-reduce.3
  265.5 24.0 reduce-scatter.3
where the time goes:
time: 300 us; the launch traced here: 298 us
  waiting for transfers between devices  177 us (59%)
  local copies, waits for them, and re-layouts  26.2 us (9%)
  between operations  25.7 us (9%)
  starting transfers between devices  24.3 us (8%)
  other arithmetic  18.6 us (6%)
  matrix products  14.8 us (5%)
  blocking collectives  12.1 us (4%)
    psum x1, waiting for transfers between devices, spread(): return lax.psum(jnp.where(mine, shard, jnp.zeros_like(shard)), axis)  153 us
    unnamed x3, waiting for transfers between devices  23.5 us
    ppermute x4, starting transfers between devices, passed_along(): return lax.ppermute(block, axis, route)  21.1 us
    all_gather x1, blocking collectives, on_device(): features = lax.all_gather(tokens, 'tp', axis=1, tiled=True)  12.1 us
    gather x4, local copies, waits for them, and re-layouts, on_device(): hist_pool[hist_pages[0, slot_number * page_count:(slot_number + 1) * page...  7.21 us
    unnamed x53, local copies, waits for them, and re-layouts  7.08 us
    dot_general x5, matrix products, partial_attention(): jnp.einsum('rhk,kd->rhd', weights.astype(jnp.bfloat16), value_vectors, pr...  6.1 us
  transfers between devices with their start and end apart: 7, of which 2 were waited for; matrix products, arithmetic and copies ran while one was open for 15% of the time, Pallas kernels for 0%

commit v1 on v0

--- a/solution.py
+++ b/solution.py
@@ -1,25 +1,49 @@
+import math
+
 import jax
 import jax.numpy as jnp
 from jax import lax
-from jax.sharding import PartitionSpec as P
+from jax.sharding import Mesh, PartitionSpec as P
 
 norm_eps = 1e-06
 rope_base = 1000000.0
 neighbour_steps = (-2, -1, 1, 2)
 masked_score = -1e30
+seq_axes = ("z", "y", "core")
 
 
 def from_partner(shard, axis, apart):
     return lax.ppermute(shard, axis, [(i, i ^ 1 << apart) for i in range(lax.axis_size(axis))])
 
 
-def spread(shard, axis, root):
-    mine = lax.axis_index(axis) == root
-    return lax.psum(jnp.where(mine, shard, jnp.zeros_like(shard)), axis)
+def copies_exchanged(block, axis, count):
+    copies = jnp.broadcast_to(block[None], (count,) + block.shape)
+    return lax.all_to_all(copies, axis, 0, 0, tiled=True)
+
+
+def gathered_nodes(head_columns, shared_owner):
+    z_count = lax.axis_size("z")
+    plane_count = lax.axis_size("y") * lax.axis_size("core")
+    rows, columns = head_columns.shape
+    chunk = rows // plane_count
+    pieces = head_columns.reshape(plane_count, chunk, columns)
+    arrived = lax.all_to_all(pieces, ("y", "core"), 0, 0, tiled=True)
+    in_plane = shared_owner % plane_count
+    plane = shared_owner // plane_count
+    node_total = shared_owner.shape[0]
+    chosen = jnp.stack(
+        [lax.dynamic_index_in_dim(arrived, in_plane[n], 0, False) for n in range(node_total)]
+    )
+    planes = copies_exchanged(chosen, "z", z_count)
+    kept = jnp.stack(
+        [lax.dynamic_index_in_dim(planes[:, n], plane[n], 0, False) for n in range(node_total)]
+    )
+    spread = lax.all_gather(kept, ("y", "core"), axis=0, tiled=False)
+    return spread.reshape(plane_count * node_total * chunk, columns), chunk
 
 
 def passed_along(block, axis, distance):
-    devices = range(lax.axis_size(axis))
+    devices = range(math.prod(lax.axis_size(name) for name in axis))
     route = [((i - distance) % len(devices), i) for i in devices]
     return lax.ppermute(block, axis, route)
 
@@ -107,7 +131,8 @@
     req_offset,
     req_parent,
 ):
-    features = lax.all_gather(tokens, "tp", axis=1, tiled=True)
+    group_count = lax.axis_size("tp")
+    features = jnp.concatenate(list(copies_exchanged(tokens, "tp", group_count)), axis=1)
     widened = features.astype(jnp.float32)
     mean_square = jnp.mean(widened * widened, axis=1, keepdims=True)
     normed = (widened * lax.rsqrt(mean_square + norm_eps) * norm_gain).astype(jnp.bfloat16)
@@ -136,14 +161,11 @@
     fresh_values = jnp.where(holds_key, partner, own_block)
     head_columns = lax.dynamic_slice_in_dim(shared_slot, kv_group * 2 * head_dim, 2 * head_dim, 1)
     node_total = shared_owner.shape[0]
-    hot_list = [
-        spread(head_columns, "seq", shared_owner[level_node]) for level_node in range(node_total)
-    ]
-    hot_rows = jnp.concatenate(hot_list, axis=0)
-    slot_length = head_columns.shape[0]
-    hot_node = jnp.repeat(jnp.arange(node_total, dtype=jnp.int32), slot_length)
-    hot_place = jnp.tile(jnp.arange(slot_length, dtype=jnp.int32), node_total)
-    hot_valid = hot_place < jnp.repeat(shared_len, slot_length)
+    hot_rows, chunk = gathered_nodes(head_columns, shared_owner)
+    hot_index = jnp.arange(hot_rows.shape[0], dtype=jnp.int32)
+    hot_node = hot_index // chunk % node_total
+    hot_place = hot_index // (chunk * node_total) * chunk + hot_index % chunk
+    hot_valid = hot_place < shared_len[hot_node]
     every_key = jnp.concatenate([hot_rows[:, :head_dim], fresh_keys], axis=0)
     every_value = jnp.concatenate([hot_rows[:, head_dim:], fresh_values], axis=0)
     block_rows = min(512, row_count)
@@ -189,7 +211,7 @@
         flat_pages = page_rows.reshape(-1, page_rows.shape[-1])
         node_places = jnp.arange(flat_pages.shape[0], dtype=jnp.int32)
         node_rows = lax.dynamic_slice_in_dim(flat_pages, kv_group * 2 * head_dim, 2 * head_dim, 1)
-        arrived_node = passed_along(node_rows, "seq", -offset_step)
+        arrived_node = passed_along(node_rows, seq_axes, -offset_step)
         depth_mask = jnp.broadcast_to(
             (node_places < node_depth[0])[None, :], (capacity, flat_pages.shape[0])
         )
@@ -216,35 +238,39 @@
         .reshape(row_count, head_count * head_dim)
     )
     terms = jnp.dot(attention, out_weight, preferred_element_type=jnp.float32)
-    summed = lax.psum_scatter(
-        terms.astype(jnp.bfloat16), "tp", scatter_dimension=1, tiled=True
-    ).astype(jnp.float32)
+    width = tokens.shape[1]
+    blocks = jnp.stack(
+        [terms[:, g * width : (g + 1) * width].astype(jnp.bfloat16) for g in range(group_count)]
+    )
+    summed = jnp.sum(lax.all_to_all(blocks, "tp", 0, 0, tiled=True).astype(jnp.float32), axis=0)
     hidden = (summed + tokens.astype(jnp.float32)).astype(jnp.bfloat16)
     return (hidden, own_block)
 
 
 def solution(mesh):
+    devices = mesh.devices
+    split = Mesh(devices.reshape(8, devices.shape[0] // 16, 2, devices.shape[1]), seq_axes + ("tp",))
     return jax.shard_map(
         on_device,
-        mesh=mesh,
+        mesh=split,
         in_specs=(
-            P("seq", "tp"),
+            P(seq_axes, "tp"),
             P(),
             P(None, "tp"),
             P("tp"),
             P(None, "tp"),
             P("tp"),
             P("tp", None),
-            P("seq", None),
+            P(seq_axes, None),
             P(),
             P(),
-            P("seq", None, None),
-            P("seq", None),
-            P("seq", None),
-            P("seq", None),
-            P("seq", None),
-            P("seq", None),
+            P(seq_axes, None, None),
+            P(seq_axes, None),
+            P(seq_axes, None),
+            P(seq_axes, None),
+            P(seq_axes, None),
+            P(seq_axes, None),
         ),
-        out_specs=(P("seq", "tp"), P("seq", "tp")),
+        out_specs=(P(seq_axes, "tp"), P(seq_axes, "tp")),
         check_vma=False,
     )

time: 300 us -> 167 us (0.56)
  waiting for transfers between devices: 177 us -> 11.2 us
  starting transfers between devices: 24.3 us -> 43 us
  blocking collectives: 12.1 us -> 22.1 us
  other arithmetic: 18.6 us -> 22.5 us
  local copies, waits for them, and re-layouts: 26.2 us -> 22.6 us
    psum x1 -> x0, waiting for transfers between devices: 153 us -> none  [spread(): return lax.psum(jnp.where(mine, shard, jnp.zeros_like(shard)), axis)]
    unnamed x3 -> x0, waiting for transfers between devices: 23.5 us -> none
    all_to_all x0 -> x4, starting transfers between devices: none -> 21.5 us  [the longest x1 10.2 us: gathered_nodes(): arrived = lax.all_to_all(pieces, ('y', 'core'), 0, 0, tiled=True)]
    all_to_all x0 -> x4, waiting for transfers between devices: none -> 11.2 us  [the longest x1 11.2 us: on_device(): lax.all_to_all(blocks, 'tp', 0, 0, tiled=True).astype(jnp.float32)]
    all_gather x1, blocking collectives: 12.1 us -> 22.1 us  [gathered_nodes(): spread = lax.all_gather(kept, ('y', 'core'), axis=0, tiled=False)]
    unnamed x53 -> x63, local copies, waits for them, and re-layouts: 7.08 us -> 3.11 us
    gather x4, local copies, waits for them, and re-layouts: 7.21 us -> 3.5 us  [on_device(): hist_pool[hist_pages[0, slot_number * page_count:(slot_number + 1) * page...]
    ppermute x4, starting transfers between devices: 21.1 us -> 17.9 us  [passed_along(): return lax.ppermute(block, axis, route)]
  transfers between devices with their start and end apart: 7 -> 9, of which waited for: 2 -> 1; matrix products, arithmetic and copies ran while one was open for 15% -> 31% of each run, Pallas kernels for 0% -> 0%
where the time goes in v1:
time: 167 us; the launch traced here: 165 us
  starting transfers between devices  43 us (26%)
  between operations  27.6 us (17%)
  local copies, waits for them, and re-layouts  22.6 us (14%)
  other arithmetic  22.5 us (13%)
  blocking collectives  22.1 us (13%)
  matrix products  15.9 us (10%)
  waiting for transfers between devices  11.2 us (7%)
    all_gather x1, blocking collectives, gathered_nodes(): spread = lax.all_gather(kept, ('y', 'core'), axis=0, tiled=False)  22.1 us
    ppermute x4, starting transfers between devices, passed_along(): return lax.ppermute(block, axis, route)  17.9 us
    all_to_all x1, waiting for transfers between devices, on_device(): lax.all_to_all(blocks, 'tp', 0, 0, tiled=True).astype(jnp.float32)  11.2 us
    all_to_all x1, starting transfers between devices, gathered_nodes(): arrived = lax.all_to_all(pieces, ('y', 'core'), 0, 0, tiled=True)  10.2 us
    all_to_all x2, starting transfers between devices, copies_exchanged(): return lax.all_to_all(copies, axis, 0, 0, tiled=True)  7.58 us
    dot_general x5, matrix products, partial_attention(): jnp.einsum('rhk,kd->rhd', weights.astype(jnp.bfloat16), value_vectors, pr...  7.43 us
    dynamic_update_slice x12, local copies, waits for them, and re-layouts, put_rows(): lax.dynamic_update_slice_in_dim(whole_rows, jnp.where(keep_rows, fresh_pa...  7.06 us
    dot_general x5, matrix products, partial_attention(): jnp.einsum('rhd,kd->rhk', queries, key_vectors, preferred_element_type=jn...  5.77 us
  transfers between devices with their start and end apart: 9, of which 1 were waited for; matrix products, arithmetic and copies ran while one was open for 31% of the time, Pallas kernels for 0%

profile of v1, /device:TPU:1, one launch (start us, length us, event | category | flops | bytes accessed | tf_op | source)
XLA Modules:
  0.0 165.0 jit_solution(1489016729982481378)
XLA Ops:
  0.7 1.7 %constant_dynamic-slice_fusion.10 = bf16[256,256]{1,0:T(8,128)(2,1)} fusion(bf16[256,512]{1,0:T(8,128)(2,1)} %param.23, s32[]{:T(128)S(6)} %select_n.391), kind=kLoop, calls=%fused_computation.171 | loop fusion | bytes 262148 | tf_op jit(solution)/shard_map/dynamic_slice | solution.py:162
  2.4 10.2 %all-to-all-start.1 = ((bf16[16,16,256]{2,1,0:T(8,128)(2,1)}), bf16[16,16,256]{2,1,0:T(8,128)(2,1)S(1)}, u32[]{:S(2)}, u32[]{:S(2)}) async-start(bf16[16,16,256]{2,1,0:T(8,128)(2,1)} %bitcast.14), calls=%async_computation.1 | async-start | bytes 262144 | tf_op jit(solution)/shard_map/all_to_all | solution.py:30
  12.6 0.9 fusion.111
  13.5 1.8 %gather_fusion.1 = bf16[4,64,512]{2,1,0:T(8,128)(2,1)S(1)} fusion(bf16[16,64,512]{2,1,0:T(8,128)(2,1)} %param.26, s32[1024]{0:T(1024)S(1)} %get-tuple-element.143), kind=kCustom, calls=%fused_computation.1 | custom fusion | bytes 524304 | tf_op jit(solution)/shard_map/gather | solution.py:208
  15.4 0.7 constant_dynamic-slice_fusion.8
  16.0 3.5 %collective-permute-start.2 = (bf16[256,256]{1,0:T(8,128)(2,1)}, bf16[256,256]{1,0:T(8,128)(2,1)}, u32[]{:S(2)}, u32[]{:S(2)}) collective-permute-start(bf16[256,256]{1,0:T(8,128)(2,1)} %constant_dynamic-slice_fusion.8), channel_id=1, source_target_pairs={{508,0},{0,4},{4,8},{8,12},{12,16},{16,20},{20,24},{24,28},{28,32}... | collective-permute-start | bytes 393224 | tf_op jit(solution)/shard_map/ppermute | solution.py:48
  19.6 0.6 gather_fusion.3
  20.2 0.7 constant_dynamic-slice_fusion.4
  20.8 9.8 %collective-permute-start.4 = (bf16[256,256]{1,0:T(8,128)(2,1)}, bf16[256,256]{1,0:T(8,128)(2,1)}, u32[]{:S(2)}, u32[]{:S(2)}) collective-permute-start(bf16[256,256]{1,0:T(8,128)(2,1)} %constant_dynamic-slice_fusion.4), channel_id=1, source_target_pairs={{8,0},{12,4},{16,8},{20,12},{24,16},{28,20},{32,24},{36,28},{40,32... | collective-permute-start | bytes 393224 | tf_op jit(solution)/shard_map/ppermute | solution.py:48
  30.7 0.6 gather_fusion
  31.2 0.7 constant_dynamic-slice_fusion.9
  31.9 1.9 %collective-permute-start.1 = (bf16[256,256]{1,0:T(8,128)(2,1)}, bf16[256,256]{1,0:T(8,128)(2,1)}, u32[]{:S(2)}, u32[]{:S(2)}) collective-permute-start(bf16[256,256]{1,0:T(8,128)(2,1)} %constant_dynamic-slice_fusion.9), channel_id=1, source_target_pairs={{504,0},{508,4},{0,8},{4,12},{8,16},{12,20},{16,24},{20,28},{24,32... | collective-permute-start | bytes 393224 | tf_op jit(solution)/shard_map/ppermute | solution.py:48
  33.8 0.6 gather_fusion.2
  34.4 0.7 constant_dynamic-slice_fusion.6
  35.0 2.7 %collective-permute-start.3 = (bf16[256,256]{1,0:T(8,128)(2,1)}, bf16[256,256]{1,0:T(8,128)(2,1)}, u32[]{:S(2)}, u32[]{:S(2)}) collective-permute-start(bf16[256,256]{1,0:T(8,128)(2,1)} %constant_dynamic-slice_fusion.6), channel_id=1, source_target_pairs={{4,0},{8,4},{12,8},{16,12},{20,16},{24,20},{28,24},{32,28},{36,32}... | collective-permute-start | bytes 393224 | tf_op jit(solution)/shard_map/ppermute | solution.py:48
  37.8 0.7 fusion.130
  39.3 3.1 %fusion.85 = s32[1280]{0:T(1024)S(1)} fusion(s32[]{:T(128)} %bitcast.2, s32[]{:T(128)} %bitcast.3, s32[]{:T(128)} %bitcast.4, s32[]{:T(128)} %bitcast.6, s32[]{:T(128)} %bitcast.5), kind=kLoop, calls=%fused_computation.174 | loop fusion | flops 32000 | bytes 5140 | tf_op jit(solution)/shard_map/gather | solution.py:168
  42.5 0.9 fusion.105
  43.3 1.2 iota_compare_fusion.8
  44.5 0.5 iota_compare_fusion.7
  45.1 0.7 iota_compare_fusion.6
  45.8 0.6 iota_compare_fusion.5
  46.4 1.2 iota_compare_fusion.4
  47.6 1.2 iota_compare_fusion.10
  48.8 0.7 fusion.131
  49.4 0.6 add_convert_fusion.2
  50.0 1.2 multiply_cosine_fusion
  51.6 1.3 iota_compare_fusion.9
  52.9 0.9 broadcast_in_dim.264
  53.9 4.0 %all-to-all-start = ((bf16[4,256,384]{2,1,0:T(8,128)(2,1)}), bf16[4,256,384]{2,1,0:T(8,128)(2,1)S(1)}, u32[]{:S(2)}, u32[]{:S(2)}) async-start(bf16[4,256,384]{2,1,0:T(8,128)(2,1)} %broadcast_in_dim.264), calls=%async_computation | async-start | bytes 1572864 | tf_op jit(solution)/shard_map/all_to_all | solution.py:21
  57.9 1.2 iota_compare_fusion.11
  85.3 0.7 broadcast_in_dim.270
  86.0 3.6 %all-to-all-start.2 = ((bf16[8,5,16,256]{3,2,1,0:T(8,128)(2,1)}), bf16[8,5,16,256]{3,2,1,0:T(8,128)(2,1)S(1)}, u32[]{:S(2)}, u32[]{:S(2)}) async-start(bf16[8,5,16,256]{3,2,1,0:T(8,128)(2,1)} %broadcast_in_dim.270), calls=%async_computation.2 | async-start | bytes 655360 | tf_op jit(solution)/shard_map/all_to_all | solution.py:21
  90.0 0.9 copy-done.21
  90.9 0.6 convolution_add_fusion
  91.7 0.7 fusion.128
  92.4 1.5 convolution_add_fusion.1
  93.9 0.3 fusion.63
  94.2 3.6 %collective-permute-start = (bf16[256,128]{0,1:T(8,128)(2,1)S(1)}, bf16[256,128]{0,1:T(8,128)(2,1)}, u32[]{:S(2)}, u32[]{:S(2)}) collective-permute-start(bf16[256,128]{0,1:T(8,128)(2,1)S(1)} %fusion.58), channel_id=1, source_target_pairs={{0,1},{1,0},{2,3},{3,2},{4,5},{5,4},{6,7},{7,6},{8,9},{9,8},{10,11... | collective-permute-start | bytes 196616 | tf_op jit(solution)/shard_map/ppermute | solution.py:16
  98.0 1.1 copy.71
  99.4 1.2 fusion.134
  100.5 0.8 fusion.32
  101.4 1.2 fusion.133
  102.5 1.8 %convolution_select_fusion.3 = f32[128,3,128]{0,2,1:T(8,128)} fusion(f32[128,3,256]{2,0,1:T(8,128)S(1)} %get-tuple-element.129, f32[128,3]{0,1:T(4,128)S(1)} %get-tuple-element.128, pred[256]{0:T(512)(128)(4,1)S(1)} %iota_compare_fusion.7, pred[128]{0:T(512)(128)(4,1)S(1)} %copy-done.12, bf16[256,256]{1,0:T(8,128)(2,1)} %collective-permute-done.1), kind=kOutput, calls=%fused_computation.34 | convolution fusion | flops 25509888 | bytes 657280 | tf_op jit(solution)/shard_map/rhk,kd->rhd/dot_general | solution.py:98
  104.4 2.0 %dynamic_update_slice.48 = f32[384,3,128]{0,2,1:T(8,128)S(1)} dynamic-update-slice(f32[384,3,128]{0,2,1:T(8,128)S(1)} %broadcast_in_dim.284, f32[128,3,128]{0,2,1:T(8,128)} %convolution_select_fusion.3, s32[]{:T(128)S(6)} %select_n.414, s32[]{:T(128)} %constant.177.clone.1, s32[]{:T(128)} %constant.177.clone.1) | dynamic-update-slice | bytes 393220 | tf_op jit(solution)/shard_map/dynamic_update_slice | solution.py:226
  106.4 1.8 %convolution_select_fusion.2 = f32[128,3,128]{0,2,1:T(8,128)} fusion(f32[128,3,256]{2,0,1:T(8,128)S(1)} %get-tuple-element.131, f32[384,3,128]{0,2,1:T(8,128)S(1)} %dynamic_update_slice.48, s32[]{:T(128)S(6)} %select_n.421, f32[128,3]{0,1:T(4,128)S(1)} %get-tuple-element.130, pred[256]{0:T(512)(128)(4,1)} %copy-done.11, ...), kind=kOutput, calls=%fused_computation.33 | convolution fusion | flops 25509888 | bytes 854532 | tf_op jit(solution)/shard_map/rhk,kd->rhd/dot_general | solution.py:98
  108.3 1.4 dynamic_update_slice.49
  110.0 1.2 fusion.135
  111.4 1.2 convolution_select_fusion.1
  112.5 1.3 dynamic_update_slice.50
  115.4 1.2 fusion.136
  116.6 1.2 convolution_select_fusion
  118.0 0.7 dynamic_update_slice.51
  119.1 0.9 broadcast_select_fusion
  120.3 22.1 %all-gather = bf16[80,16,256]{2,1,0:T(8,128)(2,1)S(1)} all-gather(bf16[5,16,256]{2,1,0:T(8,128)(2,1)S(1)} %constant_dynamic-update-slice_fusion.5), channel_id=2, replica_groups=mesh['z'=8,'y'=8,'core'=2,'tp'=4] {'y','core'}, dimensions={0}, use_global_device_ids=true | all-gather | bytes 696320 | tf_op jit(solution)/shard_map/all_gather | solution.py:41
  142.5 1.1 fusion
  143.6 1.6 fusion.1
  145.2 1.5 fusion.22
  146.7 0.6 convolution_convert_fusion
  147.4 1.0 pad_maximum_fusion.1
  148.4 3.8 %all-to-all-start.3 = ((bf16[4,256,384]{2,1,0:T(8,128)(2,1)}), bf16[4,256,384]{2,1,0:T(8,128)(2,1)S(1)}, u32[]{:S(2)}, u32[]{:S(2)}) async-start(bf16[4,256,384]{2,1,0:T(8,128)(2,1)} %pad_maximum_fusion.1), calls=%async_computation.3 | async-start | bytes 1572864 | tf_op jit(solution)/shard_map/all_to_all | solution.py:245
  152.2 0.7 copy.60
  152.9 11.2 %all-to-all-done.3 = bf16[4,256,384]{2,1,0:T(8,128)(2,1)S(1)} async-done(((bf16[4,256,384]{2,1,0:T(8,128)(2,1)}), bf16[4,256,384]{2,1,0:T(8,128)(2,1)S(1)}, u32[]{:S(2)}, u32[]{:S(2)}) %all-to-all-start.3) | async-done | bytes 786464 | tf_op jit(solution)/shard_map/all_to_all | solution.py:245
  164.3 0.7 add_convert_fusion
  (120 shorter events, 5.5 us)
Async XLA Ops:
  0.6 146.1 %copy-start = (bf16[384,1536]{1,0:T(8,128)(2,1)S(1)}, bf16[384,1536]{1,0:T(8,128)(2,1)}, u32[]{:S(2)}) copy-start(bf16[384,1536]{1,0:T(8,128)(2,1)} %param.22) | copy-start | bytes 3538948
  0.6 18.9 %copy-start.1 = (bf16[16,64,512]{2,1,0:T(8,128)(2,1)S(1)}, bf16[16,64,512]{2,1,0:T(8,128)(2,1)}, u32[]{:S(2)}) copy-start(bf16[16,64,512]{2,1,0:T(8,128)(2,1)} %param.26) | copy-start | bytes 3145732
  2.4 50.5 %all-to-all-start.1 = ((bf16[16,16,256]{2,1,0:T(8,128)(2,1)}), bf16[16,16,256]{2,1,0:T(8,128)(2,1)S(1)}, u32[]{:S(2)}, u32[]{:S(2)}) async-start(bf16[16,16,256]{2,1,0:T(8,128)(2,1)} %bitcast.14), calls=%async_computation.1 | async-start | bytes 262144 | tf_op jit(solution)/shard_map/all_to_all | solution.py:30
  13.5 24.3 %copy-start.8 = (s32[5]{0:T(128)S(1)}, s32[5]{0:T(128)}, u32[]{:S(2)}) copy-start(s32[5]{0:T(128)} %param.24) | copy-start | bytes 64
  13.5 25.0 %copy-start.18 = (s32[1,4]{1,0:T(1,128)S(1)}, s32[1,4]{1,0:T(1,128)}, u32[]{:S(2)}) copy-start(s32[1,4]{1,0:T(1,128)} %param.29) | copy-start | bytes 52
  13.5 25.5 %copy-start.24 = (s32[5]{0:T(128)S(1)}, s32[5]{0:T(128)}, u32[]{:S(2)}) copy-start(s32[5]{0:T(128)} %param.25) | copy-start | bytes 64
  13.5 25.6 %copy-start.17 = (s32[1,4]{1,0:T(1,128)S(1)}, s32[1,4]{1,0:T(1,128)}, u32[]{:S(2)}) copy-start(s32[1,4]{1,0:T(1,128)} %param.28) | copy-start | bytes 52
  13.5 25.6 %copy-start.20 = (s32[1,4]{1,0:T(1,128)S(1)}, s32[1,4]{1,0:T(1,128)}, u32[]{:S(2)}) copy-start(s32[1,4]{1,0:T(1,128)} %param.31) | copy-start | bytes 52
  13.5 29.0 %copy-start.19 = (s32[1,4]{1,0:T(1,128)S(1)}, s32[1,4]{1,0:T(1,128)}, u32[]{:S(2)}) copy-start(s32[1,4]{1,0:T(1,128)} %param.30) | copy-start | bytes 52
  16.0 83.3 %collective-permute-start.2 = (bf16[256,256]{1,0:T(8,128)(2,1)}, bf16[256,256]{1,0:T(8,128)(2,1)}, u32[]{:S(2)}, u32[]{:S(2)}) collective-permute-start(bf16[256,256]{1,0:T(8,128)(2,1)} %constant_dynamic-slice_fusion.8), channel_id=1, source_target_pairs={{508,0},{0,4},{4,8},{8,12},{12,16},{16,20},{20,24},{24,28},{28,32}... | collective-permute-start | bytes 393224 | tf_op jit(solution)/shard_map/ppermute | solution.py:48
  20.8 94.5 %collective-permute-start.4 = (bf16[256,256]{1,0:T(8,128)(2,1)}, bf16[256,256]{1,0:T(8,128)(2,1)}, u32[]{:S(2)}, u32[]{:S(2)}) collective-permute-start(bf16[256,256]{1,0:T(8,128)(2,1)} %constant_dynamic-slice_fusion.4), channel_id=1, source_target_pairs={{8,0},{12,4},{16,8},{20,12},{24,16},{28,20},{32,24},{36,28},{40,32... | collective-permute-start | bytes 393224 | tf_op jit(solution)/shard_map/ppermute | solution.py:48
  30.6 22.3 %copy-start.2 = (bf16[256,384]{1,0:T(8,128)(2,1)S(1)}, bf16[256,384]{1,0:T(8,128)(2,1)}, u32[]{:S(2)}) copy-start(bf16[256,384]{1,0:T(8,128)(2,1)} %param.16) | copy-start | bytes 589828
  31.9 69.5 %collective-permute-start.1 = (bf16[256,256]{1,0:T(8,128)(2,1)}, bf16[256,256]{1,0:T(8,128)(2,1)}, u32[]{:S(2)}, u32[]{:S(2)}) collective-permute-start(bf16[256,256]{1,0:T(8,128)(2,1)} %constant_dynamic-slice_fusion.9), channel_id=1, source_target_pairs={{504,0},{508,4},{0,8},{4,12},{8,16},{12,20},{16,24},{20,28},{24,32... | collective-permute-start | bytes 393224 | tf_op jit(solution)/shard_map/ppermute | solution.py:48
  35.0 74.9 %collective-permute-start.3 = (bf16[256,256]{1,0:T(8,128)(2,1)}, bf16[256,256]{1,0:T(8,128)(2,1)}, u32[]{:S(2)}, u32[]{:S(2)}) collective-permute-start(bf16[256,256]{1,0:T(8,128)(2,1)} %constant_dynamic-slice_fusion.6), channel_id=1, source_target_pairs={{4,0},{8,4},{12,8},{16,12},{20,16},{24,20},{28,24},{32,28},{36,32}... | collective-permute-start | bytes 393224 | tf_op jit(solution)/shard_map/ppermute | solution.py:48
  45.8 54.8 %copy-start.11 = (pred[256]{0:T(512)(128)(4,1)}, pred[256]{0:T(512)(128)(4,1)S(1)}, u32[]{:S(2)}) copy-start(pred[256]{0:T(512)(128)(4,1)S(1)} %iota_compare_fusion.6) | copy-start | bytes 772
  53.9 31.4 %all-to-all-start = ((bf16[4,256,384]{2,1,0:T(8,128)(2,1)}), bf16[4,256,384]{2,1,0:T(8,128)(2,1)S(1)}, u32[]{:S(2)}, u32[]{:S(2)}) async-start(bf16[4,256,384]{2,1,0:T(8,128)(2,1)} %broadcast_in_dim.264), calls=%async_computation | async-start | bytes 1572864 | tf_op jit(solution)/shard_map/all_to_all | solution.py:21
  86.0 3.9 %copy-start.22 = (f32[1536]{0:T(1024)S(1)}, f32[1536]{0:T(1024)}, u32[]{:S(2)}) copy-start(f32[1536]{0:T(1024)} %param.17) | copy-start | bytes 18436
  86.0 3.9 %copy-start.23 = (f32[384]{0:T(512)S(1)}, f32[384]{0:T(512)}, u32[]{:S(2)}) copy-start(f32[384]{0:T(512)} %param.19) | copy-start | bytes 4612
  86.0 34.2 %all-to-all-start.2 = ((bf16[8,5,16,256]{3,2,1,0:T(8,128)(2,1)}), bf16[8,5,16,256]{3,2,1,0:T(8,128)(2,1)S(1)}, u32[]{:S(2)}, u32[]{:S(2)}) async-start(bf16[8,5,16,256]{3,2,1,0:T(8,128)(2,1)} %broadcast_in_dim.270), calls=%async_computation.2 | async-start | bytes 655360 | tf_op jit(solution)/shard_map/all_to_all | solution.py:21
  89.6 1.3 copy-start.21
  91.5 0.9 copy-start.25
  93.9 5.2 %copy-start.4 = (f32[256,64]{1,0:T(8,128)S(1)}, f32[256,64]{1,0:T(8,128)}, u32[]{:S(2)}) copy-start(f32[256,64]{1,0:T(8,128)} %get-tuple-element.95) | copy-start | bytes 196612
  93.9 5.2 %copy-start.5 = (f32[256,64]{1,0:T(8,128)S(1)}, f32[256,64]{1,0:T(8,128)}, u32[]{:S(2)}) copy-start(f32[256,64]{1,0:T(8,128)} %get-tuple-element.96) | copy-start | bytes 196612
  94.2 24.9 %collective-permute-start = (bf16[256,128]{0,1:T(8,128)(2,1)S(1)}, bf16[256,128]{0,1:T(8,128)(2,1)}, u32[]{:S(2)}, u32[]{:S(2)}) collective-permute-start(bf16[256,128]{0,1:T(8,128)(2,1)S(1)} %fusion.58), channel_id=1, source_target_pairs={{0,1},{1,0},{2,3},{3,2},{4,5},{5,4},{6,7},{7,6},{8,9},{9,8},{10,11... | collective-permute-start | bytes 196616 | tf_op jit(solution)/shard_map/ppermute | solution.py:16
  99.1 3.4 %copy-start.12 = (pred[128]{0:T(512)(128)(4,1)S(1)}, pred[128]{0:T(512)(128)(4,1)}, u32[]{:S(2)}) copy-start(pred[128]{0:T(512)(128)(4,1)} %iota_compare_fusion.11) | copy-start | bytes 388
  100.5 7.7 %copy-start.6 = (f32[128,3]{0,1:T(4,128)}, f32[128,3]{0,1:T(4,128)S(1)}, u32[]{:S(2)}) copy-start(f32[128,3]{0,1:T(4,128)S(1)} %get-tuple-element.130) | copy-start | bytes 4612
  108.2 5.6 %copy-start.13 = (pred[128]{0:T(512)(128)(4,1)S(1)}, pred[128]{0:T(512)(128)(4,1)}, u32[]{:S(2)}) copy-start(pred[128]{0:T(512)(128)(4,1)} %iota_compare_fusion.11) | copy-start | bytes 388
  108.2 6.2 %copy-start.9 = (f32[128,3]{0,1:T(4,128)S(1)}, f32[128,3]{0,1:T(4,128)}, u32[]{:S(2)}) copy-start(f32[128,3]{0,1:T(4,128)} %fusion.32) | copy-start | bytes 4612
  108.3 6.2 %copy-start.15 = (pred[128]{0:T(512)(128)(4,1)S(1)}, pred[128]{0:T(512)(128)(4,1)}, u32[]{:S(2)}) copy-start(pred[128]{0:T(512)(128)(4,1)} %iota_compare_fusion.10) | copy-start | bytes 388
  108.3 6.6 %copy-start.16 = (pred[128]{0:T(512)(128)(4,1)S(1)}, pred[128]{0:T(512)(128)(4,1)}, u32[]{:S(2)}) copy-start(pred[128]{0:T(512)(128)(4,1)} %iota_compare_fusion.9) | copy-start | bytes 388
  108.3 7.1 %copy-start.10 = (pred[256]{0:T(512)(128)(4,1)S(1)}, pred[256]{0:T(512)(128)(4,1)}, u32[]{:S(2)}) copy-start(pred[256]{0:T(512)(128)(4,1)} %iota_compare_fusion.4) | copy-start | bytes 772
  109.7 4.7 %copy-start.7 = (f32[128,3]{0,1:T(4,128)S(1)}, f32[128,3]{0,1:T(4,128)}, u32[]{:S(2)}) copy-start(f32[128,3]{0,1:T(4,128)} %copy-done.6) | copy-start | bytes 4612
  110.0 6.6 %copy-start.14 = (pred[128]{0:T(512)(128)(4,1)S(1)}, pred[128]{0:T(512)(128)(4,1)}, u32[]{:S(2)}) copy-start(pred[128]{0:T(512)(128)(4,1)} %iota_compare_fusion.8) | copy-start | bytes 388
  148.4 15.9 %copy-start.3 = (bf16[256,384]{1,0:T(8,128)(2,1)S(1)}, bf16[256,384]{1,0:T(8,128)(2,1)}, u32[]{:S(2)}) copy-start(bf16[256,384]{1,0:T(8,128)(2,1)} %param.16) | copy-start | bytes 589828
  148.4 15.8 %all-to-all-start.3 = ((bf16[4,256,384]{2,1,0:T(8,128)(2,1)}), bf16[4,256,384]{2,1,0:T(8,128)(2,1)S(1)}, u32[]{:S(2)}, u32[]{:S(2)}) async-start(bf16[4,256,384]{2,1,0:T(8,128)(2,1)} %pad_maximum_fusion.1), calls=%async_computation.3 | async-start | bytes 1572864 | tf_op jit(solution)/shard_map/all_to_all | solution.py:245

commit v2 on v1

v2 whole, which is shorter than its diff:
```python
import math

import jax
import jax.numpy as jnp
from jax import lax
from jax.experimental import pallas as pl
from jax.experimental.pallas import tpu as pltpu
from jax.sharding import Mesh, PartitionSpec as P

norm_eps = 1e-06
rope_base = 1000000.0
neighbour_steps = (-2, -1, 1, 2)
seq_axes = ("z", "y", "core")
barred = -(2.0**100)
f32 = jnp.float32
bf16 = jnp.bfloat16
int32 = jnp.int32


def passed_along(block, axis, distance):
    devices = range(math.prod(lax.axis_size(name) for name in axis))
    return lax.ppermute(block, axis, [((i - distance) % len(devices), i) for i in devices])


def copies_exchanged(block, axis, count):
    copies = jnp.broadcast_to(block[None], (count,) + block.shape)
    return lax.all_to_all(copies, axis, 0, 0, tiled=True)


def gathered_nodes(head_columns, shared_owner):
    z_count = lax.axis_size("z")
    plane_count = lax.axis_size("y") * lax.axis_size("core")
    rows, columns = head_columns.shape
    chunk = rows // plane_count
    pieces = head_columns.reshape(plane_count, chunk, columns)
    arrived = lax.all_to_all(pieces, ("y", "core"), 0, 0, tiled=True)
    in_plane = shared_owner % plane_count
    plane = shared_owner // plane_count
    node_total = shared_owner.shape[0]
    chosen = jnp.stack(
        [lax.dynamic_index_in_dim(arrived, in_plane[n], 0, False) for n in range(node_total)]
    )
    planes = copies_exchanged(chosen, "z", z_count)
    kept = jnp.stack(
        [lax.dynamic_index_in_dim(planes[:, n], plane[n], 0, False) for n in range(node_total)]
    )
    return lax.all_gather(kept, ("y", "core"), axis=0, tiled=False)


def pages_kernel(page_ref, group_ref, pool_ref, *rest):
    outs, sems = rest[:-1], rest[-1]
    page_rows = pool_ref.shape[1]
    width = outs[0].shape[1]
    per_slot = outs[0].shape[0] // page_rows
    first = pl.multiple_of(group_ref[0] * width, width)
    copies = []
    for slot, out in enumerate(outs):
        for c in range(per_slot):
            n = slot * per_slot + c
            copies.append(
                pltpu.make_async_copy(
                    pool_ref.at[page_ref[n], :, pl.ds(first, width)],
                    out.at[pl.ds(c * page_rows, page_rows), :],
                    sems.at[n],
                )
            )
    for copy in copies:
        copy.start()
    for copy in copies:
        copy.wait()


def history_slots(hist_pool, pages, kv_group, slots, width):
    rows = pages.shape[0] // slots * hist_pool.shape[1]
    anywhere = pl.BlockSpec(memory_space=pl.ANY)
    return pl.pallas_call(
        pages_kernel,
        out_shape=[jax.ShapeDtypeStruct((rows, width), bf16)] * slots,
        grid_spec=pltpu.PrefetchScalarGridSpec(
            num_scalar_prefetch=2,
            grid=(),
            in_specs=[anywhere],
            out_specs=[anywhere] * slots,
            scratch_shapes=[pltpu.SemaphoreType.DMA((pages.shape[0],))],
        ),
        name="pages",
    )(pages, kv_group.reshape(1), hist_pool)


def projection_kernel(
    holds_ref, tok_ref, gain_ref, wq_ref, wkv_ref, qb_ref, kb_ref, cos_ref, sin_ref, q_ref, own_ref
):
    groups, rows, width = tok_ref.shape
    total = jnp.zeros((rows, 1), f32)
    for g in range(groups):
        block = tok_ref[g].astype(f32)
        total = total + jnp.sum(block * block, axis=1, keepdims=True)
    inverse = lax.rsqrt(total / (groups * width) + norm_eps)
    query = jnp.zeros((rows, wq_ref.shape[1]), f32)
    fresh = jnp.zeros((rows, wkv_ref.shape[1]), f32)
    for g in range(groups):
        span = pl.ds(g * width, width)
        normed = (tok_ref[g].astype(f32) * inverse * gain_ref[:, span]).astype(bf16)
        query = query + jnp.dot(normed, wq_ref[span, :], preferred_element_type=f32)
        fresh = fresh + jnp.dot(normed, wkv_ref[span, :], preferred_element_type=f32)
    cosine = cos_ref[...]
    sine = sin_ref[...]
    half = cosine.shape[1] // 2

    def turned(part):
        return part * cosine + pltpu.roll(part, half, 1) * sine

    query = query + qb_ref[...]
    dim = cosine.shape[1]
    for h in range(q_ref.shape[0]):
        q_ref[h] = turned(query[:, h * dim : (h + 1) * dim]).astype(bf16)
    fresh = fresh + kb_ref[...]

    @pl.when(holds_ref[0] == 1)
    def _():
        own_ref[...] = turned(fresh).astype(bf16)

    @pl.when(holds_ref[0] == 0)
    def _():
        own_ref[...] = fresh.astype(bf16)


def attention_kernel(
    info_ref, q_ref, own_ref, partner_ref, h0_ref, h1_ref, h2_ref, h3_ref, hot_ref, wo_ref,
    out_ref, key_ref, value_ref,
):
    heads, rows, dim = q_ref.shape
    hist_refs = (h0_ref, h1_ref, h2_ref, h3_ref)
    requests = len(hist_refs)
    starts = [info_ref[r] for r in range(requests)]
    hist_len = [info_ref[4 + r] for r in range(requests)]
    slot = [info_ref[8 + r] for r in range(requests)]
    parent = [info_ref[12 + r] for r in range(requests)]
    shared_len = [info_ref[16 + n] for n in range(5)]
    holds = info_ref[21]

    @pl.when(holds == 1)
    def _():
        key_ref[...] = own_ref[...]
        value_ref[...] = partner_ref[...]

    @pl.when(holds == 0)
    def _():
        key_ref[...] = partner_ref[...]
        value_ref[...] = own_ref[...]

    def by_request(index, values):
        picked = jnp.full(index.shape, values[0], int32)
        for r in range(1, requests):
            picked = jnp.where(index >= starts[r], values[r], picked)
        return picked

    row = lax.broadcasted_iota(int32, (rows, dim), 0)
    lane = lax.broadcasted_iota(int32, (rows, dim), 1)
    hit = (
        (lane == by_request(row, slot))
        | (lane == requests + by_request(row, parent))
        | (lane == 2 * requests)
    )
    marks = jnp.where(hit, 1.0, 0.0).astype(bf16)

    def bars(bad):
        return jnp.where(bad, barred, 0.0).astype(bf16)

    keys = []
    values = []
    for j in range(requests):
        deep = jnp.int32(0)
        for r in range(requests):
            deep = deep + jnp.where(slot[r] == j, hist_len[r], 0)
        place = lax.broadcasted_iota(int32, (hist_refs[j].shape[0], dim), 0)
        side = lax.broadcasted_iota(int32, (hist_refs[j].shape[0], dim), 1)
        bad = ((side < requests) & (side != j)) | ((side == 2 * requests) & (place >= deep))
        keys.append(jnp.concatenate([hist_refs[j][:, :dim], bars(bad)], axis=1))
        values.append(hist_refs[j][:, dim:])

    chunks, nodes, chunk, _ = hot_ref.shape
    index = lax.broadcasted_iota(int32, (nodes * chunk, dim), 0)
    side = lax.broadcasted_iota(int32, (nodes * chunk, dim), 1)
    node = jnp.zeros(index.shape, int32)
    left = jnp.full(index.shape, shared_len[0], int32)
    for n in range(1, nodes):
        node = jnp.where(index >= n * chunk, n, node)
        left = jnp.where(index >= n * chunk, shared_len[n], left)
    left = left - (index - node * chunk)
    other = (side >= requests) & (side < 2 * requests) & (node > 0) & (side != requests + node - 1)
    last = side == 2 * requests
    for s in range(chunks):
        block = hot_ref[s].reshape(nodes * chunk, 2 * dim)
        bad = other | (last & (left <= s * chunk))
        keys.append(jnp.concatenate([block[:, :dim], bars(bad)], axis=1))
        values.append(block[:, dim:])

    far_keys = jnp.concatenate(keys, axis=0)
    far_values = jnp.concatenate(values, axis=0)
    far_values = jnp.concatenate([far_values, jnp.ones_like(far_values)], axis=1)
    own_keys = key_ref[...]
    own_values = value_ref[...]
    own_values = jnp.concatenate([own_values, jnp.ones_like(own_values)], axis=1)

    wide_row = lax.broadcasted_iota(int32, (rows, rows), 0)
    wide_col = lax.broadcasted_iota(int32, (rows, rows), 1)
    numbers = list(range(requests))
    seen = (wide_col <= wide_row) & (by_request(wide_row, numbers) == by_request(wide_col, numbers))
    hidden_keys = jnp.where(seen, 0.0, barred)

    scale = dim ** (-0.5) * math.log2(math.e)
    across = (((1,), (1,)), ((), ()))
    merged = []
    for h in range(heads):
        query = q_ref[h]
        far = lax.dot_general(
            jnp.concatenate([query, marks], axis=1), far_keys, across, preferred_element_type=f32
        )
        own = lax.dot_general(query, own_keys, across, preferred_element_type=f32) + hidden_keys
        top = jnp.maximum(
            jnp.max(far, axis=1, keepdims=True), jnp.max(own, axis=1, keepdims=True)
        )
        far_weights = jnp.exp2((far - top) * scale).astype(bf16)
        own_weights = jnp.exp2((own - top) * scale).astype(bf16)
        mixed = jnp.dot(far_weights, far_values, preferred_element_type=f32) + jnp.dot(
            own_weights, own_values, preferred_element_type=f32
        )
        merged.append((mixed[:, :dim] / mixed[:, dim:]).astype(bf16))
    attention = jnp.concatenate(merged, axis=1)
    width = out_ref.shape[2]
    for g in range(out_ref.shape[0]):
        out_ref[g] = jnp.dot(
            attention, wo_ref[:, g * width : (g + 1) * width], preferred_element_type=f32
        ).astype(bf16)


def whole(count):
    return [pl.BlockSpec(memory_space=pltpu.VMEM)] * count


def on_device(
    tokens,
    norm_gain,
    query_weight,
    query_bias,
    kv_weight,
    kv_bias,
    out_weight,
    shared_slot,
    shared_len,
    shared_owner,
    hist_pool,
    hist_pages,
    hist_len,
    req_len,
    req_offset,
    req_parent,
):
    group_count = lax.axis_size("tp")
    row_count, width = tokens.shape
    head_dim = kv_bias.shape[0]
    head_count = query_weight.shape[1] // head_dim
    request_count = req_len.shape[1]
    tp_index = lax.axis_index("tp")
    kv_group = tp_index // 2
    holds_key = (tp_index % 2 == 0).astype(int32)
    scalars = pl.BlockSpec(memory_space=pltpu.SMEM)

    head_columns = lax.dynamic_slice_in_dim(shared_slot, kv_group * 2 * head_dim, 2 * head_dim, 1)
    hot = gathered_nodes(head_columns, shared_owner)
    features = copies_exchanged(tokens, "tp", group_count)
    slots = history_slots(hist_pool, hist_pages[0], kv_group, request_count, 2 * head_dim)
    histories = [
        passed_along(slots[j], seq_axes, -neighbour_steps[j]) for j in range(request_count)
    ]

    starts = jnp.cumsum(req_len[0]) - req_len[0]
    base = shared_len[0] + shared_len[1 + req_parent[0]] + hist_len[0] - starts
    row = jnp.arange(row_count, dtype=int32)[:, None]
    shift = jnp.broadcast_to(base[0], row.shape)
    for r in range(1, request_count):
        shift = jnp.where(row >= starts[r], base[r], shift)
    half = head_dim // 2
    frequency = rope_base ** (-2.0 * jnp.arange(half, dtype=f32) / head_dim)
    angle = (row + shift).astype(f32) * frequency[None, :]
    cosine = jnp.cos(angle)
    sine = jnp.sin(angle)
    cosine = jnp.concatenate([cosine, cosine], axis=1)
    sine = jnp.concatenate([-sine, sine], axis=1)

    queries, own_block = pl.pallas_call(
        projection_kernel,
        out_shape=[
            jax.ShapeDtypeStruct((head_count, row_count, head_dim), bf16),
            jax.ShapeDtypeStruct((row_count, head_dim), bf16),
        ],
        in_specs=[scalars] + whole(8),
        out_specs=whole(2),
        compiler_params=pltpu.CompilerParams(vmem_limit_bytes=32 * 2**20),
        name="projection",
    )(
        holds_key.reshape(1),
        features,
        norm_gain[None, :],
        query_weight,
        kv_weight,
        query_bias[None, :],
        kv_bias[None, :],
        cosine,
        sine,
    )
    partner = lax.ppermute(own_block, "tp", [(i, i ^ 1) for i in range(group_count)])
    info = jnp.concatenate(
        [starts, hist_len[0], req_offset[0], req_parent[0], shared_len, holds_key.reshape(1)]
    ).astype(int32)
    blocks = pl.pallas_call(
        attention_kernel,
        out_shape=jax.ShapeDtypeStruct((group_count, row_count, width), bf16),
        in_specs=[scalars] + whole(9),
        out_specs=whole(1)[0],
        scratch_shapes=[pltpu.VMEM((row_count, head_dim), bf16)] * 2,
        compiler_params=pltpu.CompilerParams(vmem_limit_bytes=48 * 2**20),
        name="attention",
    )(info, queries, own_block, partner, *histories, hot, out_weight)
    summed = jnp.sum(lax.all_to_all(blocks, "tp", 0, 0, tiled=True).astype(f32), axis=0)
    hidden = (summed + tokens.astype(f32)).astype(bf16)
    return (hidden, own_block)


def solution(mesh):
    devices = mesh.devices
    split = Mesh(devices.reshape(8, devices.shape[0] // 16, 2, devices.shape[1]), seq_axes + ("tp",))
    by_seq = P(seq_axes, None)
    return jax.shard_map(
        on_device,
        mesh=split,
        in_specs=(
            P(seq_axes, "tp"),
            P(),
            P(None, "tp"),
            P("tp"),
            P(None, "tp"),
            P("tp"),
            P("tp", None),
            by_seq,
            P(),
            P(),
            P(seq_axes, None, None),
            by_seq,
            by_seq,
            by_seq,
            by_seq,
            by_seq,
        ),
        out_specs=(P(seq_axes, "tp"), P(seq_axes, "tp")),
        check_vma=False,
    )
```

time: 167 us -> 143 us (0.86)
  Pallas kernels: 0 us -> 24.3 us
  local copies, waits for them, and re-layouts: 22.6 us -> 5.61 us
  other arithmetic: 22.5 us -> 6.36 us
  matrix products: 15.9 us -> 0 us
  blocking collectives: 22.1 us -> 32.7 us
  between operations: 27.6 us -> 19.9 us
  starting transfers between devices: 43 us -> 38.6 us
  waiting for transfers between devices: 11.2 us -> 14.8 us
    pallas_call x0 -> x3, Pallas kernels: none -> 24.3 us  [the longest x1 17.9 us: history_slots(): pl.pallas_call(pages_kernel, out_shape=[jax.ShapeDtypeStruct((rows, width...]
    all_to_all x0 -> x1, blocking collectives: none -> 16.1 us  [on_device(): lax.all_to_all(blocks, 'tp', 0, 0, tiled=True).astype(f32)]
    dot_general x13 -> x0, matrix products: 15.9 us -> none  [the longest x5 7.43 us: partial_attention(): jnp.einsum('rhk,kd->rhd', weights.astype(jnp.bfloat16), value_vectors, pr...]
    all_to_all x1 -> x0, waiting for transfers between devices: 11.2 us -> none  [on_device(): lax.all_to_all(blocks, 'tp', 0, 0, tiled=True).astype(jnp.float32)]
    lt x9 -> x0, other arithmetic: 7.87 us -> none  [the longest x4 4.84 us: on_device(): row_valid = capacity_rows < row_total]
    all_to_all x2, waiting for transfers between devices: 0.01 us -> 7.87 us  [copies_exchanged(): return lax.all_to_all(copies, axis, 0, 0, tiled=True)]
    dynamic_update_slice x12 -> x0, local copies, waits for them, and re-layouts: 7.06 us -> none  [put_rows(): lax.dynamic_update_slice_in_dim(whole_rows, jnp.where(keep_rows, fresh_pa...]
    all_to_all x1, waiting for transfers between devices: 0.01 us -> 6.89 us  [gathered_nodes(): arrived = lax.all_to_all(pieces, ('y', 'core'), 0, 0, tiled=True)]
  transfers between devices with their start and end apart: 9 -> 8, of which waited for: 1 -> 2; matrix products, arithmetic and copies ran while one was open for 31% -> 8% of each run, Pallas kernels for 0% -> 1%
where the time goes in v2:
time: 143 us; the launch traced here: 142 us
  starting transfers between devices  38.6 us (27%)
  blocking collectives  32.7 us (23%)
  Pallas kernels  24.3 us (17%)
  between operations  19.9 us (14%)
  waiting for transfers between devices  14.8 us (10%)
  other arithmetic  6.36 us (4%)
  local copies, waits for them, and re-layouts  5.61 us (4%)
    ppermute x4, starting transfers between devices, passed_along(): lax.ppermute(block, axis, [((i - distance) % len(devices), i) for i in de...  20.8 us
    pallas_call x1, Pallas kernels, history_slots(): pl.pallas_call(pages_kernel, out_shape=[jax.ShapeDtypeStruct((rows, width...  17.9 us
    all_gather x1, blocking collectives, gathered_nodes(): return lax.all_gather(kept, ('y', 'core'), axis=0, tiled=False)  16.6 us
    all_to_all x1, blocking collectives, on_device(): lax.all_to_all(blocks, 'tp', 0, 0, tiled=True).astype(f32)  16.1 us
    all_to_all x2, starting transfers between devices, copies_exchanged(): return lax.all_to_all(copies, axis, 0, 0, tiled=True)  9.1 us
    all_to_all x2, waiting for transfers between devices, copies_exchanged(): return lax.all_to_all(copies, axis, 0, 0, tiled=True)  7.87 us
    all_to_all x1, waiting for transfers between devices, gathered_nodes(): arrived = lax.all_to_all(pieces, ('y', 'core'), 0, 0, tiled=True)  6.89 us
    all_to_all x1, starting transfers between devices, gathered_nodes(): arrived = lax.all_to_all(pieces, ('y', 'core'), 0, 0, tiled=True)  5.31 us
  transfers between devices with their start and end apart: 8, of which 2 were waited for; matrix products, arithmetic and copies ran while one was open for 8% of the time, Pallas kernels for 1%

profile of v2, /device:TPU:1, one launch (start us, length us, event | category | flops | bytes accessed | tf_op | source)
XLA Modules:
  0.0 142.3 jit_solution(13183377744130382639)
XLA Ops:
  0.6 0.0 copy-start
  0.6 0.0 copy-start.13
  0.7 0.0 copy-start.12
  0.7 0.0 copy-start.6
  0.7 0.0 copy-start.10
  0.7 0.0 copy-start.15
  0.7 0.0 copy-start.7
  0.7 17.9 %pages.1 = (bf16[256,256]{1,0:T(8,128)(2,1)}, bf16[256,256]{1,0:T(8,128)(2,1)}, bf16[256,256]{1,0:T(8,128)(2,1)}, bf16[256,256]{1,0:T(8,128)(2,1)}) custom-call(s32[16]{0:T(128)} %bitcast.56, s32[1]{0:T(128)} %bitcast.20.group_ref, bf16[16,64,512]{2,1,0:T(8,128)(2,1)} %pool_ref.1), custom_call_target="tpu_custom_call" | custom-call | tf_op jit(solution)/shard_map/pages/pallas_call | solution.py:76
  18.7 4.0 %collective-permute-start.1 = (bf16[256,256]{1,0:T(8,128)(2,1)}, bf16[256,256]{1,0:T(8,128)(2,1)S(1)}, u32[]{:S(2)}, u32[]{:S(2)}) collective-permute-start(bf16[256,256]{1,0:T(8,128)(2,1)} %get-tuple-element.10), channel_id=1, source_target_pairs={{504,0},{508,4},{0,8},{4,12},{8,16},{12,20},{16,24},{20,28},{24,32... | collective-permute-start | bytes 393224 | tf_op jit(solution)/shard_map/ppermute | solution.py:22
  22.7 4.0 %collective-permute-start.2 = (bf16[256,256]{1,0:T(8,128)(2,1)}, bf16[256,256]{1,0:T(8,128)(2,1)S(1)}, u32[]{:S(2)}, u32[]{:S(2)}) collective-permute-start(bf16[256,256]{1,0:T(8,128)(2,1)} %get-tuple-element.11), channel_id=1, source_target_pairs={{508,0},{0,4},{4,8},{8,12},{12,16},{16,20},{20,24},{24,28},{28,32}... | collective-permute-start | bytes 393224 | tf_op jit(solution)/shard_map/ppermute | solution.py:22
  26.8 4.5 %collective-permute-start.3 = (bf16[256,256]{1,0:T(8,128)(2,1)}, bf16[256,256]{1,0:T(8,128)(2,1)S(1)}, u32[]{:S(2)}, u32[]{:S(2)}) collective-permute-start(bf16[256,256]{1,0:T(8,128)(2,1)} %get-tuple-element.12), channel_id=1, source_target_pairs={{4,0},{8,4},{12,8},{16,12},{20,16},{24,20},{28,24},{32,28},{36,32}... | collective-permute-start | bytes 393224 | tf_op jit(solution)/shard_map/ppermute | solution.py:22
  31.3 8.2 %collective-permute-start.4 = (bf16[256,256]{1,0:T(8,128)(2,1)}, bf16[256,256]{1,0:T(8,128)(2,1)S(1)}, u32[]{:S(2)}, u32[]{:S(2)}) collective-permute-start(bf16[256,256]{1,0:T(8,128)(2,1)} %get-tuple-element.13), channel_id=1, source_target_pairs={{8,0},{12,4},{16,8},{20,12},{24,16},{28,20},{32,24},{36,28},{40,32... | collective-permute-start | bytes 393224 | tf_op jit(solution)/shard_map/ppermute | solution.py:22
  39.5 0.0 copy-done
  39.5 0.7 constant_dynamic-slice_fusion
  40.2 5.3 %all-to-all-start.1 = ((bf16[16,16,256]{2,1,0:T(8,128)(2,1)}), bf16[16,16,256]{2,1,0:T(8,128)(2,1)S(1)}, u32[]{:S(2)}, u32[]{:S(2)}) async-start(bf16[16,16,256]{2,1,0:T(8,128)(2,1)} %bitcast.21), calls=%async_computation.1 | async-start | bytes 262144 | tf_op jit(solution)/shard_map/all_to_all | solution.py:36
  45.5 0.0 copy-done.13
  45.5 0.0 copy-done.12
  45.6 0.2 reduce-window.9
  45.7 0.0 copy-done.6
  45.7 0.6 gather_fusion
  46.4 0.0 copy-done.10
  46.4 0.0 copy-done.15
  46.5 0.7 fusion.7
  47.1 0.7 fusion.5
  47.8 0.0 copy-start.9
  47.8 0.0 copy-start.11
  47.8 0.0 copy-start.14
  47.8 6.9 %all-to-all-done.1 = bf16[16,16,256]{2,1,0:T(8,128)(2,1)S(1)} async-done(((bf16[16,16,256]{2,1,0:T(8,128)(2,1)}), bf16[16,16,256]{2,1,0:T(8,128)(2,1)S(1)}, u32[]{:S(2)}, u32[]{:S(2)}) %all-to-all-start.1) | async-done | bytes 131104 | tf_op jit(solution)/shard_map/all_to_all | solution.py:36
  54.7 0.0 copy-done.7
  54.7 1.0 broadcast_in_dim.37
  55.7 4.0 %all-to-all-start = ((bf16[4,256,384]{2,1,0:T(8,128)(2,1)}), bf16[4,256,384]{2,1,0:T(8,128)(2,1)S(1)}, u32[]{:S(2)}, u32[]{:S(2)}) async-start(bf16[4,256,384]{2,1,0:T(8,128)(2,1)} %broadcast_in_dim.37), calls=%async_computation | async-start | bytes 1572864 | tf_op jit(solution)/shard_map/all_to_all | solution.py:27
  59.7 0.0 copy-start.1
  59.7 4.6 %fusion.2 = f32[256]{0:T(256)S(1)} fusion(s32[]{:T(128)} %bitcast.18, s32[]{:T(128)} %bitcast.17, s32[]{:T(128)} %bitcast.16, s32[]{:T(128)} %bitcast.15, s32[]{:T(128)} %bitcast.14, s32[]{:T(128)} %bitcast.13, s32[]{:T(128)} %bitcast.8), kind=kLoop, calls=%fused_computation.30 | loop fusion | flops 2048 | bytes 1052 | tf_op jit(solution)/shard_map/convert_element_type | solution.py:286
  76.9 0.0 copy-done.9
  76.9 0.0 copy-done.11
  83.2 0.0 copy-done.14
  83.2 0.1 concatenate.9.info_ref
  83.3 0.0 all-to-all-done.tok_ref
  83.4 0.7 broadcast_in_dim.45
  84.1 5.1 %all-to-all-start.2 = ((bf16[8,5,16,256]{3,2,1,0:T(8,128)(2,1)}), bf16[8,5,16,256]{3,2,1,0:T(8,128)(2,1)}, u32[]{:S(2)}, u32[]{:S(2)}) async-start(bf16[8,5,16,256]{3,2,1,0:T(8,128)(2,1)} %broadcast_in_dim.45), calls=%async_computation.2 | async-start | bytes 655360 | tf_op jit(solution)/shard_map/all_to_all | solution.py:27
  89.2 0.5 fusion
  89.7 0.1 pad_maximum_fusion.cos_ref
  89.9 0.1 pad_maximum_fusion.1.sin_ref
  90.0 0.0 copy-done.1
  90.0 0.0 copy-done.3
  90.0 0.0 copy-done.5
  90.0 1.8 %projection.1 = (bf16[3,256,128]{2,1,0:T(8,128)(2,1)S(1)}, bf16[256,128]{1,0:T(8,128)(2,1)}) custom-call(s32[1]{0:T(128)} %bitcast.6.holds_ref, bf16[4,256,384]{2,1,0:T(8,128)(2,1)S(1)} %all-to-all-done.tok_ref, f32[1,1536]{1,0:T(1,128)S(1)} %broadcast_in_dim.38.gain_ref, bf16[1536,384]{1,0:T(8,128)(2,1)S(1)} %copy-done.1, bf16[1536,128]{1,0:T(8,128)(2,1)S(1)} %copy-done.3, ...), custom_call_target="tpu_custom_call" | custom-call | tf_op jit(solution)/shard_map/projection/pallas_call | solution.py:292
  91.8 3.4 %collective-permute-start = (bf16[256,128]{1,0:T(8,128)(2,1)}, bf16[256,128]{1,0:T(8,128)(2,1)S(1)}, u32[]{:S(2)}, u32[]{:S(2)}) collective-permute-start(bf16[256,128]{1,0:T(8,128)(2,1)} %get-tuple-element.7.own_ref), channel_id=1, source_target_pairs={{0,1},{1,0},{2,3},{3,2},{4,5},{5,4},{6,7},{7,6},{8,9},{9,8},{10,11... | collective-permute-start | bytes 196616 | tf_op jit(solution)/shard_map/ppermute | solution.py:313
  95.2 7.9 %all-to-all-done.2 = bf16[8,5,16,256]{3,2,1,0:T(8,128)(2,1)} async-done(((bf16[8,5,16,256]{3,2,1,0:T(8,128)(2,1)}), bf16[8,5,16,256]{3,2,1,0:T(8,128)(2,1)}, u32[]{:S(2)}, u32[]{:S(2)}) %all-to-all-start.2) | async-done | bytes 327712 | tf_op jit(solution)/shard_map/all_to_all | solution.py:27
  103.1 1.0 fusion.4
  104.2 16.6 %all-gather = bf16[80,16,256]{2,1,0:T(8,128)(2,1)S(1)} all-gather(bf16[5,16,256]{2,1,0:T(8,128)(2,1)S(1)} %constant_dynamic-update-slice_fusion.5), channel_id=2, replica_groups=mesh['z'=8,'y'=8,'core'=2,'tp'=4] {'y','core'}, dimensions={0}, use_global_device_ids=true | all-gather | bytes 696320 | tf_op jit(solution)/shard_map/all_gather | solution.py:47
  120.7 0.0 collective-permute-done.1.h0_ref
  120.7 0.0 collective-permute-done.2.h1_ref
  120.7 0.0 collective-permute-done.3.h2_ref
  120.7 0.0 collective-permute-done.4.h3_ref
  120.7 0.0 collective-permute-done.partner_ref
  120.8 0.0 copy-done.2
  120.8 0.0 copy-done.4
  120.8 4.6 %attention.1 = bf16[4,256,384]{2,1,0:T(8,128)(2,1)S(1)} custom-call(s32[22]{0:T(128)S(1)} %concatenate.9.info_ref, bf16[3,256,128]{2,1,0:T(8,128)(2,1)S(1)} %get-tuple-element.8.q_ref, bf16[256,128]{1,0:T(8,128)(2,1)S(1)} %copy-done.4, bf16[256,128]{1,0:T(8,128)(2,1)S(1)} %collective-permute-done.partner_ref, ...), custom_call_target="tpu_custom_call" | custom-call | tf_op jit(solution)/shard_map/attention/pallas_call | solution.py:317
  125.3 0.0 copy-start.8
  125.4 16.1 %all_to_all.20 = bf16[4,256,384]{2,1,0:T(8,128)(2,1)S(1)} all-to-all(bf16[4,256,384]{2,1,0:T(8,128)(2,1)S(1)} %attention.1), channel_id=1, replica_groups=mesh['z'=8,'y'=8,'core'=2,'tp'=4] {'tp'}, dimensions={0} | all-to-all | bytes 1572864 | tf_op jit(solution)/shard_map/all_to_all | solution.py:326
  141.5 0.1 convert_reduce_fusion
  141.6 0.0 copy-done.8
  141.6 0.7 add_convert_fusion
  (21 shorter events, 0.2 us)
Async XLA Ops:
  0.6 38.9 %copy-start = (bf16[256,512]{1,0:T(8,128)(2,1)S(1)}, bf16[256,512]{1,0:T(8,128)(2,1)}, u32[]{:S(2)}) copy-start(bf16[256,512]{1,0:T(8,128)(2,1)} %param.23) | copy-start | bytes 786436
  0.6 44.9 %copy-start.13 = (s32[1,4]{1,0:T(1,128)S(1)}, s32[1,4]{1,0:T(1,128)}, u32[]{:S(2)}) copy-start(s32[1,4]{1,0:T(1,128)} %param.31) | copy-start | bytes 52
  0.7 44.9 %copy-start.12 = (s32[1,4]{1,0:T(1,128)S(1)}, s32[1,4]{1,0:T(1,128)}, u32[]{:S(2)}) copy-start(s32[1,4]{1,0:T(1,128)} %param.29) | copy-start | bytes 52
  0.7 45.1 %copy-start.6 = (s32[5]{0:T(128)S(1)}, s32[5]{0:T(128)}, u32[]{:S(2)}) copy-start(s32[5]{0:T(128)} %param.24) | copy-start | bytes 64
  0.7 45.7 %copy-start.10 = (s32[1,4]{1,0:T(1,128)S(1)}, s32[1,4]{1,0:T(1,128)}, u32[]{:S(2)}) copy-start(s32[1,4]{1,0:T(1,128)} %param.28) | copy-start | bytes 52
  0.7 45.7 %copy-start.15 = (s32[5]{0:T(128)S(1)}, s32[5]{0:T(128)}, u32[]{:S(2)}) copy-start(s32[5]{0:T(128)} %param.25) | copy-start | bytes 64
  0.7 54.0 %copy-start.7 = (bf16[256,384]{1,0:T(8,128)(2,1)S(1)}, bf16[256,384]{1,0:T(8,128)(2,1)}, u32[]{:S(2)}) copy-start(bf16[256,384]{1,0:T(8,128)(2,1)} %param.16) | copy-start | bytes 589828
  18.7 102.1 %collective-permute-start.1 = (bf16[256,256]{1,0:T(8,128)(2,1)}, bf16[256,256]{1,0:T(8,128)(2,1)S(1)}, u32[]{:S(2)}, u32[]{:S(2)}) collective-permute-start(bf16[256,256]{1,0:T(8,128)(2,1)} %get-tuple-element.10), channel_id=1, source_target_pairs={{504,0},{508,4},{0,8},{4,12},{8,16},{12,20},{16,24},{20,28},{24,32... | collective-permute-start | bytes 393224 | tf_op jit(solution)/shard_map/ppermute | solution.py:22
  22.7 98.0 %collective-permute-start.2 = (bf16[256,256]{1,0:T(8,128)(2,1)}, bf16[256,256]{1,0:T(8,128)(2,1)S(1)}, u32[]{:S(2)}, u32[]{:S(2)}) collective-permute-start(bf16[256,256]{1,0:T(8,128)(2,1)} %get-tuple-element.11), channel_id=1, source_target_pairs={{508,0},{0,4},{4,8},{8,12},{12,16},{16,20},{20,24},{24,28},{28,32}... | collective-permute-start | bytes 393224 | tf_op jit(solution)/shard_map/ppermute | solution.py:22
  26.8 94.0 %collective-permute-start.3 = (bf16[256,256]{1,0:T(8,128)(2,1)}, bf16[256,256]{1,0:T(8,128)(2,1)S(1)}, u32[]{:S(2)}, u32[]{:S(2)}) collective-permute-start(bf16[256,256]{1,0:T(8,128)(2,1)} %get-tuple-element.12), channel_id=1, source_target_pairs={{4,0},{8,4},{12,8},{16,12},{20,16},{24,20},{28,24},{32,28},{36,32}... | collective-permute-start | bytes 393224 | tf_op jit(solution)/shard_map/ppermute | solution.py:22
  31.3 89.4 %collective-permute-start.4 = (bf16[256,256]{1,0:T(8,128)(2,1)}, bf16[256,256]{1,0:T(8,128)(2,1)S(1)}, u32[]{:S(2)}, u32[]{:S(2)}) collective-permute-start(bf16[256,256]{1,0:T(8,128)(2,1)} %get-tuple-element.13), channel_id=1, source_target_pairs={{8,0},{12,4},{16,8},{20,12},{24,16},{28,20},{32,24},{36,28},{40,32... | collective-permute-start | bytes 393224 | tf_op jit(solution)/shard_map/ppermute | solution.py:22
  40.2 14.5 %all-to-all-start.1 = ((bf16[16,16,256]{2,1,0:T(8,128)(2,1)}), bf16[16,16,256]{2,1,0:T(8,128)(2,1)S(1)}, u32[]{:S(2)}, u32[]{:S(2)}) async-start(bf16[16,16,256]{2,1,0:T(8,128)(2,1)} %bitcast.21), calls=%async_computation.1 | async-start | bytes 262144 | tf_op jit(solution)/shard_map/all_to_all | solution.py:36
  47.8 29.0 %copy-start.9 = (f32[1536]{0:T(1024)S(1)}, f32[1536]{0:T(1024)}, u32[]{:S(2)}) copy-start(f32[1536]{0:T(1024)} %param.17) | copy-start | bytes 18436
  47.8 29.1 %copy-start.11 = (f32[384]{0:T(512)S(1)}, f32[384]{0:T(512)}, u32[]{:S(2)}) copy-start(f32[384]{0:T(512)} %param.19) | copy-start | bytes 4612
  47.8 35.4 %copy-start.14 = (s32[1,4]{1,0:T(1,128)S(1)}, s32[1,4]{1,0:T(1,128)}, u32[]{:S(2)}) copy-start(s32[1,4]{1,0:T(1,128)} %param.30) | copy-start | bytes 52
  55.7 27.7 %all-to-all-start = ((bf16[4,256,384]{2,1,0:T(8,128)(2,1)}), bf16[4,256,384]{2,1,0:T(8,128)(2,1)S(1)}, u32[]{:S(2)}, u32[]{:S(2)}) async-start(bf16[4,256,384]{2,1,0:T(8,128)(2,1)} %broadcast_in_dim.37), calls=%async_computation | async-start | bytes 1572864 | tf_op jit(solution)/shard_map/all_to_all | solution.py:27
  59.7 30.3 %copy-start.1 = (bf16[1536,384]{1,0:T(8,128)(2,1)S(1)}, bf16[1536,384]{1,0:T(8,128)(2,1)}, u32[]{:S(2)}) copy-start(bf16[1536,384]{1,0:T(8,128)(2,1)} %wq_ref.1) | copy-start | bytes 3538948
  59.7 30.3 %copy-start.3 = (bf16[1536,128]{1,0:T(8,128)(2,1)S(1)}, bf16[1536,128]{1,0:T(8,128)(2,1)}, u32[]{:S(2)}) copy-start(bf16[1536,128]{1,0:T(8,128)(2,1)} %wkv_ref.1) | copy-start | bytes 1179652
  59.7 30.3 %copy-start.5 = (f32[128]{0:T(128)S(1)}, f32[128]{0:T(128)}, u32[]{:S(2)}) copy-start(f32[128]{0:T(128)} %param.21) | copy-start | bytes 1540
  84.1 19.0 %all-to-all-start.2 = ((bf16[8,5,16,256]{3,2,1,0:T(8,128)(2,1)}), bf16[8,5,16,256]{3,2,1,0:T(8,128)(2,1)}, u32[]{:S(2)}, u32[]{:S(2)}) async-start(bf16[8,5,16,256]{3,2,1,0:T(8,128)(2,1)} %broadcast_in_dim.45), calls=%async_computation.2 | async-start | bytes 655360 | tf_op jit(solution)/shard_map/all_to_all | solution.py:27
  91.8 29.0 %copy-start.2 = (bf16[384,1536]{1,0:T(8,128)(2,1)S(1)}, bf16[384,1536]{1,0:T(8,128)(2,1)}, u32[]{:S(2)}) copy-start(bf16[384,1536]{1,0:T(8,128)(2,1)} %wo_ref.1) | copy-start | bytes 3538948
  91.8 29.0 %copy-start.4 = (bf16[256,128]{1,0:T(8,128)(2,1)S(1)}, bf16[256,128]{1,0:T(8,128)(2,1)}, u32[]{:S(2)}) copy-start(bf16[256,128]{1,0:T(8,128)(2,1)} %get-tuple-element.7.own_ref) | copy-start | bytes 196612
  91.8 29.0 %collective-permute-start = (bf16[256,128]{1,0:T(8,128)(2,1)}, bf16[256,128]{1,0:T(8,128)(2,1)S(1)}, u32[]{:S(2)}, u32[]{:S(2)}) collective-permute-start(bf16[256,128]{1,0:T(8,128)(2,1)} %get-tuple-element.7.own_ref), channel_id=1, source_target_pairs={{0,1},{1,0},{2,3},{3,2},{4,5},{5,4},{6,7},{7,6},{8,9},{9,8},{10,11... | collective-permute-start | bytes 196616 | tf_op jit(solution)/shard_map/ppermute | solution.py:313
  125.3 16.2 %copy-start.8 = (bf16[256,384]{1,0:T(8,128)(2,1)S(1)}, bf16[256,384]{1,0:T(8,128)(2,1)}, u32[]{:S(2)}) copy-start(bf16[256,384]{1,0:T(8,128)(2,1)} %param.16) | copy-start | bytes 589828

commit v3 on v2

v3 whole, which is shorter than its diff:
```python
import math

import jax
import jax.numpy as jnp
from jax import lax
from jax.experimental import pallas as pl
from jax.experimental.pallas import tpu as pltpu
from jax.sharding import Mesh, PartitionSpec as P

norm_eps = 1e-06
rope_base = 1000000.0
neighbour_steps = (-2, -1, 1, 2)
seq_axes = ("z", "y", "core")
barred = -(2.0**100)
f32 = jnp.float32
bf16 = jnp.bfloat16
int32 = jnp.int32


def passed_along(block, axis, distance):
    devices = range(math.prod(lax.axis_size(name) for name in axis))
    return lax.ppermute(block, axis, [((i - distance) % len(devices), i) for i in devices])


def scalars_from(info_ref, requests):
    names = ("length", "depth", "slot", "parent")
    table = {
        name: [info_ref[n * requests + r] for r in range(requests)] for n, name in enumerate(names)
    }
    starts = [jnp.int32(0)]
    for r in range(requests - 1):
        starts.append(starts[r] + table["length"][r])
    table["start"] = starts
    return table


def by_request(index, starts, values):
    picked = jnp.full(index.shape, values[0], int32)
    for r in range(1, len(starts)):
        picked = jnp.where(index >= starts[r], values[r], picked)
    return picked


def prepare_kernel(
    info_ref, page_ref, place_ref, pool_ref, pos_ref, *rest
):
    outs, sems = rest[:-1], rest[-1]
    page_rows = pool_ref.shape[1]
    width = outs[0].shape[1]
    per_slot = outs[0].shape[0] // page_rows
    first = pl.multiple_of(place_ref[0] // 2 * width, width)
    copies = []
    for slot, out in enumerate(outs):
        for c in range(per_slot):
            n = slot * per_slot + c
            copies.append(
                pltpu.make_async_copy(
                    pool_ref.at[page_ref[n], :, pl.ds(first, width)],
                    out.at[pl.ds(c * page_rows, page_rows), :],
                    sems.at[n],
                )
            )
    for copy in copies:
        copy.start()
    requests = len(outs)
    table = scalars_from(info_ref, requests)
    base = []
    for r in range(requests):
        above = info_ref[4 * requests + 1 + table["parent"][r]]
        base.append(info_ref[4 * requests] + above + table["depth"][r] - table["start"][r])
    row = lax.broadcasted_iota(int32, pos_ref.shape, 0)
    pos_ref[...] = (row + by_request(row, table["start"], base)).astype(f32)
    for copy in copies:
        copy.wait()


def prepared(info, pages, place, hist_pool, row_count, slots, width):
    rows = pages.shape[0] // slots * hist_pool.shape[1]
    scalars = pl.BlockSpec(memory_space=pltpu.SMEM)
    anywhere = pl.BlockSpec(memory_space=pl.ANY)
    return pl.pallas_call(
        prepare_kernel,
        out_shape=[jax.ShapeDtypeStruct((row_count, width // 2), f32)]
        + [jax.ShapeDtypeStruct((rows, width), bf16)] * slots,
        in_specs=[scalars] * 3 + [anywhere],
        out_specs=whole(1 + slots),
        scratch_shapes=[pltpu.SemaphoreType.DMA((pages.shape[0],))],
        name="prepare",
    )(info, pages, place, hist_pool)


def first_pick_kernel(owner_ref, arrived_ref, out_ref):
    per_plane = arrived_ref.shape[0]
    for n in range(out_ref.shape[1]):
        chosen = arrived_ref[lax.rem(owner_ref[n], per_plane)]
        for z in range(out_ref.shape[0]):
            out_ref[z, n] = chosen


def first_pick(owner, arrived, planes):
    return pl.pallas_call(
        first_pick_kernel,
        out_shape=jax.ShapeDtypeStruct((planes, owner.shape[0]) + arrived.shape[1:], bf16),
        in_specs=[pl.BlockSpec(memory_space=pltpu.SMEM)] + whole(1),
        out_specs=whole(1)[0],
        name="first_pick",
    )(owner, arrived)


def second_pick(owner, planes, per_plane, copies):
    def kernel(owner_ref, planes_ref, out_ref):
        for n in range(out_ref.shape[1]):
            chosen = planes_ref[lax.div(owner_ref[n], per_plane), n]
            for c in range(copies):
                out_ref[c, n] = chosen

    return pl.pallas_call(
        kernel,
        out_shape=jax.ShapeDtypeStruct((copies,) + planes.shape[1:], bf16),
        in_specs=[pl.BlockSpec(memory_space=pltpu.SMEM)] + whole(1),
        out_specs=whole(1)[0],
        name="second_pick",
    )(owner, planes)


def projection_kernel(
    place_ref, tok_ref, gain_ref, wq_ref, wkv_ref, qb_ref, kb_ref, cos_ref, sin_ref, q_ref, own_ref
):
    groups, rows, width = tok_ref.shape
    total = jnp.zeros((rows, 1), f32)
    for g in range(groups):
        block = tok_ref[g].astype(f32)
        total = total + jnp.sum(block * block, axis=1, keepdims=True)
    inverse = lax.rsqrt(total / (groups * width) + norm_eps)
    query = jnp.zeros((rows, wq_ref.shape[1]), f32)
    fresh = jnp.zeros((rows, wkv_ref.shape[1]), f32)
    for g in range(groups):
        span = pl.ds(g * width, width)
        normed = (tok_ref[g].astype(f32) * inverse * gain_ref[:, span]).astype(bf16)
        query = query + jnp.dot(normed, wq_ref[span, :], preferred_element_type=f32)
        fresh = fresh + jnp.dot(normed, wkv_ref[span, :], preferred_element_type=f32)
    cosine = cos_ref[...]
    sine = sin_ref[...]
    half = cosine.shape[1] // 2

    def turned(part):
        return part * cosine + pltpu.roll(part, half, 1) * sine

    query = query + qb_ref[...]
    dim = cosine.shape[1]
    for h in range(q_ref.shape[0]):
        q_ref[h] = turned(query[:, h * dim : (h + 1) * dim]).astype(bf16)
    fresh = fresh + kb_ref[...]

    @pl.when(place_ref[0] % 2 == 0)
    def _():
        own_ref[...] = turned(fresh).astype(bf16)

    @pl.when(place_ref[0] % 2 == 1)
    def _():
        own_ref[...] = fresh.astype(bf16)


def bars(bad):
    return jnp.where(bad, barred, 0.0).astype(bf16)


across = (((1,), (1,)), ((), ()))


def scale_of(dim):
    return dim ** (-0.5) * math.log2(math.e)


def local_kernel(
    info_ref, place_ref, q_ref, own_ref, partner_ref, h0_ref, h1_ref, h2_ref, h3_ref,
    mixed_ref, top_ref, marks_ref, bars_ref, key_ref, value_ref,
):
    heads, rows, dim = q_ref.shape
    hist_refs = (h0_ref, h1_ref, h2_ref, h3_ref)
    requests = len(hist_refs)
    table = scalars_from(info_ref, requests)
    starts, hist_len, slot, parent = (table[n] for n in ("start", "depth", "slot", "parent"))
    nodes = info_ref.shape[0] - 4 * requests
    shared_len = [info_ref[4 * requests + n] for n in range(nodes)]

    @pl.when(place_ref[0] % 2 == 0)
    def _():
        key_ref[...] = own_ref[...]
        value_ref[...] = partner_ref[...]

    @pl.when(place_ref[0] % 2 == 1)
    def _():
        key_ref[...] = partner_ref[...]
        value_ref[...] = own_ref[...]

    row = lax.broadcasted_iota(int32, (rows, dim), 0)
    lane = lax.broadcasted_iota(int32, (rows, dim), 1)
    hit = (
        (lane == by_request(row, starts, slot))
        | (lane == requests + by_request(row, starts, parent))
        | (lane == 2 * requests)
    )
    marks = jnp.where(hit, 1.0, 0.0).astype(bf16)
    marks_ref[...] = marks

    chunks, per_chunk, _ = bars_ref.shape
    chunk = per_chunk // nodes
    index = lax.broadcasted_iota(int32, (per_chunk, dim), 0)
    side = lax.broadcasted_iota(int32, (per_chunk, dim), 1)
    node = jnp.zeros(index.shape, int32)
    left = jnp.full(index.shape, shared_len[0], int32)
    for n in range(1, nodes):
        node = jnp.where(index >= n * chunk, n, node)
        left = jnp.where(index >= n * chunk, shared_len[n], left)
    left = left - (index - node * chunk)
    other = (side >= requests) & (side < 2 * requests) & (node > 0) & (side != requests + node - 1)
    last = side == 2 * requests
    for s in range(chunks):
        bars_ref[s] = bars(other | (last & (left <= s * chunk)))

    keys = []
    values = []
    for j in range(requests):
        deep = jnp.int32(0)
        for r in range(requests):
            deep = deep + jnp.where(slot[r] == j, hist_len[r], 0)
        place = lax.broadcasted_iota(int32, (hist_refs[j].shape[0], dim), 0)
        side = lax.broadcasted_iota(int32, (hist_refs[j].shape[0], dim), 1)
        bad = ((side < requests) & (side != j)) | ((side == 2 * requests) & (place >= deep))
        keys.append(jnp.concatenate([hist_refs[j][:, :dim], bars(bad)], axis=1))
        values.append(hist_refs[j][:, dim:])
    far_keys = jnp.concatenate(keys, axis=0)
    far_values = jnp.concatenate(values, axis=0)
    far_values = jnp.concatenate([far_values, jnp.ones_like(far_values)], axis=1)
    own_keys = key_ref[...]
    own_values = value_ref[...]
    own_values = jnp.concatenate([own_values, jnp.ones_like(own_values)], axis=1)

    wide_row = lax.broadcasted_iota(int32, (rows, rows), 0)
    wide_col = lax.broadcasted_iota(int32, (rows, rows), 1)
    numbers = list(range(requests))
    same = by_request(wide_row, starts, numbers) == by_request(wide_col, starts, numbers)
    unseen = jnp.where((wide_col <= wide_row) & same, 0.0, barred)

    scale = scale_of(dim)
    for h in range(heads):
        query = q_ref[h]
        far = lax.dot_general(
            jnp.concatenate([query, marks], axis=1), far_keys, across, preferred_element_type=f32
        )
        own = lax.dot_general(query, own_keys, across, preferred_element_type=f32) + unseen
        top = jnp.maximum(
            jnp.max(far, axis=1, keepdims=True), jnp.max(own, axis=1, keepdims=True)
        )
        far_weights = jnp.exp2((far - top) * scale).astype(bf16)
        own_weights = jnp.exp2((own - top) * scale).astype(bf16)
        mixed_ref[h] = jnp.dot(far_weights, far_values, preferred_element_type=f32) + jnp.dot(
            own_weights, own_values, preferred_element_type=f32
        )
        top_ref[h] = jnp.broadcast_to(top, (rows, dim))


def shared_kernel(q_ref, mixed_ref, top_ref, marks_ref, bars_ref, hot_ref, wo_ref, out_ref):
    heads, rows, dim = q_ref.shape
    chunks, nodes, chunk, _ = hot_ref.shape
    hot = hot_ref[...].reshape(chunks * nodes * chunk, 2 * dim)
    keys = jnp.concatenate([hot[:, :dim], bars_ref[...].reshape(-1, dim)], axis=1)
    values = hot[:, dim:]
    values = jnp.concatenate([values, jnp.ones_like(values)], axis=1)
    marks = marks_ref[...]
    scale = scale_of(dim)
    merged = []
    for h in range(heads):
        scores = lax.dot_general(
            jnp.concatenate([q_ref[h], marks], axis=1), keys, across, preferred_element_type=f32
        )
        top = jnp.maximum(jnp.max(scores, axis=1, keepdims=True), top_ref[h][:, :1])
        weights = jnp.exp2((scores - top) * scale).astype(bf16)
        kept = jnp.exp2((top_ref[h] - top) * scale)
        local = mixed_ref[h]
        mixed = jnp.dot(weights, values, preferred_element_type=f32)
        total = mixed[:, dim:] + local[:, dim:] * kept
        merged.append(((mixed[:, :dim] + local[:, :dim] * kept) / total).astype(bf16))
    attention = jnp.concatenate(merged, axis=1)
    width = out_ref.shape[2]
    for g in range(out_ref.shape[0]):
        out_ref[g] = jnp.dot(
            attention, wo_ref[:, g * width : (g + 1) * width], preferred_element_type=f32
        ).astype(bf16)


def whole(count):
    return [pl.BlockSpec(memory_space=pltpu.VMEM)] * count


def on_device(
    tokens,
    norm_gain,
    query_weight,
    query_bias,
    kv_weight,
    kv_bias,
    out_weight,
    shared_slot,
    shared_len,
    shared_owner,
    hist_pool,
    hist_pages,
    hist_len,
    req_len,
    req_offset,
    req_parent,
):
    group_count = lax.axis_size("tp")
    row_count, width = tokens.shape
    head_dim = kv_bias.shape[0]
    head_count = query_weight.shape[1] // head_dim
    request_count = req_len.shape[1]
    tp_index = lax.axis_index("tp")
    place = jnp.stack([tp_index, lax.axis_index("core")]).astype(int32)
    scalars = pl.BlockSpec(memory_space=pltpu.SMEM)

    copies = jnp.broadcast_to(tokens[None], (group_count,) + tokens.shape)
    features = lax.all_to_all(copies, "tp", 0, 0, tiled=True)
    info = jnp.concatenate([req_len[0], hist_len[0], req_offset[0], req_parent[0], shared_len])
    position, *slots = prepared(
        info, hist_pages[0], place, hist_pool, row_count, request_count, 2 * head_dim
    )
    z_count, y_count, core_count = (lax.axis_size(name) for name in seq_axes)
    plane_count = y_count * core_count
    chunk = shared_slot.shape[0] // plane_count
    node_total = shared_owner.shape[0]

    def history(j):
        return passed_along(slots[j], seq_axes, -neighbour_steps[j])

    def after(value, *others):
        return lax.optimization_barrier((value, *others))[0]

    histories = []
    pieces = lax.dynamic_slice_in_dim(shared_slot, tp_index // 2 * 2 * head_dim, 2 * head_dim, 1)
    pieces = after(pieces, features, slots[3])
    arrived = lax.all_to_all(
        pieces.reshape(plane_count, chunk, -1), seq_axes[1:], 0, 0, tiled=True
    )

    half = head_dim // 2
    frequency = rope_base ** (-2.0 * jnp.arange(half, dtype=f32) / head_dim)
    angle = position[:, :half] * frequency[None, :]
    cosine = jnp.cos(angle)
    sine = jnp.sin(angle)
    cosine = jnp.concatenate([cosine, cosine], axis=1)
    sine = jnp.concatenate([-sine, sine], axis=1)
    queries, own_block = pl.pallas_call(
        projection_kernel,
        out_shape=[
            jax.ShapeDtypeStruct((head_count, row_count, head_dim), bf16),
            jax.ShapeDtypeStruct((row_count, head_dim), bf16),
        ],
        in_specs=[scalars] + whole(8),
        out_specs=whole(2),
        compiler_params=pltpu.CompilerParams(vmem_limit_bytes=32 * 2**20),
        name="projection",
    )(
        place,
        features,
        norm_gain[None, :],
        query_weight,
        kv_weight,
        query_bias[None, :],
        kv_bias[None, :],
        cosine,
        sine,
    )
    partner = lax.ppermute(own_block, "tp", [(i, i ^ 1) for i in range(group_count)])
    slots[1] = after(slots[1], pieces)
    histories += [history(0), history(1)]
    chosen = first_pick(shared_owner, after(arrived, own_block, *histories), z_count)
    planes = lax.all_to_all(chosen, "z", 0, 0, tiled=True)
    slots[2] = after(slots[2], chosen)
    slots[3] = after(slots[3], chosen)
    histories += [history(2), history(3)]
    local = pl.pallas_call(
        local_kernel,
        out_shape=[
            jax.ShapeDtypeStruct((head_count, row_count, 2 * head_dim), f32),
            jax.ShapeDtypeStruct((head_count, row_count, head_dim), f32),
            jax.ShapeDtypeStruct((row_count, head_dim), bf16),
            jax.ShapeDtypeStruct((plane_count, node_total * chunk, head_dim), bf16),
        ],
        in_specs=[scalars] * 2 + whole(7),
        out_specs=whole(4),
        scratch_shapes=[pltpu.VMEM((row_count, head_dim), bf16)] * 2,
        compiler_params=pltpu.CompilerParams(vmem_limit_bytes=40 * 2**20),
        name="local",
    )(info, place, queries, own_block, partner, *histories)
    kept = second_pick(shared_owner, after(planes, *local), plane_count, 1)[0]
    hot = lax.all_gather(kept, seq_axes[1:], axis=0, tiled=False)
    blocks = pl.pallas_call(
        shared_kernel,
        out_shape=jax.ShapeDtypeStruct((group_count, row_count, width), bf16),
        in_specs=whole(7),
        out_specs=whole(1)[0],
        compiler_params=pltpu.CompilerParams(vmem_limit_bytes=40 * 2**20),
        name="shared",
    )(queries, *local, hot, out_weight)
    summed = jnp.sum(lax.all_to_all(blocks, "tp", 0, 0, tiled=True).astype(f32), axis=0)
    hidden = (summed + tokens.astype(f32)).astype(bf16)
    return (hidden, own_block)


def solution(mesh):
    devices = mesh.devices
    split = Mesh(devices.reshape(8, devices.shape[0] // 16, 2, devices.shape[1]), seq_axes + ("tp",))
    by_seq = P(seq_axes, None)
    return jax.shard_map(
        on_device,
        mesh=split,
        in_specs=(
            P(seq_axes, "tp"),
            P(),
            P(None, "tp"),
            P("tp"),
            P(None, "tp"),
            P("tp"),
            P("tp", None),
            by_seq,
            P(),
            P(),
            P(seq_axes, None, None),
            by_seq,
            by_seq,
            by_seq,
            by_seq,
            by_seq,
        ),
        out_specs=(P(seq_axes, "tp"), P(seq_axes, "tp")),
        check_vma=False,
    )
```

time: 143 us -> 105 us (0.73)
  between operations: 19.9 us -> 0.97 us
  Pallas kernels: 24.3 us -> 13.5 us
  waiting for transfers between devices: 14.8 us -> 5.34 us
  starting transfers between devices: 38.6 us -> 43.5 us
  other arithmetic: 6.36 us -> 2.97 us
    all_to_all x3, waiting for transfers between devices: 14.8 us -> 1.93 us  [the longest x1 1.66 us: on_device(): lax.all_to_all(pieces.reshape(plane_count, chunk, -1), seq_axes[1:], 0, 0...]
    all_to_all x3, starting transfers between devices: 14.4 us -> 27 us  [the longest x1 12 us: on_device(): lax.all_to_all(pieces.reshape(plane_count, chunk, -1), seq_axes[1:], 0, 0...]
    pallas_call x2 -> x5, Pallas kernels: 22.5 us -> 11.2 us  [the longest x1 2.81 us: prepared(): pl.pallas_call(prepare_kernel, out_shape=[jax.ShapeDtypeStruct((row_count...]
    ppermute x4, starting transfers between devices: 20.8 us -> 14.3 us  [passed_along(): lax.ppermute(block, axis, [((i - distance) % len(devices), i) for i in de...]
    convert_element_type x1 -> x0, other arithmetic: 4.56 us -> none  [on_device(): angle = (row + shift).astype(f32) * frequency[None, :]]
    ppermute x1, waiting for transfers between devices: 0.01 us -> 3.4 us  [on_device(): lax.ppermute(own_block, 'tp', [(i, i ^ 1) for i in range(group_count)])]
    slice x3 -> x0, local copies, waits for them, and re-layouts: 2.36 us -> none  [the longest x1 0.99 us: gathered_nodes(): planes[:, n]]
    all_to_all x1, blocking collectives: 16.1 us -> 14.5 us  [on_device(): lax.all_to_all(blocks, 'tp', 0, 0, tiled=True).astype(f32)]
  transfers between devices with their start and end apart: 8 -> 8, of which waited for: 2 -> 3; matrix products, arithmetic and copies ran while one was open for 8% -> 3% of each run, Pallas kernels for 1% -> 7%
where the time goes in v3:
time: 105 us; the launch traced here: 104 us
  starting transfers between devices  43.5 us (41%)
  blocking collectives  32.7 us (31%)
  Pallas kernels  13.5 us (13%)
  waiting for transfers between devices  5.34 us (5%)
  local copies, waits for them, and re-layouts  4.86 us (5%)
  other arithmetic  2.97 us (3%)
    all_gather x1, blocking collectives, on_device(): hot = lax.all_gather(kept, seq_axes[1:], axis=0, tiled=False)  18.1 us
    all_to_all x1, blocking collectives, on_device(): lax.all_to_all(blocks, 'tp', 0, 0, tiled=True).astype(f32)  14.5 us
    ppermute x4, starting transfers between devices, passed_along(): lax.ppermute(block, axis, [((i - distance) % len(devices), i) for i in de...  14.3 us
    all_to_all x1, starting transfers between devices, on_device(): lax.all_to_all(pieces.reshape(plane_count, chunk, -1), seq_axes[1:], 0, 0...  12 us
    all_to_all x1, starting transfers between devices, on_device(): planes = lax.all_to_all(chosen, 'z', 0, 0, tiled=True)  10.2 us
    all_to_all x1, starting transfers between devices, on_device(): features = lax.all_to_all(copies, 'tp', 0, 0, tiled=True)  4.84 us
    ppermute x1, waiting for transfers between devices, on_device(): lax.ppermute(own_block, 'tp', [(i, i ^ 1) for i in range(group_count)])  3.4 us
    pallas_call x1, Pallas kernels, prepared(): pl.pallas_call(prepare_kernel, out_shape=[jax.ShapeDtypeStruct((row_count...  2.81 us
  transfers between devices with their start and end apart: 8, of which 3 were waited for; matrix products, arithmetic and copies ran while one was open for 3% of the time, Pallas kernels for 7%

profile of v3, /device:TPU:1, one launch (start us, length us, event | category | flops | bytes accessed | tf_op | source)
XLA Modules:
  0.0 103.8 jit_solution(16725776201305875855)
XLA Ops:
  0.6 0.0 copy-start
  0.6 0.0 copy-start.15
  0.7 0.0 copy-start.14
  0.7 0.0 copy-start.12
  0.7 0.0 copy-start.13
  0.7 0.0 copy-start.16
  0.7 2.0 %broadcast_in_dim.16 = bf16[4,256,384]{2,1,0:T(8,128)(2,1)} broadcast(bf16[256,384]{1,0:T(8,128)(2,1)} %param.16), dimensions={1,2} | broadcast | bytes 983040 | tf_op jit(solution)/shard_map/broadcast_in_dim | solution.py:324
  2.7 4.8 %all-to-all-start = ((bf16[4,256,384]{2,1,0:T(8,128)(2,1)}), bf16[4,256,384]{2,1,0:T(8,128)(2,1)S(1)}, u32[]{:S(2)}, u32[]{:S(2)}) async-start(bf16[4,256,384]{2,1,0:T(8,128)(2,1)} %broadcast_in_dim.16), calls=%async_computation | async-start | bytes 1572864 | tf_op jit(solution)/shard_map/all_to_all | solution.py:325
  7.5 0.0 copy-start.11
  7.5 0.0 copy-start.10
  7.5 0.0 copy-done.15
  7.5 0.0 copy-done.14
  7.5 0.0 copy-done.12
  7.5 0.0 copy-done.13
  7.5 0.0 copy-done.16
  7.6 0.7 concatenate.9.info_ref
  8.2 0.6 pad_add_fusion.place_ref
  8.8 2.8 %prepare.1 = (f32[256,128]{1,0:T(8,128)}, bf16[256,256]{1,0:T(8,128)(2,1)}, bf16[256,256]{1,0:T(8,128)(2,1)}, bf16[256,256]{1,0:T(8,128)(2,1)}, bf16[256,256]{1,0:T(8,128)(2,1)}) custom-call(s32[21]{0:T(128)} %concatenate.9.info_ref, s32[16]{0:T(128)} %bitcast.10, s32[2]{0:T(128)} %pad_add_fusion.place_ref, bf16[16,64,512]{2,1,0:T(8,128)(2,1)} %pool_ref.1), custom_call_target="tpu_custom_call" | custom-call | tf_op jit(solution)/shard_map/prepare/pallas_call | solution.py:81
  11.7 3.2 %collective-permute-start.1 = (bf16[256,256]{1,0:T(8,128)(2,1)}, bf16[256,256]{1,0:T(8,128)(2,1)S(1)}, u32[]{:S(2)}, u32[]{:S(2)}) collective-permute-start(bf16[256,256]{1,0:T(8,128)(2,1)} %get-tuple-element.22), channel_id=1, source_target_pairs={{504,0},{508,4},{0,8},{4,12},{8,16},{12,20},{16,24},{20,28},{24,32... | collective-permute-start | bytes 393224 | tf_op jit(solution)/shard_map/ppermute | solution.py:22
  14.9 0.0 copy-done
  14.9 0.7 constant_dynamic-slice_fusion
  15.6 0.3 all-to-all-done.tok_ref
  15.8 12.0 %all-to-all-start.1 = ((bf16[16,16,256]{2,1,0:T(8,128)(2,1)}), bf16[16,16,256]{2,1,0:T(8,128)(2,1)S(1)}, u32[]{:S(2)}, u32[]{:S(2)}) async-start(bf16[16,16,256]{2,1,0:T(8,128)(2,1)} %bitcast.8), calls=%async_computation.1 | async-start | bytes 262144 | tf_op jit(solution)/shard_map/all_to_all | solution.py:344
  27.9 3.5 %collective-permute-start.2 = (bf16[256,256]{1,0:T(8,128)(2,1)}, bf16[256,256]{1,0:T(8,128)(2,1)S(1)}, u32[]{:S(2)}, u32[]{:S(2)}) collective-permute-start(bf16[256,256]{1,0:T(8,128)(2,1)} %get-tuple-element.26), channel_id=1, source_target_pairs={{508,0},{0,4},{4,8},{8,12},{12,16},{16,20},{20,24},{24,28},{28,32}... | collective-permute-start | bytes 393224 | tf_op jit(solution)/shard_map/ppermute | solution.py:22
  31.4 1.4 %fusion.2 = (f32[256,64]{1,0:T(8,128)S(1)}, f32[256,64]{1,0:T(8,128)S(1)}, f32[256,64]{1,0:T(8,128)S(1)}) fusion(f32[64]{0:T(128)S(1)} %multiply_power_fusion, f32[256,128]{1,0:T(8,128)} %get-tuple-element.19), kind=kLoop, calls=%fused_computation.10 | loop fusion | flops 32768 | bytes 262400 | tf_op jit(solution)/shard_map/neg | solution.py:354
  32.8 0.0 copy-done.11
  32.8 0.0 copy-done.10
  32.8 0.1 pad_maximum_fusion
  33.0 0.0 copy-done.1
  33.0 0.0 copy-done.3
  33.0 0.0 copy-done.6
  33.0 0.0 copy-done.7
  33.0 0.0 copy-start.18
  33.0 0.0 copy-start.17
  33.0 0.0 copy-start.5
  33.0 2.3 %projection.1 = (bf16[3,256,128]{2,1,0:T(8,128)(2,1)S(1)}, bf16[256,128]{1,0:T(8,128)(2,1)}) custom-call(s32[2]{0:T(128)S(1)} %copy-done.6, bf16[4,256,384]{2,1,0:T(8,128)(2,1)S(1)} %all-to-all-done.tok_ref, f32[1,1536]{1,0:T(1,128)S(1)} %broadcast_in_dim.17.gain_ref, bf16[1536,384]{1,0:T(8,128)(2,1)S(1)} %copy-done.1, bf16[1536,128]{1,0:T(8,128)(2,1)S(1)} %copy-done.3, ...), custom_call_target="tpu_custom_call" | custom-call | tf_op jit(solution)/shard_map/projection/pallas_call | solution.py:355
  35.4 0.0 collective-permute-done.1.h0_ref
  35.4 0.0 collective-permute-done.2.h1_ref
  35.4 1.7 %all-to-all-done.1.arrived_ref = bf16[16,16,256]{2,1,0:T(8,128)(2,1)S(1)} async-done(((bf16[16,16,256]{2,1,0:T(8,128)(2,1)}), bf16[16,16,256]{2,1,0:T(8,128)(2,1)S(1)}, u32[]{:S(2)}, u32[]{:S(2)}) %all-to-all-start.1) | async-done | bytes 131104 | tf_op jit(solution)/shard_map/all_to_all | solution.py:344
  37.0 0.7 copy-done.9
  37.7 1.7 %first_pick.1 = bf16[8,5,16,256]{3,2,1,0:T(8,128)(2,1)} custom-call(s32[5]{0:T(128)} %owner_ref.3, bf16[16,16,256]{2,1,0:T(8,128)(2,1)} %copy-done.9), custom_call_target="tpu_custom_call" | custom-call | tf_op jit(solution)/shard_map/first_pick/pallas_call | solution.py:101
  39.4 10.2 %all-to-all-start.2 = ((bf16[8,5,16,256]{3,2,1,0:T(8,128)(2,1)}), bf16[8,5,16,256]{3,2,1,0:T(8,128)(2,1)}, u32[]{:S(2)}, u32[]{:S(2)}) async-start(bf16[8,5,16,256]{3,2,1,0:T(8,128)(2,1)} %first_pick.1), calls=%async_computation.2 | async-start | bytes 655360 | tf_op jit(solution)/shard_map/all_to_all | solution.py:380
  49.5 0.0 copy-done.18
  49.5 3.8 %collective-permute-start.3 = (bf16[256,256]{1,0:T(8,128)(2,1)S(1)}, bf16[256,256]{1,0:T(8,128)(2,1)S(1)}, u32[]{:S(2)}, u32[]{:S(2)}) collective-permute-start(bf16[256,256]{1,0:T(8,128)(2,1)S(1)} %copy-done.18), channel_id=1, source_target_pairs={{4,0},{8,4},{12,8},{16,12},{20,16},{24,20},{28,24},{32,28},{36,32}... | collective-permute-start | bytes 393224 | tf_op jit(solution)/shard_map/ppermute | solution.py:22
  53.3 0.0 copy-done.17
  53.3 3.8 %collective-permute-start.4 = (bf16[256,256]{1,0:T(8,128)(2,1)S(1)}, bf16[256,256]{1,0:T(8,128)(2,1)S(1)}, u32[]{:S(2)}, u32[]{:S(2)}) collective-permute-start(bf16[256,256]{1,0:T(8,128)(2,1)S(1)} %copy-done.17), channel_id=1, source_target_pairs={{8,0},{12,4},{16,8},{20,12},{24,16},{28,20},{32,24},{36,28},{40,32... | collective-permute-start | bytes 393224 | tf_op jit(solution)/shard_map/ppermute | solution.py:22
  57.1 2.2 %collective-permute-start = (bf16[256,128]{1,0:T(8,128)(2,1)}, bf16[256,128]{1,0:T(8,128)(2,1)S(1)}, u32[]{:S(2)}, u32[]{:S(2)}) collective-permute-start(bf16[256,128]{1,0:T(8,128)(2,1)} %get-tuple-element.18.own_ref), channel_id=1, source_target_pairs={{0,1},{1,0},{2,3},{3,2},{4,5},{5,4},{6,7},{7,6},{8,9},{9,8},{10,11... | collective-permute-start | bytes 196616 | tf_op jit(solution)/shard_map/ppermute | solution.py:376
  59.3 3.4 %collective-permute-done.partner_ref = bf16[256,128]{1,0:T(8,128)(2,1)S(1)} collective-permute-done((bf16[256,128]{1,0:T(8,128)(2,1)}, bf16[256,128]{1,0:T(8,128)(2,1)S(1)}, u32[]{:S(2)}, u32[]{:S(2)}) %collective-permute-start) | collective-permute-done | bytes 65568 | tf_op jit(solution)/shard_map/ppermute | solution.py:376
  62.7 0.0 collective-permute-done.3.h2_ref
  62.7 0.0 collective-permute-done.4.h3_ref
  62.7 0.0 copy-done.5
  62.7 0.0 copy-start.4
  62.7 0.8 copy-done.4
  63.6 2.6 %local.1 = (f32[3,256,256]{2,1,0:T(8,128)S(1)}, f32[3,256,128]{2,1,0:T(8,128)S(1)}, bf16[256,128]{1,0:T(8,128)(2,1)S(1)}, bf16[16,80,128]{2,1,0:T(8,128)(2,1)S(1)}) custom-call(s32[21]{0:T(128)S(1)} %copy-done.5, s32[2]{0:T(128)S(1)} %copy-done.6, bf16[3,256,128]{2,1,0:T(8,128)(2,1)S(1)} %get-tuple-element.20.q_ref, bf16[256,128]{1,0:T(8,128)(2,1)S(1)} %copy-done.4, ...), custom_call_target="tpu_custom_call" | custom-call | tf_op jit(solution)/shard_map/local/pallas_call | solution.py:384
  66.2 0.0 all-to-all-done.2.planes_ref
  66.2 1.6 %second_pick.1 = bf16[1,5,16,256]{3,2,1,0:T(8,128)(2,1)} custom-call(s32[5]{0:T(128)} %owner_ref.3, bf16[8,5,16,256]{3,2,1,0:T(8,128)(2,1)} %all-to-all-done.2.planes_ref), custom_call_target="tpu_custom_call" | custom-call | tf_op jit(solution)/shard_map/second_pick/pallas_call | solution.py:117
  67.8 18.1 %all_gather.3.hot_ref = bf16[16,5,16,256]{3,2,1,0:T(8,128)(2,1)S(1)} all-gather(bf16[1,5,16,256]{3,2,1,0:T(8,128)(2,1)} %second_pick.1), channel_id=1, replica_groups=mesh['z'=8,'y'=8,'core'=2,'tp'=4] {'y','core'}, dimensions={0}, use_global_device_ids=true | all-gather | bytes 696320 | tf_op jit(solution)/shard_map/all_gather | solution.py:399
  85.9 0.0 copy-done.2
  85.9 2.5 %shared.1 = bf16[4,256,384]{2,1,0:T(8,128)(2,1)S(1)} custom-call(bf16[3,256,128]{2,1,0:T(8,128)(2,1)S(1)} %get-tuple-element.20.q_ref, f32[3,256,256]{2,1,0:T(8,128)S(1)} %get-tuple-element.31.mixed_ref, f32[3,256,128]{2,1,0:T(8,128)S(1)} %get-tuple-element.32.top_ref, bf16[256,128]{1,0:T(8,128)(2,1)S(1)} %get-tuple-element.33.marks_ref, ...), custom_call_target="tpu_custom_call" | custom-call | tf_op jit(solution)/shard_map/shared/pallas_call | solution.py:400
  88.4 0.0 copy-start.8
  88.5 14.5 %all_to_all.20 = bf16[4,256,384]{2,1,0:T(8,128)(2,1)S(1)} all-to-all(bf16[4,256,384]{2,1,0:T(8,128)(2,1)S(1)} %shared.1), channel_id=1, replica_groups=mesh['z'=8,'y'=8,'core'=2,'tp'=4] {'tp'}, dimensions={0} | all-to-all | bytes 1572864 | tf_op jit(solution)/shard_map/all_to_all | solution.py:408
  103.0 0.1 convert_reduce_fusion
  103.1 0.0 copy-done.8
  103.1 0.7 add_convert_fusion
  (9 shorter events, 0.0 us)
Async XLA Ops:
  0.6 14.3 %copy-start = (bf16[256,512]{1,0:T(8,128)(2,1)S(1)}, bf16[256,512]{1,0:T(8,128)(2,1)}, u32[]{:S(2)}) copy-start(bf16[256,512]{1,0:T(8,128)(2,1)} %param.23) | copy-start | bytes 786436
  0.6 6.9 %copy-start.15 = (s32[1,4]{1,0:T(1,128)S(1)}, s32[1,4]{1,0:T(1,128)}, u32[]{:S(2)}) copy-start(s32[1,4]{1,0:T(1,128)} %param.31) | copy-start | bytes 52
  0.7 6.9 %copy-start.14 = (s32[1,4]{1,0:T(1,128)S(1)}, s32[1,4]{1,0:T(1,128)}, u32[]{:S(2)}) copy-start(s32[1,4]{1,0:T(1,128)} %param.30) | copy-start | bytes 52
  0.7 6.9 %copy-start.12 = (s32[1,4]{1,0:T(1,128)S(1)}, s32[1,4]{1,0:T(1,128)}, u32[]{:S(2)}) copy-start(s32[1,4]{1,0:T(1,128)} %param.29) | copy-start | bytes 52
  0.7 6.9 %copy-start.13 = (s32[1,4]{1,0:T(1,128)S(1)}, s32[1,4]{1,0:T(1,128)}, u32[]{:S(2)}) copy-start(s32[1,4]{1,0:T(1,128)} %param.28) | copy-start | bytes 52
  0.7 6.9 %copy-start.16 = (s32[5]{0:T(128)S(1)}, s32[5]{0:T(128)}, u32[]{:S(2)}) copy-start(s32[5]{0:T(128)} %param.24) | copy-start | bytes 64
  2.7 13.2 %all-to-all-start = ((bf16[4,256,384]{2,1,0:T(8,128)(2,1)}), bf16[4,256,384]{2,1,0:T(8,128)(2,1)S(1)}, u32[]{:S(2)}, u32[]{:S(2)}) async-start(bf16[4,256,384]{2,1,0:T(8,128)(2,1)} %broadcast_in_dim.16), calls=%async_computation | async-start | bytes 1572864 | tf_op jit(solution)/shard_map/all_to_all | solution.py:325
  7.5 25.3 %copy-start.11 = (f32[384]{0:T(512)S(1)}, f32[384]{0:T(512)}, u32[]{:S(2)}) copy-start(f32[384]{0:T(512)} %param.19) | copy-start | bytes 4612
  7.5 25.3 %copy-start.10 = (f32[1536]{0:T(1024)S(1)}, f32[1536]{0:T(1024)}, u32[]{:S(2)}) copy-start(f32[1536]{0:T(1024)} %param.17) | copy-start | bytes 18436
  8.8 24.1 %copy-start.1 = (bf16[1536,384]{1,0:T(8,128)(2,1)S(1)}, bf16[1536,384]{1,0:T(8,128)(2,1)}, u32[]{:S(2)}) copy-start(bf16[1536,384]{1,0:T(8,128)(2,1)} %wq_ref.1) | copy-start | bytes 3538948
  8.8 24.1 %copy-start.3 = (bf16[1536,128]{1,0:T(8,128)(2,1)S(1)}, bf16[1536,128]{1,0:T(8,128)(2,1)}, u32[]{:S(2)}) copy-start(bf16[1536,128]{1,0:T(8,128)(2,1)} %wkv_ref.1) | copy-start | bytes 1179652
  8.8 24.1 %copy-start.6 = (s32[2]{0:T(128)S(1)}, s32[2]{0:T(128)}, u32[]{:S(2)}) copy-start(s32[2]{0:T(128)} %pad_add_fusion.place_ref) | copy-start | bytes 28
  8.8 24.2 %copy-start.7 = (f32[128]{0:T(128)S(1)}, f32[128]{0:T(128)}, u32[]{:S(2)}) copy-start(f32[128]{0:T(128)} %param.21) | copy-start | bytes 1540
  11.7 23.7 %collective-permute-start.1 = (bf16[256,256]{1,0:T(8,128)(2,1)}, bf16[256,256]{1,0:T(8,128)(2,1)S(1)}, u32[]{:S(2)}, u32[]{:S(2)}) collective-permute-start(bf16[256,256]{1,0:T(8,128)(2,1)} %get-tuple-element.22), channel_id=1, source_target_pairs={{504,0},{508,4},{0,8},{4,12},{8,16},{12,20},{16,24},{20,28},{24,32... | collective-permute-start | bytes 393224 | tf_op jit(solution)/shard_map/ppermute | solution.py:22
  15.8 21.2 %all-to-all-start.1 = ((bf16[16,16,256]{2,1,0:T(8,128)(2,1)}), bf16[16,16,256]{2,1,0:T(8,128)(2,1)S(1)}, u32[]{:S(2)}, u32[]{:S(2)}) async-start(bf16[16,16,256]{2,1,0:T(8,128)(2,1)} %bitcast.8), calls=%async_computation.1 | async-start | bytes 262144 | tf_op jit(solution)/shard_map/all_to_all | solution.py:344
  27.9 7.5 %collective-permute-start.2 = (bf16[256,256]{1,0:T(8,128)(2,1)}, bf16[256,256]{1,0:T(8,128)(2,1)S(1)}, u32[]{:S(2)}, u32[]{:S(2)}) collective-permute-start(bf16[256,256]{1,0:T(8,128)(2,1)} %get-tuple-element.26), channel_id=1, source_target_pairs={{508,0},{0,4},{4,8},{8,12},{12,16},{16,20},{20,24},{24,28},{28,32}... | collective-permute-start | bytes 393224 | tf_op jit(solution)/shard_map/ppermute | solution.py:22
  33.0 16.5 %copy-start.18 = (bf16[256,256]{1,0:T(8,128)(2,1)S(1)}, bf16[256,256]{1,0:T(8,128)(2,1)}, u32[]{:S(2)}) copy-start(bf16[256,256]{1,0:T(8,128)(2,1)} %get-tuple-element.29) | copy-start | bytes 393220
  33.0 20.3 %copy-start.17 = (bf16[256,256]{1,0:T(8,128)(2,1)S(1)}, bf16[256,256]{1,0:T(8,128)(2,1)}, u32[]{:S(2)}) copy-start(bf16[256,256]{1,0:T(8,128)(2,1)} %get-tuple-element.30) | copy-start | bytes 393220
  33.0 29.7 %copy-start.5 = (s32[21]{0:T(128)S(1)}, s32[21]{0:T(128)}, u32[]{:S(2)}) copy-start(s32[21]{0:T(128)} %concatenate.9.info_ref) | copy-start | bytes 256
  37.0 0.7 copy-start.9
  39.4 46.5 %copy-start.2 = (bf16[384,1536]{1,0:T(8,128)(2,1)S(1)}, bf16[384,1536]{1,0:T(8,128)(2,1)}, u32[]{:S(2)}) copy-start(bf16[384,1536]{1,0:T(8,128)(2,1)} %wo_ref.1) | copy-start | bytes 3538948
  39.4 26.8 %all-to-all-start.2 = ((bf16[8,5,16,256]{3,2,1,0:T(8,128)(2,1)}), bf16[8,5,16,256]{3,2,1,0:T(8,128)(2,1)}, u32[]{:S(2)}, u32[]{:S(2)}) async-start(bf16[8,5,16,256]{3,2,1,0:T(8,128)(2,1)} %first_pick.1), calls=%async_computation.2 | async-start | bytes 655360 | tf_op jit(solution)/shard_map/all_to_all | solution.py:380
  49.5 13.2 %collective-permute-start.3 = (bf16[256,256]{1,0:T(8,128)(2,1)S(1)}, bf16[256,256]{1,0:T(8,128)(2,1)S(1)}, u32[]{:S(2)}, u32[]{:S(2)}) collective-permute-start(bf16[256,256]{1,0:T(8,128)(2,1)S(1)} %copy-done.18), channel_id=1, source_target_pairs={{4,0},{8,4},{12,8},{16,12},{20,16},{24,20},{28,24},{32,28},{36,32}... | collective-permute-start | bytes 393224 | tf_op jit(solution)/shard_map/ppermute | solution.py:22
  53.3 9.4 %collective-permute-start.4 = (bf16[256,256]{1,0:T(8,128)(2,1)S(1)}, bf16[256,256]{1,0:T(8,128)(2,1)S(1)}, u32[]{:S(2)}, u32[]{:S(2)}) collective-permute-start(bf16[256,256]{1,0:T(8,128)(2,1)S(1)} %copy-done.17), channel_id=1, source_target_pairs={{8,0},{12,4},{16,8},{20,12},{24,16},{28,20},{32,24},{36,28},{40,32... | collective-permute-start | bytes 393224 | tf_op jit(solution)/shard_map/ppermute | solution.py:22
  57.1 5.6 %collective-permute-start = (bf16[256,128]{1,0:T(8,128)(2,1)}, bf16[256,128]{1,0:T(8,128)(2,1)S(1)}, u32[]{:S(2)}, u32[]{:S(2)}) collective-permute-start(bf16[256,128]{1,0:T(8,128)(2,1)} %get-tuple-element.18.own_ref), channel_id=1, source_target_pairs={{0,1},{1,0},{2,3},{3,2},{4,5},{5,4},{6,7},{7,6},{8,9},{9,8},{10,11... | collective-permute-start | bytes 196616 | tf_op jit(solution)/shard_map/ppermute | solution.py:376
  62.7 0.8 copy-start.4
  88.4 14.7 %copy-start.8 = (bf16[256,384]{1,0:T(8,128)(2,1)S(1)}, bf16[256,384]{1,0:T(8,128)(2,1)}, u32[]{:S(2)}) copy-start(bf16[256,384]{1,0:T(8,128)(2,1)} %param.16) | copy-start | bytes 589828

commit v4 on v3

--- a/solution.py
+++ b/solution.py
@@ -1,3 +1,4 @@
+import functools
 import math
 
 import jax
@@ -85,6 +86,7 @@
         in_specs=[scalars] * 3 + [anywhere],
         out_specs=whole(1 + slots),
         scratch_shapes=[pltpu.SemaphoreType.DMA((pages.shape[0],))],
+        compiler_params=pltpu.CompilerParams(vmem_limit_bytes=4 * 2**20),
         name="prepare",
     )(info, pages, place, hist_pool)
 
@@ -103,6 +105,7 @@
         out_shape=jax.ShapeDtypeStruct((planes, owner.shape[0]) + arrived.shape[1:], bf16),
         in_specs=[pl.BlockSpec(memory_space=pltpu.SMEM)] + whole(1),
         out_specs=whole(1)[0],
+        compiler_params=pltpu.CompilerParams(vmem_limit_bytes=4 * 2**20),
         name="first_pick",
     )(owner, arrived)
 
@@ -124,7 +127,8 @@
 
 
 def projection_kernel(
-    place_ref, tok_ref, gain_ref, wq_ref, wkv_ref, qb_ref, kb_ref, cos_ref, sin_ref, q_ref, own_ref
+    place_ref, tok_ref, gain_ref, wq_ref, wkv_ref, qb_ref, kb_ref, cos_ref, sin_ref,
+    q_ref, own_ref, kept_ref
 ):
     groups, rows, width = tok_ref.shape
     total = jnp.zeros((rows, 1), f32)
@@ -155,10 +159,12 @@
     @pl.when(place_ref[0] % 2 == 0)
     def _():
         own_ref[...] = turned(fresh).astype(bf16)
+        kept_ref[...] = turned(fresh).astype(bf16)
 
     @pl.when(place_ref[0] % 2 == 1)
     def _():
         own_ref[...] = fresh.astype(bf16)
+        kept_ref[...] = fresh.astype(bf16)
 
 
 def bars(bad):
@@ -173,8 +179,8 @@
 
 
 def local_kernel(
-    info_ref, place_ref, q_ref, own_ref, partner_ref, h0_ref, h1_ref, h2_ref, h3_ref,
-    mixed_ref, top_ref, marks_ref, bars_ref, key_ref, value_ref,
+    chunk, info_ref, place_ref, q_ref, own_ref, partner_ref, h0_ref, h1_ref, h2_ref, h3_ref,
+    mixed_ref, top_ref, bars_ref, key_ref, value_ref,
 ):
     heads, rows, dim = q_ref.shape
     hist_refs = (h0_ref, h1_ref, h2_ref, h3_ref)
@@ -202,10 +208,11 @@
         | (lane == 2 * requests)
     )
     marks = jnp.where(hit, 1.0, 0.0).astype(bf16)
-    marks_ref[...] = marks
-
-    chunks, per_chunk, _ = bars_ref.shape
-    chunk = per_chunk // nodes
+    shared_rows = bars_ref.shape[0] - rows
+    bars_ref[shared_rows:, :] = marks
+
+    per_chunk = chunk * nodes
+    chunks = shared_rows // per_chunk
     index = lax.broadcasted_iota(int32, (per_chunk, dim), 0)
     side = lax.broadcasted_iota(int32, (per_chunk, dim), 1)
     node = jnp.zeros(index.shape, int32)
@@ -217,7 +224,7 @@
     other = (side >= requests) & (side < 2 * requests) & (node > 0) & (side != requests + node - 1)
     last = side == 2 * requests
     for s in range(chunks):
-        bars_ref[s] = bars(other | (last & (left <= s * chunk)))
+        bars_ref[s * per_chunk : (s + 1) * per_chunk, :] = bars(other | (last & (left <= s * chunk)))
 
     keys = []
     values = []
@@ -261,14 +268,14 @@
         top_ref[h] = jnp.broadcast_to(top, (rows, dim))
 
 
-def shared_kernel(q_ref, mixed_ref, top_ref, marks_ref, bars_ref, hot_ref, wo_ref, out_ref):
+def shared_kernel(q_ref, mixed_ref, top_ref, bars_ref, hot_ref, wo_ref, out_ref):
     heads, rows, dim = q_ref.shape
     chunks, nodes, chunk, _ = hot_ref.shape
     hot = hot_ref[...].reshape(chunks * nodes * chunk, 2 * dim)
-    keys = jnp.concatenate([hot[:, :dim], bars_ref[...].reshape(-1, dim)], axis=1)
+    keys = jnp.concatenate([hot[:, :dim], bars_ref[: hot.shape[0], :]], axis=1)
     values = hot[:, dim:]
     values = jnp.concatenate([values, jnp.ones_like(values)], axis=1)
-    marks = marks_ref[...]
+    marks = bars_ref[hot.shape[0] :, :]
     scale = scale_of(dim)
     merged = []
     for h in range(heads):
@@ -352,14 +359,15 @@
     sine = jnp.sin(angle)
     cosine = jnp.concatenate([cosine, cosine], axis=1)
     sine = jnp.concatenate([-sine, sine], axis=1)
-    queries, own_block = pl.pallas_call(
+    queries, own_block, own_kept = pl.pallas_call(
         projection_kernel,
         out_shape=[
             jax.ShapeDtypeStruct((head_count, row_count, head_dim), bf16),
             jax.ShapeDtypeStruct((row_count, head_dim), bf16),
+            jax.ShapeDtypeStruct((row_count, head_dim), bf16),
         ],
         in_specs=[scalars] + whole(8),
-        out_specs=whole(2),
+        out_specs=whole(3),
         compiler_params=pltpu.CompilerParams(vmem_limit_bytes=32 * 2**20),
         name="projection",
     )(
@@ -374,7 +382,6 @@
         sine,
     )
     partner = lax.ppermute(own_block, "tp", [(i, i ^ 1) for i in range(group_count)])
-    slots[1] = after(slots[1], pieces)
     histories += [history(0), history(1)]
     chosen = first_pick(shared_owner, after(arrived, own_block, *histories), z_count)
     planes = lax.all_to_all(chosen, "z", 0, 0, tiled=True)
@@ -382,25 +389,24 @@
     slots[3] = after(slots[3], chosen)
     histories += [history(2), history(3)]
     local = pl.pallas_call(
-        local_kernel,
+        functools.partial(local_kernel, chunk),
         out_shape=[
             jax.ShapeDtypeStruct((head_count, row_count, 2 * head_dim), f32),
             jax.ShapeDtypeStruct((head_count, row_count, head_dim), f32),
-            jax.ShapeDtypeStruct((row_count, head_dim), bf16),
-            jax.ShapeDtypeStruct((plane_count, node_total * chunk, head_dim), bf16),
+            jax.ShapeDtypeStruct((plane_count * node_total * chunk + row_count, head_dim), bf16),
         ],
         in_specs=[scalars] * 2 + whole(7),
-        out_specs=whole(4),
+        out_specs=whole(3),
         scratch_shapes=[pltpu.VMEM((row_count, head_dim), bf16)] * 2,
         compiler_params=pltpu.CompilerParams(vmem_limit_bytes=40 * 2**20),
         name="local",
-    )(info, place, queries, own_block, partner, *histories)
+    )(info, place, queries, own_kept, partner, *histories)
     kept = second_pick(shared_owner, after(planes, *local), plane_count, 1)[0]
     hot = lax.all_gather(kept, seq_axes[1:], axis=0, tiled=False)
     blocks = pl.pallas_call(
         shared_kernel,
         out_shape=jax.ShapeDtypeStruct((group_count, row_count, width), bf16),
-        in_specs=whole(7),
+        in_specs=whole(6),
         out_specs=whole(1)[0],
         compiler_params=pltpu.CompilerParams(vmem_limit_bytes=40 * 2**20),
         name="shared",

time: 105 us -> 103 us (0.981)
  waiting for transfers between devices: 5.34 us -> 8.48 us
  starting transfers between devices: 43.5 us -> 41.3 us
  Pallas kernels: 13.5 us -> 11.7 us
  other arithmetic: 2.97 us -> 1.51 us
  blocking collectives: 32.7 us -> 33.9 us
    all_to_all x1, waiting for transfers between devices: 1.66 us -> 5.45 us  [on_device(): lax.all_to_all(pieces.reshape(plane_count, chunk, -1), seq_axes[1:], 0, 0...]
    all_to_all x1, starting transfers between devices: 12 us -> 10.1 us  [on_device(): lax.all_to_all(pieces.reshape(plane_count, chunk, -1), seq_axes[1:], 0, 0...]
    all_gather x1, blocking collectives: 18.1 us -> 19.4 us  [on_device(): hot = lax.all_gather(kept, seq_axes[1:], axis=0, tiled=False)]
    pallas_call x1, Pallas kernels: 2.81 us -> 1.59 us  [prepared(): pl.pallas_call(prepare_kernel, out_shape=[jax.ShapeDtypeStruct((row_count...]
  transfers between devices with their start and end apart: 8 -> 8, of which waited for: 3 -> 2; matrix products, arithmetic and copies ran while one was open for 3% -> 2% of each run, Pallas kernels for 7% -> 6%
where the time goes in v4:
time: 103 us; the launch traced here: 102 us
  starting transfers between devices  41.3 us (40%)
  blocking collectives  33.9 us (33%)
  Pallas kernels  11.7 us (11%)
  waiting for transfers between devices  8.48 us (8%)
  local copies, waits for them, and re-layouts  4.44 us (4%)
  other arithmetic  1.51 us (1%)
    all_gather x1, blocking collectives, on_device(): hot = lax.all_gather(kept, seq_axes[1:], axis=0, tiled=False)  19.4 us
    all_to_all x1, blocking collectives, on_device(): lax.all_to_all(blocks, 'tp', 0, 0, tiled=True).astype(f32)  14.5 us
    ppermute x4, starting transfers between devices, passed_along(): lax.ppermute(block, axis, [((i - distance) % len(devices), i) for i in de...  14 us
    all_to_all x1, starting transfers between devices, on_device(): planes = lax.all_to_all(chosen, 'z', 0, 0, tiled=True)  10.2 us
    all_to_all x1, starting transfers between devices, on_device(): lax.all_to_all(pieces.reshape(plane_count, chunk, -1), seq_axes[1:], 0, 0...  10.1 us
    all_to_all x1, waiting for transfers between devices, on_device(): lax.all_to_all(pieces.reshape(plane_count, chunk, -1), seq_axes[1:], 0, 0...  5.45 us
    all_to_all x1, starting transfers between devices, on_device(): features = lax.all_to_all(copies, 'tp', 0, 0, tiled=True)  4.84 us
    ppermute x1, waiting for transfers between devices, on_device(): lax.ppermute(own_block, 'tp', [(i, i ^ 1) for i in range(group_count)])  3.02 us
  transfers between devices with their start and end apart: 8, of which 2 were waited for; matrix products, arithmetic and copies ran while one was open for 2% of the time, Pallas kernels for 6%

profile of v4, /device:TPU:1, one launch (start us, length us, event | category | flops | bytes accessed | tf_op | source)
XLA Modules:
  0.0 102.3 jit_solution(8803389179198579226)
XLA Ops:
  0.6 0.0 copy-start
  0.6 0.0 copy-start.17
  0.7 0.0 copy-start.16
  0.7 0.0 copy-start.14
  0.7 0.0 copy-start.15
  0.7 0.0 copy-start.18
  0.7 0.0 copy-start.8
  0.7 0.0 copy-start.3
  0.7 2.0 %broadcast_in_dim.16 = bf16[4,256,384]{2,1,0:T(8,128)(2,1)} broadcast(bf16[256,384]{1,0:T(8,128)(2,1)} %param.16), dimensions={1,2} | broadcast | bytes 983040 | tf_op jit(solution)/shard_map/broadcast_in_dim | solution.py:331
  2.7 4.8 %all-to-all-start = ((bf16[4,256,384]{2,1,0:T(8,128)(2,1)}), bf16[4,256,384]{2,1,0:T(8,128)(2,1)S(1)}, u32[]{:S(2)}, u32[]{:S(2)}) async-start(bf16[4,256,384]{2,1,0:T(8,128)(2,1)} %broadcast_in_dim.16), calls=%async_computation | async-start | bytes 1572864 | tf_op jit(solution)/shard_map/all_to_all | solution.py:332
  7.6 0.0 copy-done.17
  7.6 0.0 copy-done.16
  7.6 0.0 copy-done.14
  7.6 0.0 copy-done.15
  7.6 0.0 copy-done.18
  7.6 0.1 concatenate.9.info_ref
  7.7 0.1 pad_add_fusion.place_ref
  7.7 0.0 copy-done.8
  7.7 0.0 copy-done.3
  7.8 1.6 %prepare.1 = (f32[256,128]{1,0:T(8,128)S(1)}, bf16[256,256]{1,0:T(8,128)(2,1)}, bf16[256,256]{1,0:T(8,128)(2,1)}, bf16[256,256]{1,0:T(8,128)(2,1)S(1)}, bf16[256,256]{1,0:T(8,128)(2,1)S(1)}) custom-call(s32[21]{0:T(128)S(1)} %concatenate.9.info_ref, s32[16]{0:T(128)S(1)} %bitcast.9, s32[2]{0:T(128)S(1)} %pad_add_fusion.place_ref, ...), custom_call_target="tpu_custom_call" | custom-call | tf_op jit(solution)/shard_map/prepare/pallas_call | solution.py:82
  9.4 0.0 copy-start.10
  9.4 0.0 copy-start.11
  9.4 0.0 copy-start.4
  9.4 3.3 %collective-permute-start.1 = (bf16[256,256]{1,0:T(8,128)(2,1)}, bf16[256,256]{1,0:T(8,128)(2,1)S(1)}, u32[]{:S(2)}, u32[]{:S(2)}) collective-permute-start(bf16[256,256]{1,0:T(8,128)(2,1)} %get-tuple-element.22), channel_id=1, source_target_pairs={{504,0},{508,4},{0,8},{4,12},{8,16},{12,20},{16,24},{20,28},{24,32... | collective-permute-start | bytes 393224 | tf_op jit(solution)/shard_map/ppermute | solution.py:23
  12.7 0.0 copy-done.10
  12.7 0.0 copy-done.11
  12.8 4.3 %collective-permute-start.2 = (bf16[256,256]{1,0:T(8,128)(2,1)}, bf16[256,256]{1,0:T(8,128)(2,1)S(1)}, u32[]{:S(2)}, u32[]{:S(2)}) collective-permute-start(bf16[256,256]{1,0:T(8,128)(2,1)} %get-tuple-element.23), channel_id=1, source_target_pairs={{508,0},{0,4},{4,8},{8,12},{12,16},{16,20},{20,24},{24,28},{28,32}... | collective-permute-start | bytes 393224 | tf_op jit(solution)/shard_map/ppermute | solution.py:23
  17.1 0.0 copy-done
  17.1 0.7 constant_dynamic-slice_fusion
  17.8 0.0 all-to-all-done.tok_ref
  17.8 10.1 %all-to-all-start.1 = ((bf16[16,16,256]{2,1,0:T(8,128)(2,1)}), bf16[16,16,256]{2,1,0:T(8,128)(2,1)S(1)}, u32[]{:S(2)}, u32[]{:S(2)}) async-start(bf16[16,16,256]{2,1,0:T(8,128)(2,1)} %bitcast.8), calls=%async_computation.1 | async-start | bytes 262144 | tf_op jit(solution)/shard_map/all_to_all | solution.py:351
  27.9 0.5 fusion.2
  28.4 0.0 copy-done.13
  28.4 0.7 broadcast_in_dim.17.gain_ref
  29.1 0.1 pad_maximum_fusion
  29.2 0.0 copy-done.1
  29.3 0.0 copy-done.9
  29.3 0.0 copy-done.4
  29.3 0.0 copy-start.7
  29.3 2.3 %projection.1 = (bf16[3,256,128]{2,1,0:T(8,128)(2,1)S(1)}, bf16[256,128]{1,0:T(8,128)(2,1)}, bf16[256,128]{1,0:T(8,128)(2,1)S(1)}) custom-call(s32[2]{0:T(128)S(1)} %pad_add_fusion.place_ref, bf16[4,256,384]{2,1,0:T(8,128)(2,1)S(1)} %all-to-all-done.tok_ref, f32[1,1536]{1,0:T(1,128)S(1)} %broadcast_in_dim.17.gain_ref, bf16[1536,384]{1,0:T(8,128)(2,1)S(1)} %copy-done.1, ...), custom_call_target="tpu_custom_call" | custom-call | tf_op jit(solution)/shard_map/projection/pallas_call | solution.py:362
  31.6 0.0 collective-permute-done.1.h0_ref
  31.6 0.0 collective-permute-done.2.h1_ref
  31.6 5.4 %all-to-all-done.1.arrived_ref = bf16[16,16,256]{2,1,0:T(8,128)(2,1)S(1)} async-done(((bf16[16,16,256]{2,1,0:T(8,128)(2,1)}), bf16[16,16,256]{2,1,0:T(8,128)(2,1)S(1)}, u32[]{:S(2)}, u32[]{:S(2)}) %all-to-all-start.1) | async-done | bytes 131104 | tf_op jit(solution)/shard_map/all_to_all | solution.py:351
  37.1 0.0 copy-done.7
  37.1 1.3 %first_pick.1 = bf16[8,5,16,256]{3,2,1,0:T(8,128)(2,1)} custom-call(s32[5]{0:T(128)S(1)} %copy-done.7, bf16[16,16,256]{2,1,0:T(8,128)(2,1)S(1)} %all-to-all-done.1.arrived_ref), custom_call_target="tpu_custom_call" | custom-call | tf_op jit(solution)/shard_map/first_pick/pallas_call | solution.py:103
  38.4 10.2 %all-to-all-start.2 = ((bf16[8,5,16,256]{3,2,1,0:T(8,128)(2,1)}), bf16[8,5,16,256]{3,2,1,0:T(8,128)(2,1)}, u32[]{:S(2)}, u32[]{:S(2)}) async-start(bf16[8,5,16,256]{3,2,1,0:T(8,128)(2,1)} %first_pick.1), calls=%async_computation.2 | async-start | bytes 655360 | tf_op jit(solution)/shard_map/all_to_all | solution.py:387
  48.5 1.9 %collective-permute-start.3 = (bf16[256,256]{1,0:T(8,128)(2,1)}, bf16[256,256]{1,0:T(8,128)(2,1)S(1)}, u32[]{:S(2)}, u32[]{:S(2)}) collective-permute-start(bf16[256,256]{1,0:T(8,128)(2,1)} %copy-done.11), channel_id=1, source_target_pairs={{4,0},{8,4},{12,8},{16,12},{20,16},{24,20},{28,24},{32,28},{36,32}... | collective-permute-start | bytes 393224 | tf_op jit(solution)/shard_map/ppermute | solution.py:23
  50.5 4.4 %collective-permute-start.4 = (bf16[256,256]{1,0:T(8,128)(2,1)}, bf16[256,256]{1,0:T(8,128)(2,1)S(1)}, u32[]{:S(2)}, u32[]{:S(2)}) collective-permute-start(bf16[256,256]{1,0:T(8,128)(2,1)} %copy-done.10), channel_id=1, source_target_pairs={{8,0},{12,4},{16,8},{20,12},{24,16},{28,20},{32,24},{36,28},{40,32... | collective-permute-start | bytes 393224 | tf_op jit(solution)/shard_map/ppermute | solution.py:23
  54.9 2.2 %collective-permute-start = (bf16[256,128]{1,0:T(8,128)(2,1)}, bf16[256,128]{1,0:T(8,128)(2,1)S(1)}, u32[]{:S(2)}, u32[]{:S(2)}) collective-permute-start(bf16[256,128]{1,0:T(8,128)(2,1)} %get-tuple-element.17), channel_id=1, source_target_pairs={{0,1},{1,0},{2,3},{3,2},{4,5},{5,4},{6,7},{7,6},{8,9},{9,8},{10,11... | collective-permute-start | bytes 196616 | tf_op jit(solution)/shard_map/ppermute | solution.py:384
  57.1 3.0 %collective-permute-done.partner_ref = bf16[256,128]{1,0:T(8,128)(2,1)S(1)} collective-permute-done((bf16[256,128]{1,0:T(8,128)(2,1)}, bf16[256,128]{1,0:T(8,128)(2,1)S(1)}, u32[]{:S(2)}, u32[]{:S(2)}) %collective-permute-start) | collective-permute-done | bytes 65568 | tf_op jit(solution)/shard_map/ppermute | solution.py:384
  60.1 0.0 collective-permute-done.3.h2_ref
  60.1 0.0 collective-permute-done.4.h3_ref
  60.1 0.0 copy-done.5
  60.1 0.0 copy-start.6
  60.1 0.9 copy-done.6
  61.0 2.5 %local.1 = (f32[3,256,256]{2,1,0:T(8,128)S(1)}, f32[3,256,128]{2,1,0:T(8,128)S(1)}, bf16[1536,128]{1,0:T(8,128)(2,1)S(1)}) custom-call(s32[21]{0:T(128)S(1)} %concatenate.9.info_ref, s32[2]{0:T(128)S(1)} %pad_add_fusion.place_ref, bf16[3,256,128]{2,1,0:T(8,128)(2,1)S(1)} %get-tuple-element.19.q_ref, bf16[256,128]{1,0:T(8,128)(2,1)S(1)} %get-tuple-element.20.own_ref, ...), custom_call_target="tpu_custom_call" | custom-call | tf_op jit(solution)/shard_map/local/pallas_call | solution.py:391
  63.5 0.0 all-to-all-done.2.planes_ref
  63.5 1.6 %second_pick.1 = bf16[1,5,16,256]{3,2,1,0:T(8,128)(2,1)} custom-call(s32[5]{0:T(128)} %owner_ref.3, bf16[8,5,16,256]{3,2,1,0:T(8,128)(2,1)} %all-to-all-done.2.planes_ref), custom_call_target="tpu_custom_call" | custom-call | tf_op jit(solution)/shard_map/second_pick/pallas_call | solution.py:120
  65.2 19.4 %all_gather.3.hot_ref = bf16[16,5,16,256]{3,2,1,0:T(8,128)(2,1)S(1)} all-gather(bf16[1,5,16,256]{3,2,1,0:T(8,128)(2,1)} %second_pick.1), channel_id=1, replica_groups=mesh['z'=8,'y'=8,'core'=2,'tp'=4] {'y','core'}, dimensions={0}, use_global_device_ids=true | all-gather | bytes 696320 | tf_op jit(solution)/shard_map/all_gather | solution.py:405
  84.5 2.4 %shared.1 = bf16[4,256,384]{2,1,0:T(8,128)(2,1)S(1)} custom-call(bf16[3,256,128]{2,1,0:T(8,128)(2,1)S(1)} %get-tuple-element.19.q_ref, f32[3,256,256]{2,1,0:T(8,128)S(1)} %get-tuple-element.30.mixed_ref, f32[3,256,128]{2,1,0:T(8,128)S(1)} %get-tuple-element.31.top_ref, bf16[1536,128]{1,0:T(8,128)(2,1)S(1)} %get-tuple-element.32.bars_ref, ...), custom_call_target="tpu_custom_call" | custom-call | tf_op jit(solution)/shard_map/shared/pallas_call | solution.py:406
  86.9 0.0 copy-start.12
  86.9 14.5 %all_to_all.20 = bf16[4,256,384]{2,1,0:T(8,128)(2,1)S(1)} all-to-all(bf16[4,256,384]{2,1,0:T(8,128)(2,1)S(1)} %shared.1), channel_id=1, replica_groups=mesh['z'=8,'y'=8,'core'=2,'tp'=4] {'tp'}, dimensions={0} | all-to-all | bytes 1572864 | tf_op jit(solution)/shard_map/all_to_all | solution.py:414
  101.5 0.1 convert_reduce_fusion
  101.6 0.7 add_convert_fusion
  (9 shorter events, 0.0 us)
Async XLA Ops:
  0.6 16.5 %copy-start = (bf16[256,512]{1,0:T(8,128)(2,1)S(1)}, bf16[256,512]{1,0:T(8,128)(2,1)}, u32[]{:S(2)}) copy-start(bf16[256,512]{1,0:T(8,128)(2,1)} %param.23) | copy-start | bytes 786436
  0.6 6.9 %copy-start.17 = (s32[1,4]{1,0:T(1,128)S(1)}, s32[1,4]{1,0:T(1,128)}, u32[]{:S(2)}) copy-start(s32[1,4]{1,0:T(1,128)} %param.31) | copy-start | bytes 52
  0.7 6.9 %copy-start.16 = (s32[1,4]{1,0:T(1,128)S(1)}, s32[1,4]{1,0:T(1,128)}, u32[]{:S(2)}) copy-start(s32[1,4]{1,0:T(1,128)} %param.30) | copy-start | bytes 52
  0.7 6.9 %copy-start.14 = (s32[1,4]{1,0:T(1,128)S(1)}, s32[1,4]{1,0:T(1,128)}, u32[]{:S(2)}) copy-start(s32[1,4]{1,0:T(1,128)} %param.29) | copy-start | bytes 52
  0.7 6.9 %copy-start.15 = (s32[1,4]{1,0:T(1,128)S(1)}, s32[1,4]{1,0:T(1,128)}, u32[]{:S(2)}) copy-start(s32[1,4]{1,0:T(1,128)} %param.28) | copy-start | bytes 52
  0.7 6.9 %copy-start.18 = (s32[5]{0:T(128)S(1)}, s32[5]{0:T(128)}, u32[]{:S(2)}) copy-start(s32[5]{0:T(128)} %param.24) | copy-start | bytes 64
  0.7 7.0 %copy-start.8 = (s32[1,16]{1,0:T(1,128)S(1)}, s32[1,16]{1,0:T(1,128)}, u32[]{:S(2)}) copy-start(s32[1,16]{1,0:T(1,128)} %param.27) | copy-start | bytes 196
  0.7 7.0 %copy-start.3 = (bf16[16,64,512]{2,1,0:T(8,128)(2,1)S(1)}, bf16[16,64,512]{2,1,0:T(8,128)(2,1)}, u32[]{:S(2)}) copy-start(bf16[16,64,512]{2,1,0:T(8,128)(2,1)} %pool_ref.1) | copy-start | bytes 3145732
  2.7 15.1 %all-to-all-start = ((bf16[4,256,384]{2,1,0:T(8,128)(2,1)}), bf16[4,256,384]{2,1,0:T(8,128)(2,1)S(1)}, u32[]{:S(2)}, u32[]{:S(2)}) async-start(bf16[4,256,384]{2,1,0:T(8,128)(2,1)} %broadcast_in_dim.16), calls=%async_computation | async-start | bytes 1572864 | tf_op jit(solution)/shard_map/all_to_all | solution.py:332
  7.5 20.8 %copy-start.13 = (f32[384]{0:T(512)S(1)}, f32[384]{0:T(512)}, u32[]{:S(2)}) copy-start(f32[384]{0:T(512)} %param.19) | copy-start | bytes 4612
  7.8 21.5 %copy-start.1 = (bf16[1536,384]{1,0:T(8,128)(2,1)S(1)}, bf16[1536,384]{1,0:T(8,128)(2,1)}, u32[]{:S(2)}) copy-start(bf16[1536,384]{1,0:T(8,128)(2,1)} %wq_ref.1) | copy-start | bytes 3538948
  7.8 21.5 %copy-start.9 = (f32[128]{0:T(128)S(1)}, f32[128]{0:T(128)}, u32[]{:S(2)}) copy-start(f32[128]{0:T(128)} %param.21) | copy-start | bytes 1540
  9.4 3.4 %copy-start.10 = (bf16[256,256]{1,0:T(8,128)(2,1)}, bf16[256,256]{1,0:T(8,128)(2,1)S(1)}, u32[]{:S(2)}) copy-start(bf16[256,256]{1,0:T(8,128)(2,1)S(1)} %get-tuple-element.29) | copy-start | bytes 393220
  9.4 3.4 %copy-start.11 = (bf16[256,256]{1,0:T(8,128)(2,1)}, bf16[256,256]{1,0:T(8,128)(2,1)S(1)}, u32[]{:S(2)}) copy-start(bf16[256,256]{1,0:T(8,128)(2,1)S(1)} %get-tuple-element.28) | copy-start | bytes 393220
  9.4 19.9 %copy-start.4 = (bf16[1536,128]{1,0:T(8,128)(2,1)S(1)}, bf16[1536,128]{1,0:T(8,128)(2,1)}, u32[]{:S(2)}) copy-start(bf16[1536,128]{1,0:T(8,128)(2,1)} %wkv_ref.1) | copy-start | bytes 1179652
  9.4 22.2 %collective-permute-start.1 = (bf16[256,256]{1,0:T(8,128)(2,1)}, bf16[256,256]{1,0:T(8,128)(2,1)S(1)}, u32[]{:S(2)}, u32[]{:S(2)}) collective-permute-start(bf16[256,256]{1,0:T(8,128)(2,1)} %get-tuple-element.22), channel_id=1, source_target_pairs={{504,0},{508,4},{0,8},{4,12},{8,16},{12,20},{16,24},{20,28},{24,32... | collective-permute-start | bytes 393224 | tf_op jit(solution)/shard_map/ppermute | solution.py:23
  12.8 18.9 %collective-permute-start.2 = (bf16[256,256]{1,0:T(8,128)(2,1)}, bf16[256,256]{1,0:T(8,128)(2,1)S(1)}, u32[]{:S(2)}, u32[]{:S(2)}) collective-permute-start(bf16[256,256]{1,0:T(8,128)(2,1)} %get-tuple-element.23), channel_id=1, source_target_pairs={{508,0},{0,4},{4,8},{8,12},{12,16},{16,20},{20,24},{24,28},{28,32}... | collective-permute-start | bytes 393224 | tf_op jit(solution)/shard_map/ppermute | solution.py:23
  17.8 19.3 %all-to-all-start.1 = ((bf16[16,16,256]{2,1,0:T(8,128)(2,1)}), bf16[16,16,256]{2,1,0:T(8,128)(2,1)S(1)}, u32[]{:S(2)}, u32[]{:S(2)}) async-start(bf16[16,16,256]{2,1,0:T(8,128)(2,1)} %bitcast.8), calls=%async_computation.1 | async-start | bytes 262144 | tf_op jit(solution)/shard_map/all_to_all | solution.py:351
  29.3 7.8 %copy-start.7 = (s32[5]{0:T(128)S(1)}, s32[5]{0:T(128)}, u32[]{:S(2)}) copy-start(s32[5]{0:T(128)} %owner_ref.3) | copy-start | bytes 64
  31.6 28.5 %copy-start.5 = (bf16[256,256]{1,0:T(8,128)(2,1)}, bf16[256,256]{1,0:T(8,128)(2,1)S(1)}, u32[]{:S(2)}) copy-start(bf16[256,256]{1,0:T(8,128)(2,1)S(1)} %collective-permute-done.2.h1_ref) | copy-start | bytes 393220
  38.4 46.2 %copy-start.2 = (bf16[384,1536]{1,0:T(8,128)(2,1)S(1)}, bf16[384,1536]{1,0:T(8,128)(2,1)}, u32[]{:S(2)}) copy-start(bf16[384,1536]{1,0:T(8,128)(2,1)} %wo_ref.1) | copy-start | bytes 3538948
  38.4 25.2 %all-to-all-start.2 = ((bf16[8,5,16,256]{3,2,1,0:T(8,128)(2,1)}), bf16[8,5,16,256]{3,2,1,0:T(8,128)(2,1)}, u32[]{:S(2)}, u32[]{:S(2)}) async-start(bf16[8,5,16,256]{3,2,1,0:T(8,128)(2,1)} %first_pick.1), calls=%async_computation.2 | async-start | bytes 655360 | tf_op jit(solution)/shard_map/all_to_all | solution.py:387
  48.5 11.5 %collective-permute-start.3 = (bf16[256,256]{1,0:T(8,128)(2,1)}, bf16[256,256]{1,0:T(8,128)(2,1)S(1)}, u32[]{:S(2)}, u32[]{:S(2)}) collective-permute-start(bf16[256,256]{1,0:T(8,128)(2,1)} %copy-done.11), channel_id=1, source_target_pairs={{4,0},{8,4},{12,8},{16,12},{20,16},{24,20},{28,24},{32,28},{36,32}... | collective-permute-start | bytes 393224 | tf_op jit(solution)/shard_map/ppermute | solution.py:23
  50.5 9.6 %collective-permute-start.4 = (bf16[256,256]{1,0:T(8,128)(2,1)}, bf16[256,256]{1,0:T(8,128)(2,1)S(1)}, u32[]{:S(2)}, u32[]{:S(2)}) collective-permute-start(bf16[256,256]{1,0:T(8,128)(2,1)} %copy-done.10), channel_id=1, source_target_pairs={{8,0},{12,4},{16,8},{20,12},{24,16},{28,20},{32,24},{36,28},{40,32... | collective-permute-start | bytes 393224 | tf_op jit(solution)/shard_map/ppermute | solution.py:23
  54.9 5.2 %collective-permute-start = (bf16[256,128]{1,0:T(8,128)(2,1)}, bf16[256,128]{1,0:T(8,128)(2,1)S(1)}, u32[]{:S(2)}, u32[]{:S(2)}) collective-permute-start(bf16[256,128]{1,0:T(8,128)(2,1)} %get-tuple-element.17), channel_id=1, source_target_pairs={{0,1},{1,0},{2,3},{3,2},{4,5},{5,4},{6,7},{7,6},{8,9},{9,8},{10,11... | collective-permute-start | bytes 196616 | tf_op jit(solution)/shard_map/ppermute | solution.py:384
  60.1 0.9 copy-start.6
  86.9 14.7 %copy-start.12 = (bf16[256,384]{1,0:T(8,128)(2,1)S(1)}, bf16[256,384]{1,0:T(8,128)(2,1)}, u32[]{:S(2)}) copy-start(bf16[256,384]{1,0:T(8,128)(2,1)} %param.16) | copy-start | bytes 589828

commit v5 on v4

--- a/solution.py
+++ b/solution.py
@@ -91,6 +91,21 @@
     )(info, pages, place, hist_pool)
 
 
+def copied(tokens, count):
+    def kernel(tok_ref, out_ref):
+        for g in range(count):
+            out_ref[g] = tok_ref[...]
+
+    return pl.pallas_call(
+        kernel,
+        out_shape=jax.ShapeDtypeStruct((count,) + tokens.shape, bf16),
+        in_specs=whole(1),
+        out_specs=whole(1)[0],
+        compiler_params=pltpu.CompilerParams(vmem_limit_bytes=4 * 2**20),
+        name="copied",
+    )(tokens)
+
+
 def first_pick_kernel(owner_ref, arrived_ref, out_ref):
     per_plane = arrived_ref.shape[0]
     for n in range(out_ref.shape[1]):
@@ -328,7 +343,7 @@
     place = jnp.stack([tp_index, lax.axis_index("core")]).astype(int32)
     scalars = pl.BlockSpec(memory_space=pltpu.SMEM)
 
-    copies = jnp.broadcast_to(tokens[None], (group_count,) + tokens.shape)
+    copies = copied(tokens, group_count)
     features = lax.all_to_all(copies, "tp", 0, 0, tiled=True)
     info = jnp.concatenate([req_len[0], hist_len[0], req_offset[0], req_parent[0], shared_len])
     position, *slots = prepared(

time: 103 us -> 103 us (level)
    broadcast_in_dim x1 -> x0, local copies, waits for them, and re-layouts: 1.99 us -> none  [on_device(): copies = jnp.broadcast_to(tokens[None], (group_count,) + tokens.shape)]
where the time goes in v5:
time: 103 us; the launch traced here: 102 us
  starting transfers between devices  41.3 us (40%)
  blocking collectives  33.9 us (33%)
  Pallas kernels  12.7 us (12%)
  waiting for transfers between devices  8.48 us (8%)
  local copies, waits for them, and re-layouts  3.47 us (3%)
  other arithmetic  1.51 us (1%)
    all_gather x1, blocking collectives, on_device(): hot = lax.all_gather(kept, seq_axes[1:], axis=0, tiled=False)  19.4 us
    all_to_all x1, blocking collectives, on_device(): lax.all_to_all(blocks, 'tp', 0, 0, tiled=True).astype(f32)  14.5 us
    ppermute x4, starting transfers between devices, passed_along(): lax.ppermute(block, axis, [((i - distance) % len(devices), i) for i in de...  14 us
    all_to_all x1, starting transfers between devices, on_device(): planes = lax.all_to_all(chosen, 'z', 0, 0, tiled=True)  10.2 us
    all_to_all x1, starting transfers between devices, on_device(): lax.all_to_all(pieces.reshape(plane_count, chunk, -1), seq_axes[1:], 0, 0...  10.1 us
    all_to_all x1, waiting for transfers between devices, on_device(): lax.all_to_all(pieces.reshape(plane_count, chunk, -1), seq_axes[1:], 0, 0...  5.45 us
    all_to_all x1, starting transfers between devices, on_device(): features = lax.all_to_all(copies, 'tp', 0, 0, tiled=True)  4.84 us
    ppermute x1, waiting for transfers between devices, on_device(): lax.ppermute(own_block, 'tp', [(i, i ^ 1) for i in range(group_count)])  3.02 us
  transfers between devices with their start and end apart: 8, of which 2 were waited for; matrix products, arithmetic and copies ran while one was open for 2% of the time, Pallas kernels for 6%

profile of v5, /device:TPU:1, one launch (start us, length us, event | category | flops | bytes accessed | tf_op | source)
XLA Modules:
  0.0 102.3 jit_solution(5276480217156098702)
XLA Ops:
  0.6 0.0 copy-start
  0.6 0.0 copy-start.3
  0.7 0.0 copy-start.4
  0.7 1.0 copy-done.4
  1.7 0.0 copy-start.19
  1.7 0.0 copy-start.10
  1.7 1.0 copied.1
  2.7 4.8 %all-to-all-start = ((bf16[4,256,384]{2,1,0:T(8,128)(2,1)}), bf16[4,256,384]{2,1,0:T(8,128)(2,1)S(1)}, u32[]{:S(2)}, u32[]{:S(2)}) async-start(bf16[4,256,384]{2,1,0:T(8,128)(2,1)} %copied.1), calls=%async_computation | async-start | bytes 1572864 | tf_op jit(solution)/shard_map/all_to_all | solution.py:347
  7.5 0.0 copy-done.15
  7.5 0.0 copy-done.16
  7.5 0.0 copy-done.17
  7.6 0.0 copy-done.18
  7.6 0.0 copy-done.19
  7.6 0.1 concatenate.9.info_ref
  7.7 0.1 pad_add_fusion.place_ref
  7.7 0.0 copy-done.3
  7.7 0.0 copy-done.10
  7.7 1.6 %prepare.1 = (f32[256,128]{1,0:T(8,128)S(1)}, bf16[256,256]{1,0:T(8,128)(2,1)}, bf16[256,256]{1,0:T(8,128)(2,1)}, bf16[256,256]{1,0:T(8,128)(2,1)S(1)}, bf16[256,256]{1,0:T(8,128)(2,1)S(1)}) custom-call(s32[21]{0:T(128)S(1)} %concatenate.9.info_ref, s32[16]{0:T(128)S(1)} %bitcast.9, s32[2]{0:T(128)S(1)} %pad_add_fusion.place_ref, ...), custom_call_target="tpu_custom_call" | custom-call | tf_op jit(solution)/shard_map/prepare/pallas_call | solution.py:82
  9.3 0.0 copy-start.12
  9.4 0.0 copy-start.13
  9.4 0.0 copy-start.6
  9.4 3.3 %collective-permute-start.1 = (bf16[256,256]{1,0:T(8,128)(2,1)}, bf16[256,256]{1,0:T(8,128)(2,1)S(1)}, u32[]{:S(2)}, u32[]{:S(2)}) collective-permute-start(bf16[256,256]{1,0:T(8,128)(2,1)} %get-tuple-element.22), channel_id=1, source_target_pairs={{504,0},{508,4},{0,8},{4,12},{8,16},{12,20},{16,24},{20,28},{24,32... | collective-permute-start | bytes 393224 | tf_op jit(solution)/shard_map/ppermute | solution.py:23
  12.7 0.0 copy-done.12
  12.7 0.0 copy-done.13
  12.7 4.3 %collective-permute-start.2 = (bf16[256,256]{1,0:T(8,128)(2,1)}, bf16[256,256]{1,0:T(8,128)(2,1)S(1)}, u32[]{:S(2)}, u32[]{:S(2)}) collective-permute-start(bf16[256,256]{1,0:T(8,128)(2,1)} %get-tuple-element.23), channel_id=1, source_target_pairs={{508,0},{0,4},{4,8},{8,12},{12,16},{16,20},{20,24},{24,28},{28,32}... | collective-permute-start | bytes 393224 | tf_op jit(solution)/shard_map/ppermute | solution.py:23
  17.1 0.0 copy-done
  17.1 0.7 constant_dynamic-slice_fusion
  17.8 0.0 all-to-all-done.tok_ref
  17.8 10.1 %all-to-all-start.1 = ((bf16[16,16,256]{2,1,0:T(8,128)(2,1)}), bf16[16,16,256]{2,1,0:T(8,128)(2,1)S(1)}, u32[]{:S(2)}, u32[]{:S(2)}) async-start(bf16[16,16,256]{2,1,0:T(8,128)(2,1)} %bitcast.8), calls=%async_computation.1 | async-start | bytes 262144 | tf_op jit(solution)/shard_map/all_to_all | solution.py:366
  27.9 0.5 fusion.2
  28.4 0.0 copy-done.14
  28.4 0.7 broadcast_in_dim.10.gain_ref
  29.1 0.1 pad_maximum_fusion
  29.2 0.0 copy-done.1
  29.2 0.0 copy-done.11
  29.3 0.0 copy-done.6
  29.3 0.0 copy-start.9
  29.3 2.3 %projection.1 = (bf16[3,256,128]{2,1,0:T(8,128)(2,1)S(1)}, bf16[256,128]{1,0:T(8,128)(2,1)}, bf16[256,128]{1,0:T(8,128)(2,1)S(1)}) custom-call(s32[2]{0:T(128)S(1)} %pad_add_fusion.place_ref, bf16[4,256,384]{2,1,0:T(8,128)(2,1)S(1)} %all-to-all-done.tok_ref, f32[1,1536]{1,0:T(1,128)S(1)} %broadcast_in_dim.10.gain_ref, bf16[1536,384]{1,0:T(8,128)(2,1)S(1)} %copy-done.1, ...), custom_call_target="tpu_custom_call" | custom-call | tf_op jit(solution)/shard_map/projection/pallas_call | solution.py:377
  31.6 0.0 collective-permute-done.1.h0_ref
  31.6 0.0 collective-permute-done.2.h1_ref
  31.6 5.4 %all-to-all-done.1.arrived_ref = bf16[16,16,256]{2,1,0:T(8,128)(2,1)S(1)} async-done(((bf16[16,16,256]{2,1,0:T(8,128)(2,1)}), bf16[16,16,256]{2,1,0:T(8,128)(2,1)S(1)}, u32[]{:S(2)}, u32[]{:S(2)}) %all-to-all-start.1) | async-done | bytes 131104 | tf_op jit(solution)/shard_map/all_to_all | solution.py:366
  37.1 0.0 copy-done.9
  37.1 1.3 %first_pick.1 = bf16[8,5,16,256]{3,2,1,0:T(8,128)(2,1)} custom-call(s32[5]{0:T(128)S(1)} %copy-done.9, bf16[16,16,256]{2,1,0:T(8,128)(2,1)S(1)} %all-to-all-done.1.arrived_ref), custom_call_target="tpu_custom_call" | custom-call | tf_op jit(solution)/shard_map/first_pick/pallas_call | solution.py:118
  38.4 10.2 %all-to-all-start.2 = ((bf16[8,5,16,256]{3,2,1,0:T(8,128)(2,1)}), bf16[8,5,16,256]{3,2,1,0:T(8,128)(2,1)}, u32[]{:S(2)}, u32[]{:S(2)}) async-start(bf16[8,5,16,256]{3,2,1,0:T(8,128)(2,1)} %first_pick.1), calls=%async_computation.2 | async-start | bytes 655360 | tf_op jit(solution)/shard_map/all_to_all | solution.py:402
  48.5 1.9 %collective-permute-start.3 = (bf16[256,256]{1,0:T(8,128)(2,1)}, bf16[256,256]{1,0:T(8,128)(2,1)S(1)}, u32[]{:S(2)}, u32[]{:S(2)}) collective-permute-start(bf16[256,256]{1,0:T(8,128)(2,1)} %copy-done.13), channel_id=1, source_target_pairs={{4,0},{8,4},{12,8},{16,12},{20,16},{24,20},{28,24},{32,28},{36,32}... | collective-permute-start | bytes 393224 | tf_op jit(solution)/shard_map/ppermute | solution.py:23
  50.4 4.4 %collective-permute-start.4 = (bf16[256,256]{1,0:T(8,128)(2,1)}, bf16[256,256]{1,0:T(8,128)(2,1)S(1)}, u32[]{:S(2)}, u32[]{:S(2)}) collective-permute-start(bf16[256,256]{1,0:T(8,128)(2,1)} %copy-done.12), channel_id=1, source_target_pairs={{8,0},{12,4},{16,8},{20,12},{24,16},{28,20},{32,24},{36,28},{40,32... | collective-permute-start | bytes 393224 | tf_op jit(solution)/shard_map/ppermute | solution.py:23
  54.8 2.2 %collective-permute-start = (bf16[256,128]{1,0:T(8,128)(2,1)}, bf16[256,128]{1,0:T(8,128)(2,1)S(1)}, u32[]{:S(2)}, u32[]{:S(2)}) collective-permute-start(bf16[256,128]{1,0:T(8,128)(2,1)} %get-tuple-element.17), channel_id=1, source_target_pairs={{0,1},{1,0},{2,3},{3,2},{4,5},{5,4},{6,7},{7,6},{8,9},{9,8},{10,11... | collective-permute-start | bytes 196616 | tf_op jit(solution)/shard_map/ppermute | solution.py:399
  57.0 3.0 %collective-permute-done.partner_ref = bf16[256,128]{1,0:T(8,128)(2,1)S(1)} collective-permute-done((bf16[256,128]{1,0:T(8,128)(2,1)}, bf16[256,128]{1,0:T(8,128)(2,1)S(1)}, u32[]{:S(2)}, u32[]{:S(2)}) %collective-permute-start) | collective-permute-done | bytes 65568 | tf_op jit(solution)/shard_map/ppermute | solution.py:399
  60.1 0.0 collective-permute-done.3.h2_ref
  60.1 0.0 collective-permute-done.4.h3_ref
  60.1 0.0 copy-done.7
  60.1 0.0 copy-start.8
  60.1 0.9 copy-done.8
  61.0 2.5 %local.1 = (f32[3,256,256]{2,1,0:T(8,128)S(1)}, f32[3,256,128]{2,1,0:T(8,128)S(1)}, bf16[1536,128]{1,0:T(8,128)(2,1)S(1)}) custom-call(s32[21]{0:T(128)S(1)} %concatenate.9.info_ref, s32[2]{0:T(128)S(1)} %pad_add_fusion.place_ref, bf16[3,256,128]{2,1,0:T(8,128)(2,1)S(1)} %get-tuple-element.19.q_ref, bf16[256,128]{1,0:T(8,128)(2,1)S(1)} %get-tuple-element.20.own_ref, ...), custom_call_target="tpu_custom_call" | custom-call | tf_op jit(solution)/shard_map/local/pallas_call | solution.py:406
  63.5 0.0 all-to-all-done.2.planes_ref
  63.5 1.6 %second_pick.1 = bf16[1,5,16,256]{3,2,1,0:T(8,128)(2,1)} custom-call(s32[5]{0:T(128)} %owner_ref.3, bf16[8,5,16,256]{3,2,1,0:T(8,128)(2,1)} %all-to-all-done.2.planes_ref), custom_call_target="tpu_custom_call" | custom-call | tf_op jit(solution)/shard_map/second_pick/pallas_call | solution.py:135
  65.1 19.4 %all_gather.3.hot_ref = bf16[16,5,16,256]{3,2,1,0:T(8,128)(2,1)S(1)} all-gather(bf16[1,5,16,256]{3,2,1,0:T(8,128)(2,1)} %second_pick.1), channel_id=1, replica_groups=mesh['z'=8,'y'=8,'core'=2,'tp'=4] {'y','core'}, dimensions={0}, use_global_device_ids=true | all-gather | bytes 696320 | tf_op jit(solution)/shard_map/all_gather | solution.py:420
  84.5 0.0 copy-done.2
  84.5 2.4 %shared.1 = bf16[4,256,384]{2,1,0:T(8,128)(2,1)S(1)} custom-call(bf16[3,256,128]{2,1,0:T(8,128)(2,1)S(1)} %get-tuple-element.19.q_ref, f32[3,256,256]{2,1,0:T(8,128)S(1)} %get-tuple-element.30.mixed_ref, f32[3,256,128]{2,1,0:T(8,128)S(1)} %get-tuple-element.31.top_ref, bf16[1536,128]{1,0:T(8,128)(2,1)S(1)} %get-tuple-element.32.bars_ref, ...), custom_call_target="tpu_custom_call" | custom-call | tf_op jit(solution)/shard_map/shared/pallas_call | solution.py:421
  86.9 0.0 copy-start.5
  86.9 14.5 %all_to_all.20 = bf16[4,256,384]{2,1,0:T(8,128)(2,1)S(1)} all-to-all(bf16[4,256,384]{2,1,0:T(8,128)(2,1)S(1)} %shared.1), channel_id=1, replica_groups=mesh['z'=8,'y'=8,'core'=2,'tp'=4] {'tp'}, dimensions={0} | all-to-all | bytes 1572864 | tf_op jit(solution)/shard_map/all_to_all | solution.py:429
  101.5 0.1 convert_reduce_fusion
  101.6 0.0 copy-done.5
  101.6 0.7 add_convert_fusion
  (11 shorter events, 0.0 us)
Async XLA Ops:
  0.6 16.5 %copy-start = (bf16[256,512]{1,0:T(8,128)(2,1)S(1)}, bf16[256,512]{1,0:T(8,128)(2,1)}, u32[]{:S(2)}) copy-start(bf16[256,512]{1,0:T(8,128)(2,1)} %param.23) | copy-start | bytes 786436
  0.6 7.1 %copy-start.3 = (bf16[16,64,512]{2,1,0:T(8,128)(2,1)S(1)}, bf16[16,64,512]{2,1,0:T(8,128)(2,1)}, u32[]{:S(2)}) copy-start(bf16[16,64,512]{2,1,0:T(8,128)(2,1)} %pool_ref.1) | copy-start | bytes 3145732
  0.7 1.0 %copy-start.4 = (bf16[256,384]{1,0:T(8,128)(2,1)S(1)}, bf16[256,384]{1,0:T(8,128)(2,1)}, u32[]{:S(2)}) copy-start(bf16[256,384]{1,0:T(8,128)(2,1)} %tok_ref.1) | copy-start | bytes 589828
  1.7 5.9 %copy-start.15 = (s32[1,4]{1,0:T(1,128)S(1)}, s32[1,4]{1,0:T(1,128)}, u32[]{:S(2)}) copy-start(s32[1,4]{1,0:T(1,128)} %param.29) | copy-start | bytes 52
  1.7 5.9 %copy-start.16 = (s32[1,4]{1,0:T(1,128)S(1)}, s32[1,4]{1,0:T(1,128)}, u32[]{:S(2)}) copy-start(s32[1,4]{1,0:T(1,128)} %param.28) | copy-start | bytes 52
  1.7 5.9 %copy-start.17 = (s32[1,4]{1,0:T(1,128)S(1)}, s32[1,4]{1,0:T(1,128)}, u32[]{:S(2)}) copy-start(s32[1,4]{1,0:T(1,128)} %param.30) | copy-start | bytes 52
  1.7 5.9 %copy-start.18 = (s32[1,4]{1,0:T(1,128)S(1)}, s32[1,4]{1,0:T(1,128)}, u32[]{:S(2)}) copy-start(s32[1,4]{1,0:T(1,128)} %param.31) | copy-start | bytes 52
  1.7 5.9 %copy-start.19 = (s32[5]{0:T(128)S(1)}, s32[5]{0:T(128)}, u32[]{:S(2)}) copy-start(s32[5]{0:T(128)} %param.24) | copy-start | bytes 64
  1.7 6.0 %copy-start.10 = (s32[1,16]{1,0:T(1,128)S(1)}, s32[1,16]{1,0:T(1,128)}, u32[]{:S(2)}) copy-start(s32[1,16]{1,0:T(1,128)} %param.27) | copy-start | bytes 196
  2.7 15.1 %all-to-all-start = ((bf16[4,256,384]{2,1,0:T(8,128)(2,1)}), bf16[4,256,384]{2,1,0:T(8,128)(2,1)S(1)}, u32[]{:S(2)}, u32[]{:S(2)}) async-start(bf16[4,256,384]{2,1,0:T(8,128)(2,1)} %copied.1), calls=%async_computation | async-start | bytes 1572864 | tf_op jit(solution)/shard_map/all_to_all | solution.py:347
  7.5 20.8 %copy-start.14 = (f32[384]{0:T(512)S(1)}, f32[384]{0:T(512)}, u32[]{:S(2)}) copy-start(f32[384]{0:T(512)} %param.19) | copy-start | bytes 4612
  7.7 21.5 %copy-start.1 = (bf16[1536,384]{1,0:T(8,128)(2,1)S(1)}, bf16[1536,384]{1,0:T(8,128)(2,1)}, u32[]{:S(2)}) copy-start(bf16[1536,384]{1,0:T(8,128)(2,1)} %wq_ref.1) | copy-start | bytes 3538948
  7.7 21.5 %copy-start.11 = (f32[128]{0:T(128)S(1)}, f32[128]{0:T(128)}, u32[]{:S(2)}) copy-start(f32[128]{0:T(128)} %param.21) | copy-start | bytes 1540
  9.3 3.4 %copy-start.12 = (bf16[256,256]{1,0:T(8,128)(2,1)}, bf16[256,256]{1,0:T(8,128)(2,1)S(1)}, u32[]{:S(2)}) copy-start(bf16[256,256]{1,0:T(8,128)(2,1)S(1)} %get-tuple-element.29) | copy-start | bytes 393220
  9.4 3.4 %copy-start.13 = (bf16[256,256]{1,0:T(8,128)(2,1)}, bf16[256,256]{1,0:T(8,128)(2,1)S(1)}, u32[]{:S(2)}) copy-start(bf16[256,256]{1,0:T(8,128)(2,1)S(1)} %get-tuple-element.28) | copy-start | bytes 393220
  9.4 19.9 %copy-start.6 = (bf16[1536,128]{1,0:T(8,128)(2,1)S(1)}, bf16[1536,128]{1,0:T(8,128)(2,1)}, u32[]{:S(2)}) copy-start(bf16[1536,128]{1,0:T(8,128)(2,1)} %wkv_ref.1) | copy-start | bytes 1179652
  9.4 22.2 %collective-permute-start.1 = (bf16[256,256]{1,0:T(8,128)(2,1)}, bf16[256,256]{1,0:T(8,128)(2,1)S(1)}, u32[]{:S(2)}, u32[]{:S(2)}) collective-permute-start(bf16[256,256]{1,0:T(8,128)(2,1)} %get-tuple-element.22), channel_id=1, source_target_pairs={{504,0},{508,4},{0,8},{4,12},{8,16},{12,20},{16,24},{20,28},{24,32... | collective-permute-start | bytes 393224 | tf_op jit(solution)/shard_map/ppermute | solution.py:23
  12.7 18.9 %collective-permute-start.2 = (bf16[256,256]{1,0:T(8,128)(2,1)}, bf16[256,256]{1,0:T(8,128)(2,1)S(1)}, u32[]{:S(2)}, u32[]{:S(2)}) collective-permute-start(bf16[256,256]{1,0:T(8,128)(2,1)} %get-tuple-element.23), channel_id=1, source_target_pairs={{508,0},{0,4},{4,8},{8,12},{12,16},{16,20},{20,24},{24,28},{28,32}... | collective-permute-start | bytes 393224 | tf_op jit(solution)/shard_map/ppermute | solution.py:23
  17.8 19.3 %all-to-all-start.1 = ((bf16[16,16,256]{2,1,0:T(8,128)(2,1)}), bf16[16,16,256]{2,1,0:T(8,128)(2,1)S(1)}, u32[]{:S(2)}, u32[]{:S(2)}) async-start(bf16[16,16,256]{2,1,0:T(8,128)(2,1)} %bitcast.8), calls=%async_computation.1 | async-start | bytes 262144 | tf_op jit(solution)/shard_map/all_to_all | solution.py:366
  29.3 7.8 %copy-start.9 = (s32[5]{0:T(128)S(1)}, s32[5]{0:T(128)}, u32[]{:S(2)}) copy-start(s32[5]{0:T(128)} %owner_ref.3) | copy-start | bytes 64
  31.6 28.5 %copy-start.7 = (bf16[256,256]{1,0:T(8,128)(2,1)}, bf16[256,256]{1,0:T(8,128)(2,1)S(1)}, u32[]{:S(2)}) copy-start(bf16[256,256]{1,0:T(8,128)(2,1)S(1)} %collective-permute-done.2.h1_ref) | copy-start | bytes 393220
  38.3 46.1 %copy-start.2 = (bf16[384,1536]{1,0:T(8,128)(2,1)S(1)}, bf16[384,1536]{1,0:T(8,128)(2,1)}, u32[]{:S(2)}) copy-start(bf16[384,1536]{1,0:T(8,128)(2,1)} %wo_ref.1) | copy-start | bytes 3538948
  38.4 25.2 %all-to-all-start.2 = ((bf16[8,5,16,256]{3,2,1,0:T(8,128)(2,1)}), bf16[8,5,16,256]{3,2,1,0:T(8,128)(2,1)}, u32[]{:S(2)}, u32[]{:S(2)}) async-start(bf16[8,5,16,256]{3,2,1,0:T(8,128)(2,1)} %first_pick.1), calls=%async_computation.2 | async-start | bytes 655360 | tf_op jit(solution)/shard_map/all_to_all | solution.py:402
  48.5 11.5 %collective-permute-start.3 = (bf16[256,256]{1,0:T(8,128)(2,1)}, bf16[256,256]{1,0:T(8,128)(2,1)S(1)}, u32[]{:S(2)}, u32[]{:S(2)}) collective-permute-start(bf16[256,256]{1,0:T(8,128)(2,1)} %copy-done.13), channel_id=1, source_target_pairs={{4,0},{8,4},{12,8},{16,12},{20,16},{24,20},{28,24},{32,28},{36,32}... | collective-permute-start | bytes 393224 | tf_op jit(solution)/shard_map/ppermute | solution.py:23
  50.4 9.6 %collective-permute-start.4 = (bf16[256,256]{1,0:T(8,128)(2,1)}, bf16[256,256]{1,0:T(8,128)(2,1)S(1)}, u32[]{:S(2)}, u32[]{:S(2)}) collective-permute-start(bf16[256,256]{1,0:T(8,128)(2,1)} %copy-done.12), channel_id=1, source_target_pairs={{8,0},{12,4},{16,8},{20,12},{24,16},{28,20},{32,24},{36,28},{40,32... | collective-permute-start | bytes 393224 | tf_op jit(solution)/shard_map/ppermute | solution.py:23
  54.8 5.2 %collective-permute-start = (bf16[256,128]{1,0:T(8,128)(2,1)}, bf16[256,128]{1,0:T(8,128)(2,1)S(1)}, u32[]{:S(2)}, u32[]{:S(2)}) collective-permute-start(bf16[256,128]{1,0:T(8,128)(2,1)} %get-tuple-element.17), channel_id=1, source_target_pairs={{0,1},{1,0},{2,3},{3,2},{4,5},{5,4},{6,7},{7,6},{8,9},{9,8},{10,11... | collective-permute-start | bytes 196616 | tf_op jit(solution)/shard_map/ppermute | solution.py:399
  60.1 0.9 copy-start.8
  86.9 14.7 %copy-start.5 = (bf16[256,384]{1,0:T(8,128)(2,1)S(1)}, bf16[256,384]{1,0:T(8,128)(2,1)}, u32[]{:S(2)}) copy-start(bf16[256,384]{1,0:T(8,128)(2,1)} %tok_ref.1) | copy-start | bytes 589828
